TPU v7x, 32 devices: a whole 2x2x4 slice. The times are simulated.
32 devices in a mesh: ctx: 4 (over y, core), head: 4 (over z), wide: 2 (over x).
Axes of the slice: x: 2, y: 2, z: 4, core: 2. Of those that a mesh axis runs over, the one named last changes fastest.
Arguments:
- query_rows: bfloat16 [2, 1024, 1024], P('wide', 'ctx', 'head'), may hold values from -105 to 105
- key_rows: bfloat16 [2, 1024, 1024], P('wide', 'ctx', 'head'), may hold values from -4.5 to 4.5
- value_rows: bfloat16 [2, 1024, 1024], P('wide', 'ctx', 'head'), may hold values from -6 to 6
- grad_out: bfloat16 [2, 1024, 1024], P('wide', 'ctx', 'head'), may hold values from -6 to 6
- segment: int32 [2, 1024], P('wide', 'ctx'), may hold values from 0 to 7, never falling along the last dimension, each value on 1 to 256 neighbouring positions
- frames: bfloat16 [2, 1024, 4096], P(None, 'ctx', 'wide'), may hold values from -6 to 6
Outputs:
- grad_query: bfloat16 [2, 1024, 1024], P('wide', 'ctx', 'head')
- grad_key: bfloat16 [2, 1024, 1024], P('wide', 'ctx', 'head')
- grad_value: bfloat16 [2, 1024, 1024], P('wide', 'ctx', 'head')
- grad_wq: float32 [2, 2048, 1024], P('wide', 'ctx', 'head')
Inputs may be any that keep to these rules, and one draw needn't show every extreme that they name: Ids never fall along a recording; each segment spans 1 to 256 frames and one spans exactly 256.
All inputs are finite; a program needn't handle non-finite values.
Results may differ from a plain program's by a relative error of at most 0.01.
Values may be sent and summed in bfloat16 or wider, within the bound.
No kernel may reach another device: no remote copies, remote signals or barrier semaphores. Data moves between devices by JAX's collectives and lax.ppermute only.
A program may use at most 64 MiB of HBM per device.

v0:
```python
import jax
import jax.numpy as jnp
from jax import lax
from jax.sharding import PartitionSpec as P

HD = 128


def shifted(value, axis, steps):
    count = lax.axis_size(axis)
    initial, last = (max(0, -steps), min(count, count - steps))
    return lax.ppermute(value, axis, [(source, source + steps) for source in range(initial, last)])


def head_scores(left_heads, right_heads):
    return jnp.einsum("ihd,jhd->hij", left_heads, right_heads, preferred_element_type=jnp.float32)


def shards(query_rows, key_rows, value_rows, grad_out, segment, frames):
    length = query_rows.shape[1]
    columns = query_rows.shape[2]
    head_count = columns // HD
    factor = HD ** (-0.5)
    ctx_index = lax.axis_index("ctx")
    ctx_count = lax.axis_size("ctx")
    query_heads = query_rows.reshape(length, head_count, HD)
    key_heads = key_rows.reshape(length, head_count, HD)
    value_heads = value_rows.reshape(length, head_count, HD)
    grad_heads = grad_out.reshape(length, head_count, HD)
    own_segment = segment[0]
    prior_keys, prior_values, prior_segment = shifted((key_rows, value_rows, segment), "ctx", 1)
    prior_key_heads = prior_keys.reshape(length, head_count, HD)
    prior_value_heads = prior_values.reshape(length, head_count, HD)
    places = jnp.arange(length, dtype=jnp.int32)
    own_mask = (own_segment[:, None] == own_segment[None, :]) & (places[None, :] <= places[:, None])
    prior_mask = (own_segment[:, None] == prior_segment[0][None, :]) & (ctx_index > 0)
    own_scores = head_scores(query_heads, key_heads) * factor
    prior_scores = head_scores(query_heads, prior_key_heads) * factor
    row_max = jnp.maximum(
        jnp.max(jnp.where(own_mask, own_scores, -jnp.inf), axis=2, keepdims=True),
        jnp.max(jnp.where(prior_mask, prior_scores, -jnp.inf), axis=2, keepdims=True),
    )
    row_total = jnp.sum(
        jnp.where(own_mask, jnp.exp(own_scores - row_max), 0.0), axis=2, keepdims=True
    ) + jnp.sum(jnp.where(prior_mask, jnp.exp(prior_scores - row_max), 0.0), axis=2, keepdims=True)
    log_total = row_max + jnp.log(row_total)
    own_prob = jnp.where(own_mask, jnp.exp(own_scores - log_total), 0.0)
    prior_prob = jnp.where(prior_mask, jnp.exp(prior_scores - log_total), 0.0)
    own_grad_prob = head_scores(grad_heads, value_heads)
    prior_grad_prob = head_scores(grad_heads, prior_value_heads)
    row_delta = jnp.sum(own_prob * own_grad_prob, axis=2, keepdims=True) + jnp.sum(
        prior_prob * prior_grad_prob, axis=2, keepdims=True
    )
    own_grad_score = (own_prob * (own_grad_prob - row_delta)).astype(jnp.bfloat16)
    prior_grad_score = (prior_prob * (prior_grad_prob - row_delta)).astype(jnp.bfloat16)
    own_prob_low = own_prob.astype(jnp.bfloat16)
    grad_query_heads = (
        jnp.einsum("hij,jhd->ihd", own_grad_score, key_heads, preferred_element_type=jnp.float32)
        + jnp.einsum(
            "hij,jhd->ihd", prior_grad_score, prior_key_heads, preferred_element_type=jnp.float32
        )
    ) * factor
    grad_query = grad_query_heads.astype(jnp.bfloat16).reshape(1, length, columns)
    own_key_grad = jnp.einsum(
        "hij,ihd->jhd", own_grad_score, query_heads, preferred_element_type=jnp.float32
    )
    own_value_grad = jnp.einsum(
        "hij,ihd->jhd", own_prob_low, grad_heads, preferred_element_type=jnp.float32
    )
    prior_key_grad = jnp.einsum(
        "hij,ihd->jhd", prior_grad_score, query_heads, preferred_element_type=jnp.float32
    )
    prior_value_grad = jnp.einsum(
        "hij,ihd->jhd",
        prior_prob.astype(jnp.bfloat16),
        grad_heads,
        preferred_element_type=jnp.float32,
    )
    later_key_grad, later_value_grad = shifted((prior_key_grad, prior_value_grad), "ctx", -1)
    grad_key = (
        ((own_key_grad + later_key_grad) * factor).astype(jnp.bfloat16).reshape(1, length, columns)
    )
    grad_value = (
        (own_value_grad + later_value_grad).astype(jnp.bfloat16).reshape(1, length, columns)
    )
    width = frames.shape[2]
    row_block = width // ctx_count
    panel_sum = jnp.einsum(
        "rtd,rtc->dc",
        frames,
        lax.all_gather(grad_query, "wide", axis=0, tiled=True),
        preferred_element_type=jnp.float32,
    )
    grad_wq = lax.psum_scatter(panel_sum, "ctx", scatter_dimension=0, tiled=True).reshape(
        1, row_block, columns
    )
    return (grad_query, grad_key, grad_value, grad_wq)


def solution(mesh):
    return jax.shard_map(
        shards,
        mesh=mesh,
        in_specs=(
            P("wide", "ctx", "head"),
            P("wide", "ctx", "head"),
            P("wide", "ctx", "head"),
            P("wide", "ctx", "head"),
            P("wide", "ctx"),
            P(None, "ctx", "wide"),
        ),
        out_specs=(
            P("wide", "ctx", "head"),
            P("wide", "ctx", "head"),
            P("wide", "ctx", "head"),
            P("wide", "ctx", "head"),
        ),
        check_vma=False,
    )
```

profile of v0, /device:TPU:0, one launch (start us, length us, event | category | flops | bytes accessed | tf_op | source)
XLA Modules:
  0.0 79.4 jit_solution(1340995519553160902)
XLA Ops:
  7.2 2.5 %collective-permute-start = (s32[1,256]{1,0:T(1,128)}, s32[1,256]{1,0:T(1,128)S(1)}, u32[]{:S(2)}, u32[]{:S(2)}) collective-permute-start(s32[1,256]{1,0:T(1,128)} %param.10), channel_id=1, source_target_pairs={{0,8},{8,16},{16,24},{1,9},{9,17},{17,25},{2,10},{10,18},{18,26},{... | collective-permute-start | bytes 3080 | tf_op jit(solution)/shard_map/ppermute | solution.py:12
  9.8 1.7 %copy.64 = bf16[1,256,256]{1,2,0:T(8,128)(2,1)} copy(bf16[1,256,256]{2,1,0:T(8,128)(2,1)} %param.8) | data formatting | bytes 262144 | tf_op args[2]
  11.4 5.2 %collective-permute-start.2 = (bf16[1,256,256]{1,2,0:T(8,128)(2,1)}, bf16[1,256,256]{1,2,0:T(8,128)(2,1)}, u32[]{:S(2)}, u32[]{:S(2)}) collective-permute-start(bf16[1,256,256]{1,2,0:T(8,128)(2,1)} %copy.64), channel_id=1, source_target_pairs={{0,8},{8,16},{16,24},{1,9},{9,17},{17,25},{2,10},{10,18},{18,26},{... | collective-permute-start | bytes 393224 | tf_op jit(solution)/shard_map/ppermute | solution.py:12
  16.6 1.0 %copy.93 = bf16[1,256,256]{1,2,0:T(8,128)(2,1)S(1)} copy(bf16[1,256,256]{2,1,0:T(8,128)(2,1)} %param.7) | data formatting | bytes 262144 | tf_op jit(solution)/shard_map/reshape | solution.py:27
  17.6 1.3 %collective-permute-start.1 = (bf16[1,256,256]{1,2,0:T(8,128)(2,1)S(1)}, bf16[1,256,256]{1,2,0:T(8,128)(2,1)S(1)}, u32[]{:S(2)}, u32[]{:S(2)}) collective-permute-start(bf16[1,256,256]{1,2,0:T(8,128)(2,1)S(1)} %copy.93), channel_id=1, source_target_pairs={{0,8},{8,16},{16,24},{1,9},{9,17},{17,25},{2,10},{10,18},{18,26},{... | collective-permute-start | bytes 393224 | tf_op jit(solution)/shard_map/ppermute | solution.py:12
  18.9 0.9 %reshape.69 = bf16[256,2,128]{2,1,0:T(2,128)(2,1)S(1)} reshape(bf16[1,256,256]{2,1,0:T(8,128)(2,1)} %param.8) | data formatting | bytes 262144 | tf_op jit(solution)/shard_map/reshape | solution.py:28
  19.9 0.9 %reshape.68 = bf16[256,2,128]{2,1,0:T(2,128)(2,1)S(1)} reshape(bf16[1,256,256]{2,1,0:T(8,128)(2,1)} %param.9) | data formatting | bytes 262144 | tf_op jit(solution)/shard_map/reshape | solution.py:29
  20.8 1.0 %fusion.18 = f32[2,256,256]{1,2,0:T(8,128)} fusion(bf16[256,2,128]{2,1,0:T(2,128)(2,1)S(1)} %reshape.69, bf16[256,2,128]{2,1,0:T(2,128)(2,1)S(1)} %reshape.68), kind=kOutput, calls=%fused_computation.36 | convolution fusion | flops 33554432 | bytes 786432 | tf_op jit(solution)/shard_map/ihd,jhd->hij/dot_general | solution.py:16
  21.8 0.9 %reshape.65 = bf16[256,2,128]{2,1,0:T(2,128)(2,1)S(1)} reshape(bf16[1,256,256]{2,1,0:T(8,128)(2,1)} %param.6) | data formatting | bytes 262144 | tf_op jit(solution)/shard_map/reshape | solution.py:26
  23.9 1.2 %select_reduce_fusion.2 = (f32[2,256]{1,0:T(2,128)S(1)}, f32[2,256,256]{1,2,0:T(8,128)S(1)}) fusion(pred[256,256]{0,1:T(8,128)(4,1)S(1)} %get-tuple-element.22, bf16[256,2,128]{0,2,1:T(8,128)(2,1)} %bitcast.50, bf16[256,2,128]{2,1,0:T(2,128)(2,1)S(1)} %reshape.65), kind=kOutput, calls=%fused_computation.23 | convolution fusion | flops 33947136 | bytes 854016 | tf_op jit(solution)/shard_map/ihd,jhd->hij/dot_general | solution.py:16
  25.4 1.4 %multiply_reduce_fusion = (f32[2,256]{1,0:T(2,128)S(1)}, f32[2,256]{1,0:T(2,128)S(1)}, f32[2,256,256]{1,2,0:T(8,128)S(1)}) fusion(f32[2,256,256]{1,2,0:T(8,128)S(1)} %get-tuple-element.27, f32[2,256]{1,0:T(2,128)S(1)} %log_add_fusion, pred[256,256]{0,1:T(8,128)(4,1)S(1)} %get-tuple-element.22, f32[2,256,256]{1,2,0:T(8,128)S(1)} %copy-done.1, ...), kind=kOutput, calls=%fused_computation.17 | convolution fusion | flops 34601984 | bytes 2496512 | tf_op jit(solution)/shard_map/ihd,jhd->hij/dot_general | solution.py:16
  28.0 0.8 %fusion.6 = bf16[2,256,128]{1,2,0:T(8,128)(2,1)} fusion(f32[2,256,128]{1,2,0:T(8,128)S(1)} %fusion.31, bf16[256,2,128]{0,2,1:T(8,128)(2,1)S(1)} %bitcast.51, bf16[2,256,256]{1,2,0:T(8,128)(2,1)S(1)} %get-tuple-element.20), kind=kOutput, calls=%fused_computation.14 | convolution fusion | flops 33751040 | bytes 786432 | tf_op jit(solution)/shard_map/hij,jhd->ihd/dot_general | solution.py:59
  28.9 1.7 %copy.80 = bf16[1,256,256]{2,1,0:T(8,128)(2,1)} copy(bf16[1,256,256]{1,2,0:T(8,128)(2,1)} %bitcast.49) | data formatting | bytes 262144
  30.5 6.3 %all_gather.3 = bf16[2,256,256]{2,1,0:T(8,128)(2,1)S(1)} all-gather(bf16[1,256,256]{2,1,0:T(8,128)(2,1)} %copy.80), channel_id=1, replica_groups=mesh['ctx'=4,'head'=4,'wide'=2] {'wide'}, dimensions={0}, use_global_device_ids=true | all-gather | bytes 393216 | tf_op jit(solution)/shard_map/all_gather | solution.py:91
  36.8 2.1 %convolution_bitcast_fusion = f32[2048,256]{0,1:T(8,128)} fusion(bf16[2,256,256]{2,1,0:T(8,128)(2,1)S(1)} %all_gather.3, bf16[2,256,2048]{2,1,0:T(8,128)(2,1)S(1)} %copy-done), kind=kOutput, calls=%fused_computation | convolution fusion | flops 536870912 | bytes 4456448 | tf_op jit(solution)/shard_map/rtd,rtc->dc/dot_general | solution.py:88
  39.2 1.4 %collective-permute-start.4 = (f32[256,2,128]{0,2,1:T(8,128)S(1)}, f32[256,2,128]{0,2,1:T(8,128)S(1)}, u32[]{:S(2)}, u32[]{:S(2)}) collective-permute-start(f32[256,2,128]{0,2,1:T(8,128)S(1)} %convolution_bitcast_fusion.1), channel_id=1, source_target_pairs={{8,0},{16,8},{24,16},{9,1},{17,9},{25,17},{10,2},{18,10},{26,18},{... | collective-permute-start | bytes 786440 | tf_op jit(solution)/shard_map/ppermute | solution.py:12
  40.6 1.9 %convolution_bitcast_fusion.3 = f32[256,2,128]{0,2,1:T(8,128)} fusion(bf16[2,256,256]{1,2,0:T(8,128)(2,1)} %copy-done.4, bf16[256,2,128]{2,1,0:T(2,128)(2,1)S(1)} %reshape.65), kind=kOutput, calls=%fused_computation.8 | convolution fusion | flops 33554432 | bytes 655360 | tf_op jit(solution)/shard_map/hij,ihd->jhd/dot_general | solution.py:70
  42.5 1.3 %collective-permute-start.3 = (f32[256,2,128]{0,2,1:T(8,128)}, f32[256,2,128]{0,2,1:T(8,128)}, u32[]{:S(2)}, u32[]{:S(2)}) collective-permute-start(f32[256,2,128]{0,2,1:T(8,128)} %convolution_bitcast_fusion.3), channel_id=1, source_target_pairs={{8,0},{16,8},{24,16},{9,1},{17,9},{25,17},{10,2},{18,10},{26,18},{... | collective-permute-start | bytes 786440 | tf_op jit(solution)/shard_map/ppermute | solution.py:12
  44.0 0.8 copy.82
  44.8 2.3 %collective-permute-done.3 = f32[256,2,128]{0,2,1:T(8,128)} collective-permute-done((f32[256,2,128]{0,2,1:T(8,128)}, f32[256,2,128]{0,2,1:T(8,128)}, u32[]{:S(2)}, u32[]{:S(2)}) %collective-permute-start.3) | collective-permute-done | bytes 262176 | tf_op jit(solution)/shard_map/ppermute | solution.py:12
  47.1 1.2 %fusion.4 = bf16[256,2,128]{0,2,1:T(8,128)(2,1)S(1)} fusion(f32[256,2,128]{0,2,1:T(8,128)} %collective-permute-done.3, bf16[2,256,256]{1,2,0:T(8,128)(2,1)S(1)} %copy-done.3, bf16[256,2,128]{2,1,0:T(2,128)(2,1)S(1)} %reshape.65), kind=kOutput, calls=%fused_computation.12 | convolution fusion | flops 33751040 | bytes 786432 | tf_op jit(solution)/shard_map/hij,ihd->jhd/dot_general | solution.py:64
  48.3 0.8 copy.81
  49.1 21.4 %reduce-scatter.2.cloned.1.call-done = f32[512,256]{0,1:T(8,128)} async-done(((f32[2048,256]{0,1:T(8,128)}), f32[512,256]{0,1:T(8,128)}) %reduce-scatter.2.cloned.1.call-update) | async-done | bytes 524304 | tf_op jit(solution)/shard_map/reduce_scatter | solution.py:94
  70.5 2.0 %copy.83 = f32[1,512,256]{2,1,0:T(8,128)} copy(f32[1,512,256]{1,2,0:T(8,128)} %bitcast.47) | data formatting | bytes 1048576
  (36 shorter events, 3.1 us)
Async XLA Ops:
  7.2 29.6 %copy-start = (bf16[2,256,2048]{2,1,0:T(8,128)(2,1)S(1)}, bf16[2,256,2048]{2,1,0:T(8,128)(2,1)}, u32[]{:S(2)}) copy-start(bf16[2,256,2048]{2,1,0:T(8,128)(2,1)} %param.11) | copy-start | bytes 6291460
  7.2 15.6 %copy-start.9 = (s32[1,256]{1,0:T(1,128)S(1)}, s32[1,256]{1,0:T(1,128)}, u32[]{:S(2)}) copy-start(s32[1,256]{1,0:T(1,128)} %param.10) | copy-start | bytes 3076
  7.2 63.3 %reduce-scatter.2.cloned.1.call-start = ((), (), s32[]{:S(2)}) async-start(), calls=%async_computation.1 | async-start | bytes 2621440 | tf_op jit(solution)/shard_map/reduce_scatter | solution.py:94
  7.2 15.6 %collective-permute-start = (s32[1,256]{1,0:T(1,128)}, s32[1,256]{1,0:T(1,128)S(1)}, u32[]{:S(2)}, u32[]{:S(2)}) collective-permute-start(s32[1,256]{1,0:T(1,128)} %param.10), channel_id=1, source_target_pairs={{0,8},{8,16},{16,24},{1,9},{9,17},{17,25},{2,10},{10,18},{18,26},{... | collective-permute-start | bytes 3080 | tf_op jit(solution)/shard_map/ppermute | solution.py:12
  11.4 13.9 %collective-permute-start.2 = (bf16[1,256,256]{1,2,0:T(8,128)(2,1)}, bf16[1,256,256]{1,2,0:T(8,128)(2,1)}, u32[]{:S(2)}, u32[]{:S(2)}) collective-permute-start(bf16[1,256,256]{1,2,0:T(8,128)(2,1)} %copy.64), channel_id=1, source_target_pairs={{0,8},{8,16},{16,24},{1,9},{9,17},{17,25},{2,10},{10,18},{18,26},{... | collective-permute-start | bytes 393224 | tf_op jit(solution)/shard_map/ppermute | solution.py:12
  17.6 5.7 %copy-start.5 = (bf16[1,256,256]{1,2,0:T(8,128)(2,1)}, bf16[1,256,256]{1,2,0:T(8,128)(2,1)S(1)}, u32[]{:S(2)}) copy-start(bf16[1,256,256]{1,2,0:T(8,128)(2,1)S(1)} %copy.93) | copy-start | bytes 393220
  17.6 5.6 %collective-permute-start.1 = (bf16[1,256,256]{1,2,0:T(8,128)(2,1)S(1)}, bf16[1,256,256]{1,2,0:T(8,128)(2,1)S(1)}, u32[]{:S(2)}, u32[]{:S(2)}) collective-permute-start(bf16[1,256,256]{1,2,0:T(8,128)(2,1)S(1)} %copy.93), channel_id=1, source_target_pairs={{0,8},{8,16},{16,24},{1,9},{9,17},{17,25},{2,10},{10,18},{18,26},{... | collective-permute-start | bytes 393224 | tf_op jit(solution)/shard_map/ppermute | solution.py:12
  22.8 2.6 %copy-start.1 = (f32[2,256,256]{1,2,0:T(8,128)S(1)}, f32[2,256,256]{1,2,0:T(8,128)}, u32[]{:S(2)}) copy-start(f32[2,256,256]{1,2,0:T(8,128)} %fusion.18) | copy-start | bytes 1572868
  23.3 0.7 copy-start.7
  25.4 2.4 %copy-start.6 = (bf16[1,256,256]{1,2,0:T(8,128)(2,1)S(1)}, bf16[1,256,256]{1,2,0:T(8,128)(2,1)}, u32[]{:S(2)}) copy-start(bf16[1,256,256]{1,2,0:T(8,128)(2,1)} %copy-done.5) | copy-start | bytes 393220
  26.8 1.2 %copy-start.8 = (bf16[1,256,256]{1,2,0:T(8,128)(2,1)S(1)}, bf16[1,256,256]{1,2,0:T(8,128)(2,1)}, u32[]{:S(2)}) copy-start(bf16[1,256,256]{1,2,0:T(8,128)(2,1)} %copy-done.7) | copy-start | bytes 393220
  27.1 0.7 copy-start.2
  27.1 0.9 %copy-start.4 = (bf16[2,256,256]{1,2,0:T(8,128)(2,1)}, bf16[2,256,256]{1,2,0:T(8,128)(2,1)S(1)}, u32[]{:S(2)}) copy-start(bf16[2,256,256]{1,2,0:T(8,128)(2,1)S(1)} %get-tuple-element.20) | copy-start | bytes 786436
  39.1 8.0 %copy-start.3 = (bf16[2,256,256]{1,2,0:T(8,128)(2,1)S(1)}, bf16[2,256,256]{1,2,0:T(8,128)(2,1)}, u32[]{:S(2)}) copy-start(bf16[2,256,256]{1,2,0:T(8,128)(2,1)} %copy-done.2) | copy-start | bytes 786436
  39.2 4.6 %collective-permute-start.4 = (f32[256,2,128]{0,2,1:T(8,128)S(1)}, f32[256,2,128]{0,2,1:T(8,128)S(1)}, u32[]{:S(2)}, u32[]{:S(2)}) collective-permute-start(f32[256,2,128]{0,2,1:T(8,128)S(1)} %convolution_bitcast_fusion.1), channel_id=1, source_target_pairs={{8,0},{16,8},{24,16},{9,1},{17,9},{25,17},{10,2},{18,10},{26,18},{... | collective-permute-start | bytes 786440 | tf_op jit(solution)/shard_map/ppermute | solution.py:12
  42.5 4.6 %collective-permute-start.3 = (f32[256,2,128]{0,2,1:T(8,128)}, f32[256,2,128]{0,2,1:T(8,128)}, u32[]{:S(2)}, u32[]{:S(2)}) collective-permute-start(f32[256,2,128]{0,2,1:T(8,128)} %convolution_bitcast_fusion.3), channel_id=1, source_target_pairs={{8,0},{16,8},{24,16},{9,1},{17,9},{25,17},{10,2},{18,10},{26,18},{... | collective-permute-start | bytes 786440 | tf_op jit(solution)/shard_map/ppermute | solution.py:12
Sparse Core Ops, SparseCore 0:
  39.0 31.4 reduce-scatter.1
where the time goes:
time: 79.9 us; the launch traced here: 79.4 us
  waiting for transfers between devices  23.8 us (30%)
  between operations  14.3 us (18%)
  local copies, waits for them, and re-layouts  12.1 us (15%)
  starting transfers between devices  11.7 us (15%)
  matrix products  10.5 us (13%)
  blocking collectives  6.28 us (8%)
    reduce_scatter x1, waiting for transfers between devices, shards(): lax.psum_scatter(panel_sum, 'ctx', scatter_dimension=0, tiled=True)  21.4 us
    ppermute x5, starting transfers between devices, shifted(): lax.ppermute(value, axis, [(source, source + steps) for source in range(i...  11.7 us
    unnamed x25, local copies, waits for them, and re-layouts  8.25 us
    all_gather x1, blocking collectives, shards(): lax.all_gather(grad_query, 'wide', axis=0, tiled=True)  6.28 us
    dot_general x4, matrix products, head_scores(): jnp.einsum('ihd,jhd->hij', left_heads, right_heads, preferred_element_typ...  3.87 us
    ppermute x5, waiting for transfers between devices, shifted(): lax.ppermute(value, axis, [(source, source + steps) for source in range(i...  2.34 us
    dot_general x1, matrix products, shards(): jnp.einsum('rtd,rtc->dc', frames, lax.all_gather(grad_query, 'wide', axis...  2.06 us
    dot_general x1, matrix products, shards(): jnp.einsum('hij,ihd->jhd', prior_grad_score, query_heads, preferred_eleme...  1.87 us
  transfers between devices with their start and end apart: 6, of which 2 were waited for; matrix products, arithmetic and copies ran while one was open for 17% of the time, Pallas kernels for 0%

commit v1 on v0

v1 whole, which is shorter than its diff:
```python
import functools

import jax
import jax.numpy as jnp
from jax import lax
from jax.experimental import pallas as pl
from jax.experimental.pallas import tpu as pltpu
from jax.sharding import PartitionSpec as P

HD = 128
F32 = jnp.float32
BF16 = jnp.bfloat16


def dot(left, right, left_dim, right_dim):
    return lax.dot_general(
        left, right, (((left_dim,), (right_dim,)), ((), ())), preferred_element_type=F32
    )


def call(body, outs, *args, flops=1 << 20, name=None):
    whole = pl.BlockSpec(memory_space=pltpu.VMEM)
    size = sum(a.size * a.dtype.itemsize for a in args)
    return pl.pallas_call(
        body,
        out_shape=outs,
        in_specs=[whole] * len(args),
        out_specs=jax.tree.map(lambda _: whole, outs),
        cost_estimate=pl.CostEstimate(flops=flops, bytes_accessed=size, transcendentals=0),
        name=name,
    )(*args)


def shape(dims, dtype):
    return jax.ShapeDtypeStruct(dims, dtype)


def spread(row, length):
    part = jnp.transpose(jnp.broadcast_to(row.astype(F32), (HD, length)))
    return jnp.concatenate([part] * (length // HD), axis=1)


def lower(length):
    rows = lax.broadcasted_iota(jnp.int32, (length, length), 0)
    columns = lax.broadcasted_iota(jnp.int32, (length, length), 1)
    return rows, columns


def scores_body(length, heads, q, k, v, g, pk, pv, seg, pseg, dq, ds_out, p_out):
    factor = HD ** (-0.5)
    key_place, query_place = lower(length)
    own = key_place <= query_place
    seg_row = seg[...].astype(F32)
    seg_column = jnp.where(own, spread(seg[...], length), spread(pseg[...], length))
    valid = seg_column == seg_row
    for h in range(heads):
        at = slice(h * HD, (h + 1) * HD)
        qh, gh, kh, pkh = q[:, at], g[:, at], k[:, at], pk[:, at]
        scores = jnp.where(own, dot(kh, qh, 1, 1), dot(pkh, qh, 1, 1)) * factor
        scores = jnp.where(valid, scores, -jnp.inf)
        top = jnp.max(scores, axis=0, keepdims=True)
        weight = jnp.exp(scores - top)
        prob = weight * (1.0 / jnp.sum(weight, axis=0, keepdims=True))
        grad_prob = jnp.where(own, dot(v[:, at], gh, 1, 1), dot(pv[:, at], gh, 1, 1))
        delta = jnp.sum(prob * grad_prob, axis=0, keepdims=True)
        grad_score = prob * (grad_prob - delta)
        own_part = jnp.where(own, grad_score, 0.0).astype(BF16)
        prior_part = jnp.where(own, 0.0, grad_score).astype(BF16)
        dq[:, at] = (
            (dot(own_part, kh, 0, 0) + dot(prior_part, pkh, 0, 0)) * factor
        ).astype(BF16)
        ds_out[h] = grad_score.astype(BF16)
        p_out[h] = prob.astype(BF16)


def terms_body(length, heads, q, g, ds, p, own_out, back_out):
    key_place, query_place = lower(length)
    own = key_place <= query_place
    for h in range(heads):
        at = slice(h * HD, (h + 1) * HD)
        for index, (left, right) in enumerate(((ds, q), (p, g))):
            value = left[h].astype(F32)
            own_out[index, :, at] = dot(
                jnp.where(own, value, 0.0).astype(BF16), right[:, at], 1, 0
            )
            back_out[index, :, at] = dot(
                jnp.where(own, 0.0, value).astype(BF16), right[:, at], 1, 0
            ).astype(BF16)


def join_body(own, later, dk, dv):
    dk[...] = ((own[0] + later[0].astype(F32)) * HD ** (-0.5)).astype(BF16)
    dv[...] = (own[1] + later[1].astype(F32)).astype(BF16)


def turn_body(recs, length, block, parts, frames, mine, theirs):
    for side in range(2):

        @pl.when(lax.rem(lax.axis_index("ctx"), 2) == side)
        def _():
            for part in range(parts):
                for r in range(recs):
                    for out, which in ((mine, side), (theirs, 1 - side)):
                        start = (2 * part + which) * block
                        tile = frames[r, :, start : start + block]
                        out[part, :, r * length : (r + 1) * length] = jnp.transpose(tile)


def panel_body(count, length, block, step, *refs):
    frames, grads, out = refs[:2], refs[2:-1], refs[-1]
    part = lax.rem(lax.div(lax.axis_index("ctx"), 2) + step, lax.axis_size("ctx") // 2)
    wide = lax.axis_index("wide")
    total = None
    for k in range(count):
        rec = lax.rem(wide - k + count, count)
        at = pl.ds(pl.multiple_of(rec * length, HD), length)
        for core in range(2):
            term = dot(frames[core][part, :, at], grads[2 * k + core][...], 1, 0)
            total = term if total is None else total + term
    out[...] = total.astype(out.dtype)


def add_body(*refs):
    total = refs[0][...]
    for ref in refs[1:-1]:
        total = total + ref[...].astype(F32)
    refs[-1][...] = total


def shards(query_rows, key_rows, value_rows, grad_out, segment, frames):
    length, columns = query_rows.shape[1:]
    heads = columns // HD
    ctx_count = lax.axis_size("ctx")
    wide_count = lax.axis_size("wide")
    recs, _, width = frames.shape
    block = width // ctx_count
    parts = ctx_count // 2
    assert ctx_count >= 4 and recs == wide_count
    onward = [(i, (i + 1) % ctx_count) for i in range(ctx_count)]
    back = [(i, (i - 1) % ctx_count) for i in range(ctx_count)]
    other = [(i, i ^ 1) for i in range(ctx_count)]

    q, k, v, g = (a[0] for a in (query_rows, key_rows, value_rows, grad_out))
    pseg = lax.ppermute(segment, "ctx", onward)
    pk = lax.ppermute(k, "ctx", onward)
    pv = lax.ppermute(v, "ctx", onward)

    turned = shape((parts, block, recs * length), BF16)
    mine, theirs = call(
        functools.partial(turn_body, recs, length, block, parts), (turned, turned), frames, name="turn"
    )
    given = lax.ppermute(theirs, "ctx", other)

    square = shape((heads, length, length), BF16)
    dq, ds, p = call(
        functools.partial(scores_body, length, heads),
        (shape((length, columns), BF16), square, square),
        q, k, v, g, pk, pv, segment, pseg, name="scores",
    )
    grads = []
    for step in range(wide_count):
        ring = [(i, (i + step) % wide_count) for i in range(wide_count)]
        piece = lax.ppermute(dq, "wide", ring) if step else dq
        grads += [piece, lax.ppermute(piece, "ctx", other)]

    own, to_prior = call(
        functools.partial(terms_body, length, heads),
        (shape((2, length, columns), F32), shape((2, length, columns), BF16)),
        q, g, ds, p, name="terms",
    )
    later = lax.ppermute(to_prior, "ctx", back)

    def panel(step):
        return call(
            functools.partial(panel_body, wide_count, length, block, step),
            shape((block, columns), BF16 if step else F32),
            mine, given, *grads, name="panel" + str(step),
        )

    arrived = []
    for step in range(1, parts):
        ring = [(i, (i + 2 * step) % ctx_count) for i in range(ctx_count)]
        arrived.append(lax.ppermute(panel(step), "ctx", ring))
    dk, dv = call(join_body, (shape((length, columns), BF16),) * 2, own, later, name="join")
    grad_wq = call(add_body, shape((block, columns), F32), panel(0), *arrived, name="add")
    return (dq[None], dk[None], dv[None], grad_wq[None])


def solution(mesh):
    rows = P("wide", "ctx", "head")
    return jax.shard_map(
        shards,
        mesh=mesh,
        in_specs=(rows, rows, rows, rows, P("wide", "ctx"), P(None, "ctx", "wide")),
        out_specs=(rows, rows, rows, rows),
        check_vma=False,
    )
```

time: 79.9 us -> 38.6 us (0.48)
  Pallas kernels: 0 us -> 18.5 us
  waiting for transfers between devices: 23.8 us -> 8.58 us
  between operations: 14.3 us -> 0.72 us
  matrix products: 10.5 us -> 0 us
  local copies, waits for them, and re-layouts: 12.1 us -> 3.14 us
  blocking collectives: 6.28 us -> 0 us
  starting transfers between devices: 11.7 us -> 7.32 us
    reduce_scatter x1 -> x0, waiting for transfers between devices: 21.4 us -> none  [shards(): lax.psum_scatter(panel_sum, 'ctx', scatter_dimension=0, tiled=True)]
    pallas_call x0 -> x7, Pallas kernels: none -> 18.5 us  [call(): pl.pallas_call(body, out_shape=outs, in_specs=[whole] * len(args), out_sp...]
    dot_general x11 -> x0, matrix products: 10.5 us -> none  [the longest x4 3.87 us: head_scores(): jnp.einsum('ihd,jhd->hij', left_heads, right_heads, preferred_element_typ...]
    all_gather x1 -> x0, blocking collectives: 6.28 us -> none  [shards(): lax.all_gather(grad_query, 'wide', axis=0, tiled=True)]
    ppermute x5 -> x9, waiting for transfers between devices: 2.34 us -> 8.58 us  [the longest x1 3.59 us: shards(): pseg = lax.ppermute(segment, 'ctx', onward)]
    unnamed x25 -> x24, local copies, waits for them, and re-layouts: 8.25 us -> 3.14 us
    ppermute x5 -> x9, starting transfers between devices: 11.7 us -> 7.32 us  [the longest x1 2.6 us: shards(): pv = lax.ppermute(v, 'ctx', onward)]
    reshape x4 -> x0, local copies, waits for them, and re-layouts: 3.82 us -> none  [the longest x1 1 us: shards(): key_heads = key_rows.reshape(length, head_count, HD)]
  transfers between devices with their start and end apart: 6 -> 9, of which waited for: 2 -> 3; matrix products, arithmetic and copies ran while one was open for 17% -> 0% of each run, Pallas kernels for 0% -> 34%
where the time goes in v1:
time: 38.6 us; the launch traced here: 38.2 us
  Pallas kernels  18.5 us (48%)
  waiting for transfers between devices  8.58 us (22%)
  starting transfers between devices  7.32 us (19%)
  local copies, waits for them, and re-layouts  3.14 us (8%)
  between operations  0.72 us (2%)
    pallas_call x7, Pallas kernels, call(): pl.pallas_call(body, out_shape=outs, in_specs=[whole] * len(args), out_sp...  18.5 us
    ppermute x1, waiting for transfers between devices, shards(): pseg = lax.ppermute(segment, 'ctx', onward)  3.59 us
    ppermute x1, waiting for transfers between devices, shards(): piece = lax.ppermute(dq, 'wide', ring) if step else dq  3.57 us
    unnamed x24, local copies, waits for them, and re-layouts  3.14 us
    ppermute x1, starting transfers between devices, shards(): pv = lax.ppermute(v, 'ctx', onward)  2.6 us
    ppermute x1, starting transfers between devices, shards(): later = lax.ppermute(to_prior, 'ctx', back)  1.7 us
    ppermute x1, starting transfers between devices, shards(): piece = lax.ppermute(dq, 'wide', ring) if step else dq  1.6 us
    ppermute x1, waiting for transfers between devices, shards(): arrived.append(lax.ppermute(panel(step), 'ctx', ring))  1.4 us
  transfers between devices with their start and end apart: 9, of which 3 were waited for; matrix products, arithmetic and copies ran while one was open for 0% of the time, Pallas kernels for 34%

profile of v1, /device:TPU:0, one launch (start us, length us, event | category | flops | bytes accessed | tf_op | source)
XLA Modules:
  0.0 38.2 jit_solution(4909959513227762969)
XLA Ops:
  0.7 3.6 %turn.1 = (bf16[2,512,512]{2,1,0:T(8,128)(2,1)}, bf16[2,512,512]{2,1,0:T(8,128)(2,1)}) custom-call(bf16[2,256,2048]{2,1,0:T(8,128)(2,1)} %frames.1), custom_call_target="tpu_custom_call" | custom-call | flops 1048576 | bytes 2097152 | tf_op jit(solution)/shard_map/turn/pallas_call | solution.py:24
  4.2 0.5 %collective-permute-start.4 = (bf16[2,512,512]{2,1,0:T(8,128)(2,1)}, bf16[2,512,512]{2,1,0:T(8,128)(2,1)S(1)}, u32[]{:S(2)}, u32[]{:S(2)}) collective-permute-start(bf16[2,512,512]{2,1,0:T(8,128)(2,1)} %get-tuple-element.21), channel_id=1, source_target_pairs={{0,8},{8,0},{16,24},{24,16},{1,9},{9,1},{17,25},{25,17},{2,10},{10... | collective-permute-start | bytes 3145736 | tf_op jit(solution)/shard_map/ppermute | solution.py:152
  4.8 2.6 %collective-permute-start.1 = (bf16[256,256]{1,0:T(8,128)(2,1)S(1)}, bf16[256,256]{1,0:T(8,128)(2,1)S(1)}, u32[]{:S(2)}, u32[]{:S(2)}) collective-permute-start(bf16[256,256]{1,0:T(8,128)(2,1)S(1)} %bitcast.17), channel_id=1, source_target_pairs={{0,8},{8,16},{16,24},{24,0},{1,9},{9,17},{17,25},{25,1},{2,10},{10... | collective-permute-start | bytes 393224 | tf_op jit(solution)/shard_map/ppermute | solution.py:146
  7.4 0.5 %collective-permute-start.2 = (s32[1,256]{1,0:T(1,128)S(1)}, s32[1,256]{1,0:T(1,128)S(1)}, u32[]{:S(2)}, u32[]{:S(2)}) collective-permute-start(s32[1,256]{1,0:T(1,128)S(1)} %copy-done.10), channel_id=1, source_target_pairs={{0,8},{8,16},{16,24},{24,0},{1,9},{9,17},{17,25},{25,1},{2,10},{10... | collective-permute-start | bytes 3080 | tf_op jit(solution)/shard_map/ppermute | solution.py:144
  7.9 3.6 %collective-permute-done.2.pseg = s32[1,256]{1,0:T(1,128)S(1)} collective-permute-done((s32[1,256]{1,0:T(1,128)S(1)}, s32[1,256]{1,0:T(1,128)S(1)}, u32[]{:S(2)}, u32[]{:S(2)}) %collective-permute-start.2) | collective-permute-done | bytes 1056 | tf_op jit(solution)/shard_map/ppermute | solution.py:144
  11.5 0.5 %copy-done.11 = s32[1,256]{1,0:T(1,128)} copy-done((s32[1,256]{1,0:T(1,128)}, s32[1,256]{1,0:T(1,128)S(1)}, u32[]{:S(2)}) %copy-start.11) | copy-done | bytes 1048
  12.0 0.1 copy-done.8
  12.1 0.0 copy-done.9
  12.2 2.9 %scores.1 = (bf16[256,256]{1,0:T(8,128)(2,1)}, bf16[2,256,256]{2,1,0:T(8,128)(2,1)}, bf16[2,256,256]{2,1,0:T(8,128)(2,1)}) custom-call(bf16[256,256]{1,0:T(8,128)(2,1)} %bitcast.10, bf16[256,256]{1,0:T(8,128)(2,1)} %bitcast.14, bf16[256,256]{1,0:T(8,128)(2,1)} %bitcast.16, bf16[256,256]{1,0:T(8,128)(2,1)} %bitcast.12, bf16[256,256]{1,0:T(8,128)(2,1)} %copy-done.8, ...), custom_call_target="tpu_custom_call" | custom-call | flops 1048576 | bytes 788480 | tf_op jit(solution)/shard_map/scores/pallas_call | solution.py:24
  15.1 1.6 %collective-permute-start.6 = (bf16[256,256]{1,0:T(8,128)(2,1)}, bf16[256,256]{1,0:T(8,128)(2,1)S(1)}, u32[]{:S(2)}, u32[]{:S(2)}) collective-permute-start(bf16[256,256]{1,0:T(8,128)(2,1)} %get-tuple-element.13.refs_2_), channel_id=1, source_target_pairs={{0,1},{1,0},{2,3},{3,2},{4,5},{5,4},{6,7},{7,6},{8,9},{9,8},{10,11... | collective-permute-start | bytes 393224 | tf_op jit(solution)/shard_map/ppermute | solution.py:163
  16.7 3.6 %collective-permute-done.6.refs_4_ = bf16[256,256]{1,0:T(8,128)(2,1)S(1)} collective-permute-done((bf16[256,256]{1,0:T(8,128)(2,1)}, bf16[256,256]{1,0:T(8,128)(2,1)S(1)}, u32[]{:S(2)}, u32[]{:S(2)}) %collective-permute-start.6) | collective-permute-done | bytes 131104 | tf_op jit(solution)/shard_map/ppermute | solution.py:163
  20.3 2.5 %terms.1 = (f32[2,256,256]{2,1,0:T(8,128)}, bf16[2,256,256]{2,1,0:T(8,128)(2,1)}) custom-call(bf16[256,256]{1,0:T(8,128)(2,1)} %bitcast.11, bf16[256,256]{1,0:T(8,128)(2,1)} %bitcast.13, bf16[2,256,256]{2,1,0:T(8,128)(2,1)} %get-tuple-element.14.ds, bf16[2,256,256]{2,1,0:T(8,128)(2,1)} %get-tuple-element.15.p), custom_call_target="tpu_custom_call" | custom-call | flops 1048576 | bytes 786432 | tf_op jit(solution)/shard_map/terms/pallas_call | solution.py:24
  22.8 1.7 %collective-permute-start.3 = (bf16[2,256,256]{2,1,0:T(8,128)(2,1)}, bf16[2,256,256]{2,1,0:T(8,128)(2,1)S(1)}, u32[]{:S(2)}, u32[]{:S(2)}) collective-permute-start(bf16[2,256,256]{2,1,0:T(8,128)(2,1)} %get-tuple-element.17), channel_id=1, source_target_pairs={{0,24},{8,0},{16,8},{24,16},{1,25},{9,1},{17,9},{25,17},{2,26},{10... | collective-permute-start | bytes 786440 | tf_op jit(solution)/shard_map/ppermute | solution.py:171
  24.5 0.6 %copy-done.2 = bf16[256,256]{1,0:T(8,128)(2,1)} copy-done((bf16[256,256]{1,0:T(8,128)(2,1)}, bf16[256,256]{1,0:T(8,128)(2,1)S(1)}, u32[]{:S(2)}) %copy-start.2) | copy-done | bytes 131096
  25.2 0.0 copy-done.3
  25.2 0.4 copy-done
  25.5 2.8 %panel1.1 = bf16[512,256]{1,0:T(8,128)(2,1)} custom-call(bf16[2,512,512]{2,1,0:T(8,128)(2,1)} %get-tuple-element.20.refs_0_, bf16[2,512,512]{2,1,0:T(8,128)(2,1)} %copy-done, bf16[256,256]{1,0:T(8,128)(2,1)} %get-tuple-element.13.refs_2_, bf16[256,256]{1,0:T(8,128)(2,1)} %copy-done.2, bf16[256,256]{1,0:T(8,128)(2,1)} %copy-done.1, bf16[256,256]{1,0:T(8,128)(2,1)} %copy-done.3), custom_call_target="tpu_custom_call" | custom-call | flops 1048576 | bytes 2621440 | tf_op jit(solution)/shard_map/panel1/pallas_call | solution.py:24
  28.4 0.4 %collective-permute-start.8 = (bf16[512,256]{1,0:T(8,128)(2,1)}, bf16[512,256]{1,0:T(8,128)(2,1)S(1)}, u32[]{:S(2)}, u32[]{:S(2)}) collective-permute-start(bf16[512,256]{1,0:T(8,128)(2,1)} %panel1.1), channel_id=1, source_target_pairs={{0,16},{8,24},{16,0},{24,8},{1,17},{9,25},{17,1},{25,9},{2,18},{10... | collective-permute-start | bytes 786440 | tf_op jit(solution)/shard_map/ppermute | solution.py:183
  28.8 0.7 %copy-done.4 = bf16[2,256,256]{2,1,0:T(8,128)(2,1)} copy-done((bf16[2,256,256]{2,1,0:T(8,128)(2,1)}, bf16[2,256,256]{2,1,0:T(8,128)(2,1)S(1)}, u32[]{:S(2)}) %copy-start.4) | copy-done | bytes 262168
  29.5 1.8 %join.1 = (bf16[256,256]{1,0:T(8,128)(2,1)}, bf16[256,256]{1,0:T(8,128)(2,1)}) custom-call(f32[2,256,256]{2,1,0:T(8,128)} %get-tuple-element.16.own, bf16[2,256,256]{2,1,0:T(8,128)(2,1)} %copy-done.4), custom_call_target="tpu_custom_call" | custom-call | flops 1048576 | bytes 786432 | tf_op jit(solution)/shard_map/join/pallas_call | solution.py:24
  31.3 2.9 %panel0.1.refs_0_ = f32[512,256]{1,0:T(8,128)} custom-call(bf16[2,512,512]{2,1,0:T(8,128)(2,1)} %get-tuple-element.20.refs_0_, bf16[2,512,512]{2,1,0:T(8,128)(2,1)} %copy-done, bf16[256,256]{1,0:T(8,128)(2,1)} %get-tuple-element.13.refs_2_, bf16[256,256]{1,0:T(8,128)(2,1)} %copy-done.2, bf16[256,256]{1,0:T(8,128)(2,1)} %copy-done.1, bf16[256,256]{1,0:T(8,128)(2,1)} %copy-done.3), custom_call_target="tpu_custom_call" | custom-call | flops 1048576 | bytes 2621440 | tf_op jit(solution)/shard_map/panel0/pallas_call | solution.py:24
  34.2 1.4 %collective-permute-done.8.refs_1_ = bf16[512,256]{1,0:T(8,128)(2,1)S(1)} collective-permute-done((bf16[512,256]{1,0:T(8,128)(2,1)}, bf16[512,256]{1,0:T(8,128)(2,1)S(1)}, u32[]{:S(2)}, u32[]{:S(2)}) %collective-permute-start.8) | collective-permute-done | bytes 262176 | tf_op jit(solution)/shard_map/ppermute | solution.py:183
  35.6 0.7 %copy-done.5 = bf16[512,256]{1,0:T(8,128)(2,1)} copy-done((bf16[512,256]{1,0:T(8,128)(2,1)}, bf16[512,256]{1,0:T(8,128)(2,1)S(1)}, u32[]{:S(2)}) %copy-start.5) | copy-done | bytes 262168
  36.3 1.9 %add.1 = f32[512,256]{1,0:T(8,128)} custom-call(f32[512,256]{1,0:T(8,128)} %panel0.1.refs_0_, bf16[512,256]{1,0:T(8,128)(2,1)} %copy-done.5), custom_call_target="tpu_custom_call" | custom-call | flops 1048576 | bytes 786432 | tf_op jit(solution)/shard_map/add/pallas_call | solution.py:24
  (25 shorter events, 0.1 us)
Async XLA Ops:
  0.6 4.1 %copy-start.6 = (bf16[1,256,256]{2,1,0:T(8,128)(2,1)S(1)}, bf16[1,256,256]{2,1,0:T(8,128)(2,1)}, u32[]{:S(2)}) copy-start(bf16[1,256,256]{2,1,0:T(8,128)(2,1)} %param.7) | copy-start | bytes 393220
  0.6 4.1 %copy-start.7 = (bf16[1,256,256]{2,1,0:T(8,128)(2,1)S(1)}, bf16[1,256,256]{2,1,0:T(8,128)(2,1)}, u32[]{:S(2)}) copy-start(bf16[1,256,256]{2,1,0:T(8,128)(2,1)} %param.8) | copy-start | bytes 393220
  0.7 6.7 %copy-start.10 = (s32[1,256]{1,0:T(1,128)S(1)}, s32[1,256]{1,0:T(1,128)}, u32[]{:S(2)}) copy-start(s32[1,256]{1,0:T(1,128)} %seg.1) | copy-start | bytes 3076
  4.2 20.3 %collective-permute-start.4 = (bf16[2,512,512]{2,1,0:T(8,128)(2,1)}, bf16[2,512,512]{2,1,0:T(8,128)(2,1)S(1)}, u32[]{:S(2)}, u32[]{:S(2)}) collective-permute-start(bf16[2,512,512]{2,1,0:T(8,128)(2,1)} %get-tuple-element.21), channel_id=1, source_target_pairs={{0,8},{8,0},{16,24},{24,16},{1,9},{9,1},{17,25},{25,17},{2,10},{10... | collective-permute-start | bytes 3145736 | tf_op jit(solution)/shard_map/ppermute | solution.py:152
  4.7 6.7 %collective-permute-start = (bf16[256,256]{1,0:T(8,128)(2,1)S(1)}, bf16[256,256]{1,0:T(8,128)(2,1)S(1)}, u32[]{:S(2)}, u32[]{:S(2)}) collective-permute-start(bf16[256,256]{1,0:T(8,128)(2,1)S(1)} %bitcast.15), channel_id=1, source_target_pairs={{0,8},{8,16},{16,24},{24,0},{1,9},{9,17},{17,25},{25,1},{2,10},{10... | collective-permute-start | bytes 393224 | tf_op jit(solution)/shard_map/ppermute | solution.py:145
  4.8 6.7 %collective-permute-start.1 = (bf16[256,256]{1,0:T(8,128)(2,1)S(1)}, bf16[256,256]{1,0:T(8,128)(2,1)S(1)}, u32[]{:S(2)}, u32[]{:S(2)}) collective-permute-start(bf16[256,256]{1,0:T(8,128)(2,1)S(1)} %bitcast.17), channel_id=1, source_target_pairs={{0,8},{8,16},{16,24},{24,0},{1,9},{9,17},{17,25},{25,1},{2,10},{10... | collective-permute-start | bytes 393224 | tf_op jit(solution)/shard_map/ppermute | solution.py:146
  7.4 4.1 %collective-permute-start.2 = (s32[1,256]{1,0:T(1,128)S(1)}, s32[1,256]{1,0:T(1,128)S(1)}, u32[]{:S(2)}, u32[]{:S(2)}) collective-permute-start(s32[1,256]{1,0:T(1,128)S(1)} %copy-done.10), channel_id=1, source_target_pairs={{0,8},{8,16},{16,24},{24,0},{1,9},{9,17},{17,25},{25,1},{2,10},{10... | collective-permute-start | bytes 3080 | tf_op jit(solution)/shard_map/ppermute | solution.py:144
  11.5 0.6 %copy-start.11 = (s32[1,256]{1,0:T(1,128)}, s32[1,256]{1,0:T(1,128)S(1)}, u32[]{:S(2)}) copy-start(s32[1,256]{1,0:T(1,128)S(1)} %collective-permute-done.2.pseg) | copy-start | bytes 3076
  11.5 0.7 %copy-start.8 = (bf16[256,256]{1,0:T(8,128)(2,1)}, bf16[256,256]{1,0:T(8,128)(2,1)S(1)}, u32[]{:S(2)}) copy-start(bf16[256,256]{1,0:T(8,128)(2,1)S(1)} %collective-permute-done.pk) | copy-start | bytes 393220
  11.5 0.7 %copy-start.9 = (bf16[256,256]{1,0:T(8,128)(2,1)}, bf16[256,256]{1,0:T(8,128)(2,1)S(1)}, u32[]{:S(2)}) copy-start(bf16[256,256]{1,0:T(8,128)(2,1)S(1)} %collective-permute-done.1.pv) | copy-start | bytes 393220
  15.1 5.2 %collective-permute-start.6 = (bf16[256,256]{1,0:T(8,128)(2,1)}, bf16[256,256]{1,0:T(8,128)(2,1)S(1)}, u32[]{:S(2)}, u32[]{:S(2)}) collective-permute-start(bf16[256,256]{1,0:T(8,128)(2,1)} %get-tuple-element.13.refs_2_), channel_id=1, source_target_pairs={{0,1},{1,0},{2,3},{3,2},{4,5},{5,4},{6,7},{7,6},{8,9},{9,8},{10,11... | collective-permute-start | bytes 393224 | tf_op jit(solution)/shard_map/ppermute | solution.py:163
  16.7 7.8 %collective-permute-start.5 = (bf16[256,256]{1,0:T(8,128)(2,1)}, bf16[256,256]{1,0:T(8,128)(2,1)S(1)}, u32[]{:S(2)}, u32[]{:S(2)}) collective-permute-start(bf16[256,256]{1,0:T(8,128)(2,1)} %get-tuple-element.13.refs_2_), channel_id=1, source_target_pairs={{0,8},{8,0},{16,24},{24,16},{1,9},{9,1},{17,25},{25,17},{2,10},{10... | collective-permute-start | bytes 393224 | tf_op jit(solution)/shard_map/ppermute | solution.py:164
  20.3 4.2 %copy-start.1 = (bf16[256,256]{1,0:T(8,128)(2,1)}, bf16[256,256]{1,0:T(8,128)(2,1)S(1)}, u32[]{:S(2)}) copy-start(bf16[256,256]{1,0:T(8,128)(2,1)S(1)} %collective-permute-done.6.refs_4_) | copy-start | bytes 393220
  20.3 4.2 %collective-permute-start.7 = (bf16[256,256]{1,0:T(8,128)(2,1)S(1)}, bf16[256,256]{1,0:T(8,128)(2,1)S(1)}, u32[]{:S(2)}, u32[]{:S(2)}) collective-permute-start(bf16[256,256]{1,0:T(8,128)(2,1)S(1)} %collective-permute-done.6.refs_4_), channel_id=1, source_target_pairs={{0,8},{8,0},{16,24},{24,16},{1,9},{9,1},{17,25},{25,17},{2,10},{10... | collective-permute-start | bytes 393224 | tf_op jit(solution)/shard_map/ppermute | solution.py:164
  22.8 6.0 %collective-permute-start.3 = (bf16[2,256,256]{2,1,0:T(8,128)(2,1)}, bf16[2,256,256]{2,1,0:T(8,128)(2,1)S(1)}, u32[]{:S(2)}, u32[]{:S(2)}) collective-permute-start(bf16[2,256,256]{2,1,0:T(8,128)(2,1)} %get-tuple-element.17), channel_id=1, source_target_pairs={{0,24},{8,0},{16,8},{24,16},{1,25},{9,1},{17,9},{25,17},{2,26},{10... | collective-permute-start | bytes 786440 | tf_op jit(solution)/shard_map/ppermute | solution.py:171
  24.5 0.7 %copy-start.2 = (bf16[256,256]{1,0:T(8,128)(2,1)}, bf16[256,256]{1,0:T(8,128)(2,1)S(1)}, u32[]{:S(2)}) copy-start(bf16[256,256]{1,0:T(8,128)(2,1)S(1)} %collective-permute-done.5.refs_3_) | copy-start | bytes 393220
  24.5 0.7 %copy-start.3 = (bf16[256,256]{1,0:T(8,128)(2,1)}, bf16[256,256]{1,0:T(8,128)(2,1)S(1)}, u32[]{:S(2)}) copy-start(bf16[256,256]{1,0:T(8,128)(2,1)S(1)} %collective-permute-done.7.refs_5_) | copy-start | bytes 393220
  24.5 1.0 %copy-start = (bf16[2,512,512]{2,1,0:T(8,128)(2,1)}, bf16[2,512,512]{2,1,0:T(8,128)(2,1)S(1)}, u32[]{:S(2)}) copy-start(bf16[2,512,512]{2,1,0:T(8,128)(2,1)S(1)} %collective-permute-done.4.refs_1_) | copy-start | bytes 3145732
  28.4 7.2 %collective-permute-start.8 = (bf16[512,256]{1,0:T(8,128)(2,1)}, bf16[512,256]{1,0:T(8,128)(2,1)S(1)}, u32[]{:S(2)}, u32[]{:S(2)}) collective-permute-start(bf16[512,256]{1,0:T(8,128)(2,1)} %panel1.1), channel_id=1, source_target_pairs={{0,16},{8,24},{16,0},{24,8},{1,17},{9,25},{17,1},{25,9},{2,18},{10... | collective-permute-start | bytes 786440 | tf_op jit(solution)/shard_map/ppermute | solution.py:183
  28.8 0.7 %copy-start.4 = (bf16[2,256,256]{2,1,0:T(8,128)(2,1)}, bf16[2,256,256]{2,1,0:T(8,128)(2,1)S(1)}, u32[]{:S(2)}) copy-start(bf16[2,256,256]{2,1,0:T(8,128)(2,1)S(1)} %collective-permute-done.3.later) | copy-start | bytes 786436
  35.6 0.7 %copy-start.5 = (bf16[512,256]{1,0:T(8,128)(2,1)}, bf16[512,256]{1,0:T(8,128)(2,1)S(1)}, u32[]{:S(2)}) copy-start(bf16[512,256]{1,0:T(8,128)(2,1)S(1)} %collective-permute-done.8.refs_1_) | copy-start | bytes 786436

commit v2 on v1

--- a/solution.py
+++ b/solution.py
@@ -7,6 +7,7 @@
 from jax.experimental.pallas import tpu as pltpu
 from jax.sharding import PartitionSpec as P
 
+
 HD = 128
 F32 = jnp.float32
 BF16 = jnp.bfloat16
@@ -18,16 +19,20 @@
     )
 
 
-def call(body, outs, *args, flops=1 << 20, name=None):
+def vmem(dims, dtype):
+    return pltpu.VMEM(dims, dtype)
+
+
+def call(body, outs, *args, cost=1):
     whole = pl.BlockSpec(memory_space=pltpu.VMEM)
-    size = sum(a.size * a.dtype.itemsize for a in args)
+    args = [pltpu.with_memory_space_constraint(a, pltpu.VMEM) for a in args]
     return pl.pallas_call(
         body,
         out_shape=outs,
         in_specs=[whole] * len(args),
-        out_specs=jax.tree.map(lambda _: whole, outs),
-        cost_estimate=pl.CostEstimate(flops=flops, bytes_accessed=size, transcendentals=0),
-        name=name,
+        out_specs=jax.tree.map(lambda _: whole, outs, is_leaf=lambda o: not isinstance(o, tuple)),
+        cost_estimate=pl.CostEstimate(flops=cost << 20, bytes_accessed=1 << 20, transcendentals=0),
+        compiler_params=pltpu.CompilerParams(vmem_limit_bytes=24 << 20),
     )(*args)
 
 
@@ -106,7 +111,7 @@
                         out[part, :, r * length : (r + 1) * length] = jnp.transpose(tile)
 
 
-def panel_body(count, length, block, step, *refs):
+def panel_body(count, length, step, *refs):
     frames, grads, out = refs[:2], refs[2:-1], refs[-1]
     part = lax.rem(lax.div(lax.axis_index("ctx"), 2) + step, lax.axis_size("ctx") // 2)
     wide = lax.axis_index("wide")
@@ -145,44 +150,48 @@
     pk = lax.ppermute(k, "ctx", onward)
     pv = lax.ppermute(v, "ctx", onward)
 
-    turned = shape((parts, block, recs * length), BF16)
+    turned = vmem((parts, block, recs * length), BF16)
     mine, theirs = call(
-        functools.partial(turn_body, recs, length, block, parts), (turned, turned), frames, name="turn"
+        functools.partial(turn_body, recs, length, block, parts), (turned, turned), frames
     )
     given = lax.ppermute(theirs, "ctx", other)
 
-    square = shape((heads, length, length), BF16)
+    square = vmem((heads, length, length), BF16)
     dq, ds, p = call(
         functools.partial(scores_body, length, heads),
-        (shape((length, columns), BF16), square, square),
-        q, k, v, g, pk, pv, segment, pseg, name="scores",
+        (vmem((length, columns), BF16), square, square),
+        q, k, v, g, pk, pv, segment, pseg,
     )
     grads = []
     for step in range(wide_count):
         ring = [(i, (i + step) % wide_count) for i in range(wide_count)]
-        piece = lax.ppermute(dq, "wide", ring) if step else dq
+        piece = dq
+        if step:
+            piece = lax.ppermute(dq, "wide", ring)
         grads += [piece, lax.ppermute(piece, "ctx", other)]
 
     own, to_prior = call(
         functools.partial(terms_body, length, heads),
-        (shape((2, length, columns), F32), shape((2, length, columns), BF16)),
-        q, g, ds, p, name="terms",
+        (vmem((2, length, columns), F32), vmem((2, length, columns), BF16)),
+        q, g, ds, p,
     )
     later = lax.ppermute(to_prior, "ctx", back)
 
     def panel(step):
         return call(
-            functools.partial(panel_body, wide_count, length, block, step),
-            shape((block, columns), BF16 if step else F32),
-            mine, given, *grads, name="panel" + str(step),
+            functools.partial(panel_body, wide_count, length, step),
+            vmem((block, columns), BF16 if step else F32),
+            mine, given, *grads,
         )
 
     arrived = []
     for step in range(1, parts):
         ring = [(i, (i + 2 * step) % ctx_count) for i in range(ctx_count)]
-        arrived.append(lax.ppermute(panel(step), "ctx", ring))
-    dk, dv = call(join_body, (shape((length, columns), BF16),) * 2, own, later, name="join")
-    grad_wq = call(add_body, shape((block, columns), F32), panel(0), *arrived, name="add")
+        piece = panel(step)
+        arrived.append(lax.ppermute(piece, "ctx", ring))
+    dk, dv = call(join_body, (shape((length, columns), BF16),) * 2, own, later)
+    kept = panel(0)
+    grad_wq = call(add_body, shape((block, columns), F32), kept, *arrived)
     return (dq[None], dk[None], dv[None], grad_wq[None])
 
 

time: 38.6 us -> 29.8 us (0.77)
  Pallas kernels: 18.5 us -> 4.53 us
  waiting for transfers between devices: 8.58 us -> 13.8 us
  starting transfers between devices: 7.32 us -> 8.36 us
  local copies, waits for them, and re-layouts: 3.14 us -> 2.26 us
    pallas_call x7, Pallas kernels: 18.5 us -> 4.53 us  [call(): pl.pallas_call(body, out_shape=outs, in_specs=[whole] * len(args), out_sp...]
    ppermute x1, waiting for transfers between devices: 0.01 us -> 4.33 us  [shards(): later = lax.ppermute(to_prior, 'ctx', back)]
    ppermute x2, waiting for transfers between devices: 4.97 us -> 5.9 us  [the longest x1 3.17 us: shards(): piece = lax.ppermute(dq, 'wide', ring)]
    unnamed x24 -> x13, local copies, waits for them, and re-layouts: 3.14 us -> 2.26 us
    ppermute x2, starting transfers between devices: 2 us -> 2.67 us  [the longest x1 1.86 us: shards(): piece = lax.ppermute(dq, 'wide', ring)]
  transfers between devices with their start and end apart: 9 -> 9, of which waited for: 3 -> 4; matrix products, arithmetic and copies ran while one was open for 0% -> 2% of each run, Pallas kernels for 34% -> 10%
where the time goes in v2:
time: 29.8 us; the launch traced here: 29.7 us
  waiting for transfers between devices  13.8 us (46%)
  starting transfers between devices  8.36 us (28%)
  Pallas kernels  4.53 us (15%)
  local copies, waits for them, and re-layouts  2.26 us (8%)
  between operations  0.71 us (2%)
    pallas_call x7, Pallas kernels, call(): pl.pallas_call(body, out_shape=outs, in_specs=[whole] * len(args), out_sp...  4.53 us
    ppermute x1, waiting for transfers between devices, shards(): later = lax.ppermute(to_prior, 'ctx', back)  4.33 us
    ppermute x1, waiting for transfers between devices, shards(): pseg = lax.ppermute(segment, 'ctx', onward)  3.59 us
    ppermute x1, waiting for transfers between devices, shards(): piece = lax.ppermute(dq, 'wide', ring)  3.17 us
    ppermute x1, waiting for transfers between devices, shards(): arrived.append(lax.ppermute(piece, 'ctx', ring))  2.74 us
    ppermute x1, starting transfers between devices, shards(): pv = lax.ppermute(v, 'ctx', onward)  2.62 us
    unnamed x13, local copies, waits for them, and re-layouts  2.26 us
    ppermute x1, starting transfers between devices, shards(): later = lax.ppermute(to_prior, 'ctx', back)  1.99 us
  transfers between devices with their start and end apart: 9, of which 4 were waited for; matrix products, arithmetic and copies ran while one was open for 2% of the time, Pallas kernels for 10%

profile of v2, /device:TPU:0, one launch (start us, length us, event | category | flops | bytes accessed | tf_op | source)
XLA Modules:
  0.0 29.7 jit_solution(2605115787418480550)
XLA Ops:
  0.6 1.6 %copy-done = bf16[2,256,2048]{2,1,0:T(8,128)(2,1)S(1)} copy-done((bf16[2,256,2048]{2,1,0:T(8,128)(2,1)S(1)}, bf16[2,256,2048]{2,1,0:T(8,128)(2,1)}, u32[]{:S(2)}) %copy-start) | copy-done | bytes 2097176
  2.2 0.6 %shard_map.96 = (bf16[2,512,512]{2,1,0:T(8,128)(2,1)S(1)}, bf16[2,512,512]{2,1,0:T(8,128)(2,1)S(1)}) custom-call(bf16[2,256,2048]{2,1,0:T(8,128)(2,1)S(1)} %copy-done), custom_call_target="tpu_custom_call" | custom-call | flops 1048576 | bytes 1048576 | tf_op jit(solution)/shard_map/pallas_call | solution.py:29
  2.9 0.6 %collective-permute-start.4 = (bf16[2,512,512]{2,1,0:T(8,128)(2,1)S(1)}, bf16[2,512,512]{2,1,0:T(8,128)(2,1)S(1)}, u32[]{:S(2)}, u32[]{:S(2)}) collective-permute-start(bf16[2,512,512]{2,1,0:T(8,128)(2,1)S(1)} %get-tuple-element.21), channel_id=1, source_target_pairs={{0,8},{8,0},{16,24},{24,16},{1,9},{9,1},{17,25},{25,17},{2,10},{10... | collective-permute-start | bytes 3145736 | tf_op jit(solution)/shard_map/ppermute | solution.py:157
  3.4 0.2 collective-permute-start
  3.6 2.6 %collective-permute-start.1 = (bf16[256,256]{1,0:T(8,128)(2,1)S(1)}, bf16[256,256]{1,0:T(8,128)(2,1)S(1)}, u32[]{:S(2)}, u32[]{:S(2)}) collective-permute-start(bf16[256,256]{1,0:T(8,128)(2,1)S(1)} %bitcast.15), channel_id=1, source_target_pairs={{0,8},{8,16},{16,24},{24,0},{1,9},{9,17},{17,25},{25,1},{2,10},{10... | collective-permute-start | bytes 393224 | tf_op jit(solution)/shard_map/ppermute | solution.py:151
  6.2 0.3 %collective-permute-start.2 = (s32[1,256]{1,0:T(1,128)S(1)}, s32[1,256]{1,0:T(1,128)S(1)}, u32[]{:S(2)}, u32[]{:S(2)}) collective-permute-start(s32[1,256]{1,0:T(1,128)S(1)} %copy-done.5), channel_id=1, source_target_pairs={{0,8},{8,16},{16,24},{24,0},{1,9},{9,17},{17,25},{25,1},{2,10},{10... | collective-permute-start | bytes 3080 | tf_op jit(solution)/shard_map/ppermute | solution.py:149
  6.6 3.6 %collective-permute-done.2.pseg = s32[1,256]{1,0:T(1,128)S(1)} collective-permute-done((s32[1,256]{1,0:T(1,128)S(1)}, s32[1,256]{1,0:T(1,128)S(1)}, u32[]{:S(2)}, u32[]{:S(2)}) %collective-permute-start.2) | collective-permute-done | bytes 1056 | tf_op jit(solution)/shard_map/ppermute | solution.py:149
  10.1 0.0 collective-permute-done.pk
  10.2 0.0 collective-permute-done.1.pv
  10.2 1.1 %shard_map.93 = (bf16[256,256]{1,0:T(8,128)(2,1)S(1)}, bf16[2,256,256]{2,1,0:T(8,128)(2,1)S(1)}, bf16[2,256,256]{2,1,0:T(8,128)(2,1)S(1)}) custom-call(bf16[256,256]{1,0:T(8,128)(2,1)S(1)} %bitcast.9, bf16[256,256]{1,0:T(8,128)(2,1)S(1)} %bitcast.14, bf16[256,256]{1,0:T(8,128)(2,1)S(1)} %bitcast.16, bf16[256,256]{1,0:T(8,128)(2,1)S(1)} %bitcast.11, ...), custom_call_target="tpu_custom_call" | custom-call | flops 1048576 | bytes 1048576 | tf_op jit(solution)/shard_map/pallas_call | solution.py:29
  11.2 1.9 %collective-permute-start.6 = (bf16[256,256]{1,0:T(8,128)(2,1)S(1)}, bf16[256,256]{1,0:T(8,128)(2,1)S(1)}, u32[]{:S(2)}, u32[]{:S(2)}) collective-permute-start(bf16[256,256]{1,0:T(8,128)(2,1)S(1)} %get-tuple-element.13.refs_2_), channel_id=1, source_target_pairs={{0,1},{1,0},{2,3},{3,2},{4,5},{5,4},{6,7},{7,6},{8,9},{9,8},{10,11... | collective-permute-start | bytes 393224 | tf_op jit(solution)/shard_map/ppermute | solution.py:170
  13.1 3.2 %collective-permute-done.6.refs_4_ = bf16[256,256]{1,0:T(8,128)(2,1)S(1)} collective-permute-done((bf16[256,256]{1,0:T(8,128)(2,1)S(1)}, bf16[256,256]{1,0:T(8,128)(2,1)S(1)}, u32[]{:S(2)}, u32[]{:S(2)}) %collective-permute-start.6) | collective-permute-done | bytes 131104 | tf_op jit(solution)/shard_map/ppermute | solution.py:170
  16.3 0.4 %shard_map.94 = (f32[2,256,256]{2,1,0:T(8,128)S(1)}, bf16[2,256,256]{2,1,0:T(8,128)(2,1)S(1)}) custom-call(bf16[256,256]{1,0:T(8,128)(2,1)S(1)} %bitcast.10, bf16[256,256]{1,0:T(8,128)(2,1)S(1)} %bitcast.12, bf16[2,256,256]{2,1,0:T(8,128)(2,1)S(1)} %get-tuple-element.14.ds, bf16[2,256,256]{2,1,0:T(8,128)(2,1)S(1)} %get-tuple-element.15.p), custom_call_target="tpu_custom_call" | custom-call | flops 1048576 | bytes 1048576 | tf_op jit(solution)/shard_map/pallas_call | solution.py:29
  16.7 2.0 %collective-permute-start.3 = (bf16[2,256,256]{2,1,0:T(8,128)(2,1)S(1)}, bf16[2,256,256]{2,1,0:T(8,128)(2,1)S(1)}, u32[]{:S(2)}, u32[]{:S(2)}) collective-permute-start(bf16[2,256,256]{2,1,0:T(8,128)(2,1)S(1)} %get-tuple-element.17), channel_id=1, source_target_pairs={{0,24},{8,0},{16,8},{24,16},{1,25},{9,1},{17,9},{25,17},{2,26},{10... | collective-permute-start | bytes 786440 | tf_op jit(solution)/shard_map/ppermute | solution.py:178
  18.7 0.0 collective-permute-done.5.refs_3_
  18.7 0.0 collective-permute-done.7.refs_5_
  18.7 0.4 %shard_map.98 = bf16[512,256]{1,0:T(8,128)(2,1)S(1)} custom-call(bf16[2,512,512]{2,1,0:T(8,128)(2,1)S(1)} %get-tuple-element.20.refs_0_, bf16[2,512,512]{2,1,0:T(8,128)(2,1)S(1)} %collective-permute-done.4.refs_1_, bf16[256,256]{1,0:T(8,128)(2,1)S(1)} %get-tuple-element.13.refs_2_, bf16[256,256]{1,0:T(8,128)(2,1)S(1)} %collective-permute-done.5.refs_3_, ...), custom_call_target="tpu_custom_call" | custom-call | flops 1048576 | bytes 1048576 | tf_op jit(solution)/shard_map/pallas_call | solution.py:29
  19.1 0.8 %collective-permute-start.8 = (bf16[512,256]{1,0:T(8,128)(2,1)S(1)}, bf16[512,256]{1,0:T(8,128)(2,1)S(1)}, u32[]{:S(2)}, u32[]{:S(2)}) collective-permute-start(bf16[512,256]{1,0:T(8,128)(2,1)S(1)} %shard_map.98), channel_id=1, source_target_pairs={{0,16},{8,24},{16,0},{24,8},{1,17},{9,25},{17,1},{25,9},{2,18},{10... | collective-permute-start | bytes 786440 | tf_op jit(solution)/shard_map/ppermute | solution.py:191
  20.0 0.7 %copy.10 = bf16[1,256,256]{2,1,0:T(8,128)(2,1)} copy(bf16[1,256,256]{2,1,0:T(8,128)(2,1)S(1)} %bitcast.8) | data formatting | bytes 262144
  20.6 4.3 %collective-permute-done.3.later = bf16[2,256,256]{2,1,0:T(8,128)(2,1)S(1)} collective-permute-done((bf16[2,256,256]{2,1,0:T(8,128)(2,1)S(1)}, bf16[2,256,256]{2,1,0:T(8,128)(2,1)S(1)}, u32[]{:S(2)}, u32[]{:S(2)}) %collective-permute-start.3) | collective-permute-done | bytes 262176 | tf_op jit(solution)/shard_map/ppermute | solution.py:178
  24.9 0.7 %shard_map.95 = (bf16[256,256]{1,0:T(8,128)(2,1)}, bf16[256,256]{1,0:T(8,128)(2,1)}) custom-call(f32[2,256,256]{2,1,0:T(8,128)S(1)} %get-tuple-element.16.own, bf16[2,256,256]{2,1,0:T(8,128)(2,1)S(1)} %collective-permute-done.3.later), custom_call_target="tpu_custom_call" | custom-call | flops 1048576 | bytes 1048576 | tf_op jit(solution)/shard_map/pallas_call | solution.py:29
  25.7 0.4 %shard_map.97.refs_0_ = f32[512,256]{1,0:T(8,128)S(1)} custom-call(bf16[2,512,512]{2,1,0:T(8,128)(2,1)S(1)} %get-tuple-element.20.refs_0_, bf16[2,512,512]{2,1,0:T(8,128)(2,1)S(1)} %collective-permute-done.4.refs_1_, bf16[256,256]{1,0:T(8,128)(2,1)S(1)} %get-tuple-element.13.refs_2_, bf16[256,256]{1,0:T(8,128)(2,1)S(1)} %collective-permute-done.5.refs_3_, ...), custom_call_target="tpu_custom_call" | custom-call | flops 1048576 | bytes 1048576 | tf_op jit(solution)/shard_map/pallas_call | solution.py:29
  26.1 2.7 %collective-permute-done.8.refs_1_ = bf16[512,256]{1,0:T(8,128)(2,1)S(1)} collective-permute-done((bf16[512,256]{1,0:T(8,128)(2,1)S(1)}, bf16[512,256]{1,0:T(8,128)(2,1)S(1)}, u32[]{:S(2)}, u32[]{:S(2)}) %collective-permute-start.8) | collective-permute-done | bytes 262176 | tf_op jit(solution)/shard_map/ppermute | solution.py:191
  28.9 0.8 %shard_map.99 = f32[512,256]{1,0:T(8,128)} custom-call(f32[512,256]{1,0:T(8,128)S(1)} %shard_map.97.refs_0_, bf16[512,256]{1,0:T(8,128)(2,1)S(1)} %collective-permute-done.8.refs_1_), custom_call_target="tpu_custom_call" | custom-call | flops 1048576 | bytes 1048576 | tf_op jit(solution)/shard_map/pallas_call | solution.py:29
  (14 shorter events, 0.0 us)
Async XLA Ops:
  0.6 1.6 %copy-start = (bf16[2,256,2048]{2,1,0:T(8,128)(2,1)S(1)}, bf16[2,256,2048]{2,1,0:T(8,128)(2,1)}, u32[]{:S(2)}) copy-start(bf16[2,256,2048]{2,1,0:T(8,128)(2,1)} %frames.1) | copy-start | bytes 6291460
  2.2 1.2 %copy-start.3 = (bf16[1,256,256]{2,1,0:T(8,128)(2,1)S(1)}, bf16[1,256,256]{2,1,0:T(8,128)(2,1)}, u32[]{:S(2)}) copy-start(bf16[1,256,256]{2,1,0:T(8,128)(2,1)} %param.7) | copy-start | bytes 393220
  2.2 1.4 %copy-start.4 = (bf16[1,256,256]{2,1,0:T(8,128)(2,1)S(1)}, bf16[1,256,256]{2,1,0:T(8,128)(2,1)}, u32[]{:S(2)}) copy-start(bf16[1,256,256]{2,1,0:T(8,128)(2,1)} %param.8) | copy-start | bytes 393220
  2.2 4.0 %copy-start.5 = (s32[1,256]{1,0:T(1,128)S(1)}, s32[1,256]{1,0:T(1,128)}, u32[]{:S(2)}) copy-start(s32[1,256]{1,0:T(1,128)} %seg.1) | copy-start | bytes 3076
  2.2 7.9 %copy-start.1 = (bf16[1,256,256]{2,1,0:T(8,128)(2,1)S(1)}, bf16[1,256,256]{2,1,0:T(8,128)(2,1)}, u32[]{:S(2)}) copy-start(bf16[1,256,256]{2,1,0:T(8,128)(2,1)} %param.6) | copy-start | bytes 393220
  2.2 7.9 %copy-start.2 = (bf16[1,256,256]{2,1,0:T(8,128)(2,1)S(1)}, bf16[1,256,256]{2,1,0:T(8,128)(2,1)}, u32[]{:S(2)}) copy-start(bf16[1,256,256]{2,1,0:T(8,128)(2,1)} %param.9) | copy-start | bytes 393220
  2.9 15.8 %collective-permute-start.4 = (bf16[2,512,512]{2,1,0:T(8,128)(2,1)S(1)}, bf16[2,512,512]{2,1,0:T(8,128)(2,1)S(1)}, u32[]{:S(2)}, u32[]{:S(2)}) collective-permute-start(bf16[2,512,512]{2,1,0:T(8,128)(2,1)S(1)} %get-tuple-element.21), channel_id=1, source_target_pairs={{0,8},{8,0},{16,24},{24,16},{1,9},{9,1},{17,25},{25,17},{2,10},{10... | collective-permute-start | bytes 3145736 | tf_op jit(solution)/shard_map/ppermute | solution.py:157
  3.4 6.7 %collective-permute-start = (bf16[256,256]{1,0:T(8,128)(2,1)S(1)}, bf16[256,256]{1,0:T(8,128)(2,1)S(1)}, u32[]{:S(2)}, u32[]{:S(2)}) collective-permute-start(bf16[256,256]{1,0:T(8,128)(2,1)S(1)} %bitcast.13), channel_id=1, source_target_pairs={{0,8},{8,16},{16,24},{24,0},{1,9},{9,17},{17,25},{25,1},{2,10},{10... | collective-permute-start | bytes 393224 | tf_op jit(solution)/shard_map/ppermute | solution.py:150
  3.6 6.5 %collective-permute-start.1 = (bf16[256,256]{1,0:T(8,128)(2,1)S(1)}, bf16[256,256]{1,0:T(8,128)(2,1)S(1)}, u32[]{:S(2)}, u32[]{:S(2)}) collective-permute-start(bf16[256,256]{1,0:T(8,128)(2,1)S(1)} %bitcast.15), channel_id=1, source_target_pairs={{0,8},{8,16},{16,24},{24,0},{1,9},{9,17},{17,25},{25,1},{2,10},{10... | collective-permute-start | bytes 393224 | tf_op jit(solution)/shard_map/ppermute | solution.py:151
  6.2 3.9 %collective-permute-start.2 = (s32[1,256]{1,0:T(1,128)S(1)}, s32[1,256]{1,0:T(1,128)S(1)}, u32[]{:S(2)}, u32[]{:S(2)}) collective-permute-start(s32[1,256]{1,0:T(1,128)S(1)} %copy-done.5), channel_id=1, source_target_pairs={{0,8},{8,16},{16,24},{24,0},{1,9},{9,17},{17,25},{25,1},{2,10},{10... | collective-permute-start | bytes 3080 | tf_op jit(solution)/shard_map/ppermute | solution.py:149
  11.2 5.0 %collective-permute-start.6 = (bf16[256,256]{1,0:T(8,128)(2,1)S(1)}, bf16[256,256]{1,0:T(8,128)(2,1)S(1)}, u32[]{:S(2)}, u32[]{:S(2)}) collective-permute-start(bf16[256,256]{1,0:T(8,128)(2,1)S(1)} %get-tuple-element.13.refs_2_), channel_id=1, source_target_pairs={{0,1},{1,0},{2,3},{3,2},{4,5},{5,4},{6,7},{7,6},{8,9},{9,8},{10,11... | collective-permute-start | bytes 393224 | tf_op jit(solution)/shard_map/ppermute | solution.py:170
  13.1 5.6 %collective-permute-start.5 = (bf16[256,256]{1,0:T(8,128)(2,1)S(1)}, bf16[256,256]{1,0:T(8,128)(2,1)S(1)}, u32[]{:S(2)}, u32[]{:S(2)}) collective-permute-start(bf16[256,256]{1,0:T(8,128)(2,1)S(1)} %get-tuple-element.13.refs_2_), channel_id=1, source_target_pairs={{0,8},{8,0},{16,24},{24,16},{1,9},{9,1},{17,25},{25,17},{2,10},{10... | collective-permute-start | bytes 393224 | tf_op jit(solution)/shard_map/ppermute | solution.py:171
  16.3 2.4 %collective-permute-start.7 = (bf16[256,256]{1,0:T(8,128)(2,1)S(1)}, bf16[256,256]{1,0:T(8,128)(2,1)S(1)}, u32[]{:S(2)}, u32[]{:S(2)}) collective-permute-start(bf16[256,256]{1,0:T(8,128)(2,1)S(1)} %collective-permute-done.6.refs_4_), channel_id=1, source_target_pairs={{0,8},{8,0},{16,24},{24,16},{1,9},{9,1},{17,25},{25,17},{2,10},{10... | collective-permute-start | bytes 393224 | tf_op jit(solution)/shard_map/ppermute | solution.py:171
  16.7 8.2 %collective-permute-start.3 = (bf16[2,256,256]{2,1,0:T(8,128)(2,1)S(1)}, bf16[2,256,256]{2,1,0:T(8,128)(2,1)S(1)}, u32[]{:S(2)}, u32[]{:S(2)}) collective-permute-start(bf16[2,256,256]{2,1,0:T(8,128)(2,1)S(1)} %get-tuple-element.17), channel_id=1, source_target_pairs={{0,24},{8,0},{16,8},{24,16},{1,25},{9,1},{17,9},{25,17},{2,26},{10... | collective-permute-start | bytes 786440 | tf_op jit(solution)/shard_map/ppermute | solution.py:178
  19.1 9.7 %collective-permute-start.8 = (bf16[512,256]{1,0:T(8,128)(2,1)S(1)}, bf16[512,256]{1,0:T(8,128)(2,1)S(1)}, u32[]{:S(2)}, u32[]{:S(2)}) collective-permute-start(bf16[512,256]{1,0:T(8,128)(2,1)S(1)} %shard_map.98), channel_id=1, source_target_pairs={{0,16},{8,24},{16,0},{24,8},{1,17},{9,25},{17,1},{25,9},{2,18},{10... | collective-permute-start | bytes 786440 | tf_op jit(solution)/shard_map/ppermute | solution.py:191

commit v3 on v2

v3 whole, which is shorter than its diff:
```python
import functools

import jax
import jax.numpy as jnp
from jax import lax
from jax.experimental import pallas as pl
from jax.experimental.pallas import tpu as pltpu
from jax.sharding import PartitionSpec as P


CHUNKS = 2
HD = 128
F32 = jnp.float32
BF16 = jnp.bfloat16


def dot(left, right, left_dim, right_dim):
    return lax.dot_general(
        left, right, (((left_dim,), (right_dim,)), ((), ())), preferred_element_type=F32
    )


def vmem(dims, dtype):
    return pltpu.VMEM(dims, dtype)


def call(body, outs, *args, cost=1):
    whole = pl.BlockSpec(memory_space=pltpu.VMEM)
    args = [pltpu.with_memory_space_constraint(a, pltpu.VMEM) for a in args]
    return pl.pallas_call(
        body,
        out_shape=outs,
        in_specs=[whole] * len(args),
        out_specs=jax.tree.map(lambda _: whole, outs, is_leaf=lambda o: not isinstance(o, tuple)),
        cost_estimate=pl.CostEstimate(flops=cost << 20, bytes_accessed=1 << 20, transcendentals=0),
        compiler_params=pltpu.CompilerParams(vmem_limit_bytes=24 << 20),
    )(*args)


def shape(dims, dtype):
    return jax.ShapeDtypeStruct(dims, dtype)


def spread(row, length):
    part = jnp.transpose(jnp.broadcast_to(row.astype(F32), (HD, length)))
    return jnp.concatenate([part] * (length // HD), axis=1)


def lower(length):
    rows = lax.broadcasted_iota(jnp.int32, (length, length), 0)
    return rows <= lax.broadcasted_iota(jnp.int32, (length, length), 1)


def masks(length, seg, pseg):
    own = lower(length)
    column = jnp.where(own, spread(seg[...], length), spread(pseg[...], length))
    return own, column == seg[...].astype(F32)


def head_prob(own, valid, qh, kh, pkh):
    scores = jnp.where(own, dot(kh, qh, 1, 1), dot(pkh, qh, 1, 1)) * HD ** (-0.5)
    scores = jnp.where(valid, scores, -jnp.inf)
    top = jnp.max(scores, axis=0, keepdims=True)
    weight = jnp.exp(scores - top)
    return weight * (1.0 / jnp.sum(weight, axis=0, keepdims=True))


def prob_body(length, heads, q, k, v, g, pk, seg, pseg, prob, own_grad):
    own, valid = masks(length, seg, pseg)
    for h in range(heads):
        at = slice(h * HD, (h + 1) * HD)
        prob[h] = head_prob(own, valid, q[:, at], k[:, at], pk[:, at])
        own_grad[h] = dot(v[:, at], g[:, at], 1, 1)


def query_body(length, heads, k, g, pk, pv, prob, own_grad, dq, ds):
    own = lower(length)
    own_query = jnp.logical_not(own) | (
        lax.broadcasted_iota(jnp.int32, (length, length), 0)
        == lax.broadcasted_iota(jnp.int32, (length, length), 1)
    )
    for h in range(heads):
        at = slice(h * HD, (h + 1) * HD)
        grad_prob = jnp.where(own, own_grad[h], dot(pv[:, at], g[:, at], 1, 1))
        grad_score = prob[h] * (
            grad_prob - jnp.sum(prob[h] * grad_prob, axis=0, keepdims=True)
        )
        ds[h] = grad_score
        turned = jnp.transpose(grad_score)
        own_part = jnp.where(own_query, turned, 0.0).astype(BF16)
        prior_part = jnp.where(own_query, 0.0, turned).astype(BF16)
        total = dot(own_part, k[:, at], 1, 0) + dot(prior_part, pk[:, at], 1, 0)
        dq[:, at] = (total * HD ** (-0.5)).astype(BF16)


def terms_body(length, heads, q, g, prob, ds, own_out, back_out):
    own = lower(length)
    for h in range(heads):
        at = slice(h * HD, (h + 1) * HD)
        for index, (left, right) in enumerate(((ds[h], q), (prob[h], g))):
            own_out[index, :, at] = dot(
                jnp.where(own, left, 0.0).astype(BF16), right[:, at], 1, 0
            )
            back_out[index, :, at] = dot(
                jnp.where(own, 0.0, left).astype(BF16), right[:, at], 1, 0
            ).astype(BF16)


def join_body(own, later, dk, dv):
    dk[...] = ((own[0] + later[0].astype(F32)) * HD ** (-0.5)).astype(BF16)
    dv[...] = (own[1] + later[1].astype(F32)).astype(BF16)


def turn_body(recs, length, block, parts, frames, mine, theirs):
    for side in range(2):

        @pl.when(lax.rem(lax.axis_index("ctx"), 2) == side)
        def _():
            for part in range(parts):
                for r in range(recs):
                    for out, which in ((mine, side), (theirs, 1 - side)):
                        start = (2 * part + which) * block
                        tile = frames[r, :, start : start + block]
                        out[part, :, r * length : (r + 1) * length] = jnp.transpose(tile)


def panel_body(count, length, first, step, *refs):
    frames, grads, out = refs[:2], refs[2:-1], refs[-1]
    part = lax.rem(lax.div(lax.axis_index("ctx"), 2) + step, lax.axis_size("ctx") // 2)
    wide = lax.axis_index("wide")
    total = None
    for k in range(count):
        rec = lax.rem(wide - k + count, count)
        at = pl.ds(pl.multiple_of(rec * length, HD), length)
        for core in range(2):
            rows = frames[core][part, first : first + out.shape[0], at]
            term = dot(rows, grads[2 * k + core][...], 1, 0)
            total = term if total is None else total + term
    out[...] = total.astype(out.dtype)


def add_body(first, *refs):
    refs, out = (refs[:-1] if first == 0 else refs[:-2]), refs[-1]
    total = refs[0][first : first + out.shape[0]]
    for ref in refs[1:]:
        total = total + ref[...].astype(F32)
    out[...] = total


def add(first, kept, arrived, held):
    whole = pl.BlockSpec(memory_space=pltpu.VMEM)
    rows, columns = arrived[0].shape
    args = [pltpu.with_memory_space_constraint(a, pltpu.VMEM) for a in (kept, *arrived)]
    return pl.pallas_call(
        functools.partial(add_body, first),
        grid=(1,),
        out_shape=shape(kept.shape, F32),
        in_specs=[whole] * len(args) + [pl.BlockSpec(memory_space=pl.ANY)] * len(held),
        out_specs=pl.BlockSpec((rows, columns), lambda i: (first // rows, 0)),
        input_output_aliases={len(args): 0} if held else {},
        cost_estimate=pl.CostEstimate(flops=1 << 20, bytes_accessed=1 << 20, transcendentals=0),
        compiler_params=pltpu.CompilerParams(vmem_limit_bytes=24 << 20),
    )(*args, *held)


def shards(query_rows, key_rows, value_rows, grad_out, segment, frames):
    length, columns = query_rows.shape[1:]
    heads = columns // HD
    ctx_count = lax.axis_size("ctx")
    wide_count = lax.axis_size("wide")
    recs, _, width = frames.shape
    block = width // ctx_count
    parts = ctx_count // 2
    assert ctx_count >= 4 and recs == wide_count
    onward = [(i, (i + 1) % ctx_count) for i in range(ctx_count)]
    back = [(i, (i - 1) % ctx_count) for i in range(ctx_count)]
    other = [(i, i ^ 1) for i in range(ctx_count)]
    q, k, v, g = (a[0] for a in (query_rows, key_rows, value_rows, grad_out))

    def sent(value, pairs):
        return lax.ppermute(value, "ctx", pairs)

    pseg = sent(segment, onward)
    pk = sent(k, onward)
    pv = sent(v, onward)

    turned = vmem((parts, block, recs * length), BF16)
    mine, theirs = call(
        functools.partial(turn_body, recs, length, block, parts), (turned, turned), frames
    )
    given = lax.ppermute(theirs, "ctx", other)

    square = vmem((heads, length, length), F32)
    prob, own_grad = call(
        functools.partial(prob_body, length, heads), (square, square),
        q, k, v, g, pk, segment, pseg,
    )
    dq, ds = call(
        functools.partial(query_body, length, heads), (vmem((length, columns), BF16), square),
        k, g, pk, pv, prob, own_grad,
    )
    grads = []
    for step in range(wide_count):
        ring = [(i, (i + step) % wide_count) for i in range(wide_count)]
        piece = dq
        if step:
            piece = lax.ppermute(dq, "wide", ring)
        grads += [piece, sent(piece, other)]

    own, to_prior = call(
        functools.partial(terms_body, length, heads),
        (vmem((2, length, columns), F32), vmem((2, length, columns), BF16)),
        q, g, prob, ds,
    )
    later = sent(to_prior, back)

    def panel(first, rows, step, dtype):
        return call(
            functools.partial(panel_body, wide_count, length, first, step),
            vmem((rows, columns), dtype),
            mine, given, *grads,
        )

    chunks = CHUNKS
    rows = block // chunks
    arrived = [[] for _ in range(chunks)]
    for step in range(1, parts):
        ring = [(i, (i + 2 * step) % ctx_count) for i in range(ctx_count)]
        for c in range(chunks):
            piece = panel(c * rows, rows, step, BF16)
            arrived[c].append(sent(piece, ring))
    dk, dv = call(join_body, (shape((length, columns), BF16),) * 2, own, later)
    kept = panel(0, block, 0, F32)
    held = []
    for c in range(chunks):
        held = [add(c * rows, kept, arrived[c], held)]
    return (dq[None], dk[None], dv[None], held[0][None])


def solution(mesh):
    rows = P("wide", "ctx", "head")
    return jax.shard_map(
        shards,
        mesh=mesh,
        in_specs=(rows, rows, rows, rows, P("wide", "ctx"), P(None, "ctx", "wide")),
        out_specs=(rows, rows, rows, rows),
        check_vma=False,
    )
```

time: 29.8 us -> 27.4 us (0.919)
  waiting for transfers between devices: 13.8 us -> 9.49 us
  starting transfers between devices: 8.36 us -> 9.39 us
  Pallas kernels: 4.53 us -> 5.38 us
    ppermute x7 -> x8, waiting for transfers between devices: 10.7 us -> 8.43 us  [sent(): return lax.ppermute(value, 'ctx', pairs)]
    ppermute x1, waiting for transfers between devices: 3.17 us -> 1.06 us  [shards(): piece = lax.ppermute(dq, 'wide', ring)]
    pallas_call x0 -> x2, Pallas kernels: none -> 1.45 us  [add(): pl.pallas_call(functools.partial(add_body, first), grid=(1,), out_shape=s...]
    ppermute x7 -> x8, starting transfers between devices: 5.94 us -> 6.97 us  [sent(): return lax.ppermute(value, 'ctx', pairs)]
    pallas_call x7 -> x8, Pallas kernels: 4.53 us -> 3.93 us  [call(): pl.pallas_call(body, out_shape=outs, in_specs=[whole] * len(args), out_sp...]
  transfers between devices with their start and end apart: 9 -> 10, of which waited for: 4 -> 5; matrix products, arithmetic and copies ran while one was open for 2% -> 2% of each run, Pallas kernels for 10% -> 15%
where the time goes in v3:
time: 27.4 us; the launch traced here: 27.2 us
  waiting for transfers between devices  9.49 us (35%)
  starting transfers between devices  9.39 us (34%)
  Pallas kernels  5.38 us (20%)
  local copies, waits for them, and re-layouts  2.26 us (8%)
  between operations  0.72 us (3%)
    ppermute x8, waiting for transfers between devices, sent(): return lax.ppermute(value, 'ctx', pairs)  8.43 us
    ppermute x8, starting transfers between devices, sent(): return lax.ppermute(value, 'ctx', pairs)  6.97 us
    pallas_call x8, Pallas kernels, call(): pl.pallas_call(body, out_shape=outs, in_specs=[whole] * len(args), out_sp...  3.93 us
    unnamed x13, local copies, waits for them, and re-layouts  2.26 us
    ppermute x1, starting transfers between devices, shards(): piece = lax.ppermute(dq, 'wide', ring)  1.86 us
    pallas_call x2, Pallas kernels, add(): pl.pallas_call(functools.partial(add_body, first), grid=(1,), out_shape=s...  1.45 us
    ppermute x1, waiting for transfers between devices, shards(): piece = lax.ppermute(dq, 'wide', ring)  1.06 us
    ppermute x1, starting transfers between devices, shards(): given = lax.ppermute(theirs, 'ctx', other)  0.56 us
  transfers between devices with their start and end apart: 10, of which 5 were waited for; matrix products, arithmetic and copies ran while one was open for 2% of the time, Pallas kernels for 15%

profile of v3, /device:TPU:0, one launch (start us, length us, event | category | flops | bytes accessed | tf_op | source)
XLA Modules:
  0.0 27.2 jit_solution(15587165978865532225)
XLA Ops:
  0.6 1.6 %copy-done = bf16[2,256,2048]{2,1,0:T(8,128)(2,1)S(1)} copy-done((bf16[2,256,2048]{2,1,0:T(8,128)(2,1)S(1)}, bf16[2,256,2048]{2,1,0:T(8,128)(2,1)}, u32[]{:S(2)}) %copy-start) | copy-done | bytes 2097176
  2.2 0.6 %shard_map.97 = (bf16[2,512,512]{2,1,0:T(8,128)(2,1)S(1)}, bf16[2,512,512]{2,1,0:T(8,128)(2,1)S(1)}) custom-call(bf16[2,256,2048]{2,1,0:T(8,128)(2,1)S(1)} %copy-done), custom_call_target="tpu_custom_call" | custom-call | flops 1048576 | bytes 1048576 | tf_op jit(solution)/shard_map/pallas_call | solution.py:30
  2.9 0.6 %collective-permute-start.4 = (bf16[2,512,512]{2,1,0:T(8,128)(2,1)S(1)}, bf16[2,512,512]{2,1,0:T(8,128)(2,1)S(1)}, u32[]{:S(2)}, u32[]{:S(2)}) collective-permute-start(bf16[2,512,512]{2,1,0:T(8,128)(2,1)S(1)} %get-tuple-element.23), channel_id=1, source_target_pairs={{0,8},{8,0},{16,24},{24,16},{1,9},{9,1},{17,25},{25,17},{2,10},{10... | collective-permute-start | bytes 3145736 | tf_op jit(solution)/shard_map/ppermute | solution.py:191
  3.6 2.6 %collective-permute-start.1 = (bf16[256,256]{1,0:T(8,128)(2,1)S(1)}, bf16[256,256]{1,0:T(8,128)(2,1)S(1)}, u32[]{:S(2)}, u32[]{:S(2)}) collective-permute-start(bf16[256,256]{1,0:T(8,128)(2,1)S(1)} %bitcast.17), channel_id=1, source_target_pairs={{0,8},{8,16},{16,24},{24,0},{1,9},{9,17},{17,25},{25,1},{2,10},{10... | collective-permute-start | bytes 393224 | tf_op jit(solution)/shard_map/ppermute | solution.py:181
  6.2 0.3 %collective-permute-start.2 = (s32[1,256]{1,0:T(1,128)S(1)}, s32[1,256]{1,0:T(1,128)S(1)}, u32[]{:S(2)}, u32[]{:S(2)}) collective-permute-start(s32[1,256]{1,0:T(1,128)S(1)} %copy-done.5), channel_id=1, source_target_pairs={{0,8},{8,16},{16,24},{24,0},{1,9},{9,17},{17,25},{25,1},{2,10},{10... | collective-permute-start | bytes 3080 | tf_op jit(solution)/shard_map/ppermute | solution.py:181
  6.6 3.6 %collective-permute-done.2.pseg = s32[1,256]{1,0:T(1,128)S(1)} collective-permute-done((s32[1,256]{1,0:T(1,128)S(1)}, s32[1,256]{1,0:T(1,128)S(1)}, u32[]{:S(2)}, u32[]{:S(2)}) %collective-permute-start.2) | collective-permute-done | bytes 1056 | tf_op jit(solution)/shard_map/ppermute | solution.py:181
  10.2 0.5 %shard_map.93 = (f32[2,256,256]{2,1,0:T(8,128)S(1)}, f32[2,256,256]{2,1,0:T(8,128)S(1)}) custom-call(bf16[256,256]{1,0:T(8,128)(2,1)S(1)} %bitcast.15, bf16[256,256]{1,0:T(8,128)(2,1)S(1)} %bitcast.13, bf16[256,256]{1,0:T(8,128)(2,1)S(1)} %bitcast.18, bf16[256,256]{1,0:T(8,128)(2,1)S(1)} %bitcast.9, bf16[256,256]{1,0:T(8,128)(2,1)S(1)} %collective-permute-done.pk, ...), custom_call_target="tpu_custom_call" | custom-call | flops 1048576 | bytes 1048576 | tf_op jit(solution)/shard_map/pallas_call | solution.py:30
  10.6 0.7 %shard_map.94 = (bf16[256,256]{1,0:T(8,128)(2,1)S(1)}, f32[2,256,256]{2,1,0:T(8,128)S(1)}) custom-call(bf16[256,256]{1,0:T(8,128)(2,1)S(1)} %bitcast.14, bf16[256,256]{1,0:T(8,128)(2,1)S(1)} %bitcast.10, bf16[256,256]{1,0:T(8,128)(2,1)S(1)} %collective-permute-done.pk, bf16[256,256]{1,0:T(8,128)(2,1)S(1)} %collective-permute-done.1.pv, ...), custom_call_target="tpu_custom_call" | custom-call | flops 1048576 | bytes 1048576 | tf_op jit(solution)/shard_map/pallas_call | solution.py:30
  11.3 1.9 %collective-permute-start.6 = (bf16[256,256]{1,0:T(8,128)(2,1)S(1)}, bf16[256,256]{1,0:T(8,128)(2,1)S(1)}, u32[]{:S(2)}, u32[]{:S(2)}) collective-permute-start(bf16[256,256]{1,0:T(8,128)(2,1)S(1)} %get-tuple-element.16.refs_2_), channel_id=1, source_target_pairs={{0,1},{1,0},{2,3},{3,2},{4,5},{5,4},{6,7},{7,6},{8,9},{9,8},{10,11... | collective-permute-start | bytes 393224 | tf_op jit(solution)/shard_map/ppermute | solution.py:207
  13.2 0.4 %shard_map.95 = (f32[2,256,256]{2,1,0:T(8,128)S(1)}, bf16[2,256,256]{2,1,0:T(8,128)(2,1)S(1)}) custom-call(bf16[256,256]{1,0:T(8,128)(2,1)S(1)} %bitcast.16, bf16[256,256]{1,0:T(8,128)(2,1)S(1)} %bitcast.11, f32[2,256,256]{2,1,0:T(8,128)S(1)} %get-tuple-element.14.prob, f32[2,256,256]{2,1,0:T(8,128)S(1)} %get-tuple-element.17.ds), custom_call_target="tpu_custom_call" | custom-call | flops 1048576 | bytes 1048576 | tf_op jit(solution)/shard_map/pallas_call | solution.py:30
  13.6 1.7 %collective-permute-start.3 = (bf16[2,256,256]{2,1,0:T(8,128)(2,1)S(1)}, bf16[2,256,256]{2,1,0:T(8,128)(2,1)S(1)}, u32[]{:S(2)}, u32[]{:S(2)}) collective-permute-start(bf16[2,256,256]{2,1,0:T(8,128)(2,1)S(1)} %get-tuple-element.19), channel_id=1, source_target_pairs={{0,24},{8,0},{16,8},{24,16},{1,25},{9,1},{17,9},{25,17},{2,26},{10... | collective-permute-start | bytes 786440 | tf_op jit(solution)/shard_map/ppermute | solution.py:181
  15.3 1.1 %collective-permute-done.6.refs_4_ = bf16[256,256]{1,0:T(8,128)(2,1)S(1)} collective-permute-done((bf16[256,256]{1,0:T(8,128)(2,1)S(1)}, bf16[256,256]{1,0:T(8,128)(2,1)S(1)}, u32[]{:S(2)}, u32[]{:S(2)}) %collective-permute-start.6) | collective-permute-done | bytes 131104 | tf_op jit(solution)/shard_map/ppermute | solution.py:207
  16.4 1.3 %collective-permute-done.7.refs_5_ = bf16[256,256]{1,0:T(8,128)(2,1)S(1)} collective-permute-done((bf16[256,256]{1,0:T(8,128)(2,1)S(1)}, bf16[256,256]{1,0:T(8,128)(2,1)S(1)}, u32[]{:S(2)}, u32[]{:S(2)}) %collective-permute-start.7) | collective-permute-done | bytes 131104 | tf_op jit(solution)/shard_map/ppermute | solution.py:181
  17.7 0.3 %shard_map.100 = bf16[256,256]{1,0:T(8,128)(2,1)S(1)} custom-call(bf16[2,512,512]{2,1,0:T(8,128)(2,1)S(1)} %get-tuple-element.22.refs_0_, bf16[2,512,512]{2,1,0:T(8,128)(2,1)S(1)} %collective-permute-done.4.refs_1_, bf16[256,256]{1,0:T(8,128)(2,1)S(1)} %get-tuple-element.16.refs_2_, bf16[256,256]{1,0:T(8,128)(2,1)S(1)} %collective-permute-done.5.refs_3_, ...), custom_call_target="tpu_custom_call" | custom-call | flops 1048576 | bytes 1048576 | tf_op jit(solution)/shard_map/pallas_call | solution.py:30
  18.0 1.9 %collective-permute-start.9 = (bf16[256,256]{1,0:T(8,128)(2,1)S(1)}, bf16[256,256]{1,0:T(8,128)(2,1)S(1)}, u32[]{:S(2)}, u32[]{:S(2)}) collective-permute-start(bf16[256,256]{1,0:T(8,128)(2,1)S(1)} %shard_map.100), channel_id=1, source_target_pairs={{0,16},{8,24},{16,0},{24,8},{1,17},{9,25},{17,1},{25,9},{2,18},{10... | collective-permute-start | bytes 393224 | tf_op jit(solution)/shard_map/ppermute | solution.py:181
  19.9 0.3 %shard_map.99 = bf16[256,256]{1,0:T(8,128)(2,1)S(1)} custom-call(bf16[2,512,512]{2,1,0:T(8,128)(2,1)S(1)} %get-tuple-element.22.refs_0_, bf16[2,512,512]{2,1,0:T(8,128)(2,1)S(1)} %collective-permute-done.4.refs_1_, bf16[256,256]{1,0:T(8,128)(2,1)S(1)} %get-tuple-element.16.refs_2_, bf16[256,256]{1,0:T(8,128)(2,1)S(1)} %collective-permute-done.5.refs_3_, ...), custom_call_target="tpu_custom_call" | custom-call | flops 1048576 | bytes 1048576 | tf_op jit(solution)/shard_map/pallas_call | solution.py:30
  20.2 0.3 collective-permute-start.8
  20.5 0.7 %copy.12 = bf16[1,256,256]{2,1,0:T(8,128)(2,1)} copy(bf16[1,256,256]{2,1,0:T(8,128)(2,1)S(1)} %bitcast.8) | data formatting | bytes 262144
  21.1 0.7 %shard_map.96 = (bf16[256,256]{1,0:T(8,128)(2,1)}, bf16[256,256]{1,0:T(8,128)(2,1)}) custom-call(f32[2,256,256]{2,1,0:T(8,128)S(1)} %get-tuple-element.18.own, bf16[2,256,256]{2,1,0:T(8,128)(2,1)S(1)} %collective-permute-done.3.later), custom_call_target="tpu_custom_call" | custom-call | flops 1048576 | bytes 1048576 | tf_op jit(solution)/shard_map/pallas_call | solution.py:30
  21.9 0.4 %shard_map.98.refs_0_ = f32[512,256]{1,0:T(8,128)S(1)} custom-call(bf16[2,512,512]{2,1,0:T(8,128)(2,1)S(1)} %get-tuple-element.22.refs_0_, bf16[2,512,512]{2,1,0:T(8,128)(2,1)S(1)} %collective-permute-done.4.refs_1_, bf16[256,256]{1,0:T(8,128)(2,1)S(1)} %get-tuple-element.16.refs_2_, bf16[256,256]{1,0:T(8,128)(2,1)S(1)} %collective-permute-done.5.refs_3_, ...), custom_call_target="tpu_custom_call" | custom-call | flops 1048576 | bytes 1048576 | tf_op jit(solution)/shard_map/pallas_call | solution.py:30
  22.3 2.1 %collective-permute-done.9.refs_1_ = bf16[256,256]{1,0:T(8,128)(2,1)S(1)} collective-permute-done((bf16[256,256]{1,0:T(8,128)(2,1)S(1)}, bf16[256,256]{1,0:T(8,128)(2,1)S(1)}, u32[]{:S(2)}, u32[]{:S(2)}) %collective-permute-start.9) | collective-permute-done | bytes 131104 | tf_op jit(solution)/shard_map/ppermute | solution.py:181
  24.4 0.7 %shard_map.101.refs_2_ = f32[512,256]{1,0:T(8,128)} custom-call(f32[512,256]{1,0:T(8,128)S(1)} %shard_map.98.refs_0_, bf16[256,256]{1,0:T(8,128)(2,1)S(1)} %collective-permute-done.9.refs_1_), custom_call_target="tpu_custom_call" | custom-call | flops 1048576 | bytes 1048576 | tf_op jit(solution)/shard_map/pallas_call | solution.py:154
  25.2 1.4 %collective-permute-done.8.refs_1_ = bf16[256,256]{1,0:T(8,128)(2,1)S(1)} collective-permute-done((bf16[256,256]{1,0:T(8,128)(2,1)S(1)}, bf16[256,256]{1,0:T(8,128)(2,1)S(1)}, u32[]{:S(2)}, u32[]{:S(2)}) %collective-permute-start.8) | collective-permute-done | bytes 131104 | tf_op jit(solution)/shard_map/ppermute | solution.py:181
  26.5 0.7 %shard_map.102 = f32[512,256]{1,0:T(8,128)} custom-call(f32[512,256]{1,0:T(8,128)S(1)} %shard_map.98.refs_0_, bf16[256,256]{1,0:T(8,128)(2,1)S(1)} %collective-permute-done.8.refs_1_, f32[512,256]{1,0:T(8,128)} %shard_map.101.refs_2_), custom_call_target="tpu_custom_call", output_to_operand_aliasing={{}: (2, {})} | custom-call | flops 1048576 | bytes 1048576 | tf_op jit(solution)/shard_map/pallas_call | solution.py:154
  (19 shorter events, 0.2 us)
Async XLA Ops:
  0.6 1.6 %copy-start = (bf16[2,256,2048]{2,1,0:T(8,128)(2,1)S(1)}, bf16[2,256,2048]{2,1,0:T(8,128)(2,1)}, u32[]{:S(2)}) copy-start(bf16[2,256,2048]{2,1,0:T(8,128)(2,1)} %frames.1) | copy-start | bytes 6291460
  2.2 1.2 %copy-start.2 = (bf16[1,256,256]{2,1,0:T(8,128)(2,1)S(1)}, bf16[1,256,256]{2,1,0:T(8,128)(2,1)}, u32[]{:S(2)}) copy-start(bf16[1,256,256]{2,1,0:T(8,128)(2,1)} %param.7) | copy-start | bytes 393220
  2.2 1.4 %copy-start.4 = (bf16[1,256,256]{2,1,0:T(8,128)(2,1)S(1)}, bf16[1,256,256]{2,1,0:T(8,128)(2,1)}, u32[]{:S(2)}) copy-start(bf16[1,256,256]{2,1,0:T(8,128)(2,1)} %param.8) | copy-start | bytes 393220
  2.2 4.0 %copy-start.5 = (s32[1,256]{1,0:T(1,128)S(1)}, s32[1,256]{1,0:T(1,128)}, u32[]{:S(2)}) copy-start(s32[1,256]{1,0:T(1,128)} %seg.1) | copy-start | bytes 3076
  2.2 7.9 %copy-start.1 = (bf16[1,256,256]{2,1,0:T(8,128)(2,1)S(1)}, bf16[1,256,256]{2,1,0:T(8,128)(2,1)}, u32[]{:S(2)}) copy-start(bf16[1,256,256]{2,1,0:T(8,128)(2,1)} %param.9) | copy-start | bytes 393220
  2.2 7.9 %copy-start.3 = (bf16[1,256,256]{2,1,0:T(8,128)(2,1)S(1)}, bf16[1,256,256]{2,1,0:T(8,128)(2,1)}, u32[]{:S(2)}) copy-start(bf16[1,256,256]{2,1,0:T(8,128)(2,1)} %param.6) | copy-start | bytes 393220
  2.9 14.8 %collective-permute-start.4 = (bf16[2,512,512]{2,1,0:T(8,128)(2,1)S(1)}, bf16[2,512,512]{2,1,0:T(8,128)(2,1)S(1)}, u32[]{:S(2)}, u32[]{:S(2)}) collective-permute-start(bf16[2,512,512]{2,1,0:T(8,128)(2,1)S(1)} %get-tuple-element.23), channel_id=1, source_target_pairs={{0,8},{8,0},{16,24},{24,16},{1,9},{9,1},{17,25},{25,17},{2,10},{10... | collective-permute-start | bytes 3145736 | tf_op jit(solution)/shard_map/ppermute | solution.py:191
  3.4 6.7 %collective-permute-start = (bf16[256,256]{1,0:T(8,128)(2,1)S(1)}, bf16[256,256]{1,0:T(8,128)(2,1)S(1)}, u32[]{:S(2)}, u32[]{:S(2)}) collective-permute-start(bf16[256,256]{1,0:T(8,128)(2,1)S(1)} %bitcast.12), channel_id=1, source_target_pairs={{0,8},{8,16},{16,24},{24,0},{1,9},{9,17},{17,25},{25,1},{2,10},{10... | collective-permute-start | bytes 393224 | tf_op jit(solution)/shard_map/ppermute | solution.py:181
  3.6 7.0 %collective-permute-start.1 = (bf16[256,256]{1,0:T(8,128)(2,1)S(1)}, bf16[256,256]{1,0:T(8,128)(2,1)S(1)}, u32[]{:S(2)}, u32[]{:S(2)}) collective-permute-start(bf16[256,256]{1,0:T(8,128)(2,1)S(1)} %bitcast.17), channel_id=1, source_target_pairs={{0,8},{8,16},{16,24},{24,0},{1,9},{9,17},{17,25},{25,1},{2,10},{10... | collective-permute-start | bytes 393224 | tf_op jit(solution)/shard_map/ppermute | solution.py:181
  6.2 3.9 %collective-permute-start.2 = (s32[1,256]{1,0:T(1,128)S(1)}, s32[1,256]{1,0:T(1,128)S(1)}, u32[]{:S(2)}, u32[]{:S(2)}) collective-permute-start(s32[1,256]{1,0:T(1,128)S(1)} %copy-done.5), channel_id=1, source_target_pairs={{0,8},{8,16},{16,24},{24,0},{1,9},{9,17},{17,25},{25,1},{2,10},{10... | collective-permute-start | bytes 3080 | tf_op jit(solution)/shard_map/ppermute | solution.py:181
  11.3 5.0 %collective-permute-start.6 = (bf16[256,256]{1,0:T(8,128)(2,1)S(1)}, bf16[256,256]{1,0:T(8,128)(2,1)S(1)}, u32[]{:S(2)}, u32[]{:S(2)}) collective-permute-start(bf16[256,256]{1,0:T(8,128)(2,1)S(1)} %get-tuple-element.16.refs_2_), channel_id=1, source_target_pairs={{0,1},{1,0},{2,3},{3,2},{4,5},{5,4},{6,7},{7,6},{8,9},{9,8},{10,11... | collective-permute-start | bytes 393224 | tf_op jit(solution)/shard_map/ppermute | solution.py:207
  13.2 3.2 %collective-permute-start.5 = (bf16[256,256]{1,0:T(8,128)(2,1)S(1)}, bf16[256,256]{1,0:T(8,128)(2,1)S(1)}, u32[]{:S(2)}, u32[]{:S(2)}) collective-permute-start(bf16[256,256]{1,0:T(8,128)(2,1)S(1)} %get-tuple-element.16.refs_2_), channel_id=1, source_target_pairs={{0,8},{8,0},{16,24},{24,16},{1,9},{9,1},{17,25},{25,17},{2,10},{10... | collective-permute-start | bytes 393224 | tf_op jit(solution)/shard_map/ppermute | solution.py:181
  13.6 7.5 %collective-permute-start.3 = (bf16[2,256,256]{2,1,0:T(8,128)(2,1)S(1)}, bf16[2,256,256]{2,1,0:T(8,128)(2,1)S(1)}, u32[]{:S(2)}, u32[]{:S(2)}) collective-permute-start(bf16[2,256,256]{2,1,0:T(8,128)(2,1)S(1)} %get-tuple-element.19), channel_id=1, source_target_pairs={{0,24},{8,0},{16,8},{24,16},{1,25},{9,1},{17,9},{25,17},{2,26},{10... | collective-permute-start | bytes 786440 | tf_op jit(solution)/shard_map/ppermute | solution.py:181
  16.3 1.3 %collective-permute-start.7 = (bf16[256,256]{1,0:T(8,128)(2,1)S(1)}, bf16[256,256]{1,0:T(8,128)(2,1)S(1)}, u32[]{:S(2)}, u32[]{:S(2)}) collective-permute-start(bf16[256,256]{1,0:T(8,128)(2,1)S(1)} %collective-permute-done.6.refs_4_), channel_id=1, source_target_pairs={{0,8},{8,0},{16,24},{24,16},{1,9},{9,1},{17,25},{25,17},{2,10},{10... | collective-permute-start | bytes 393224 | tf_op jit(solution)/shard_map/ppermute | solution.py:181
  18.0 6.4 %collective-permute-start.9 = (bf16[256,256]{1,0:T(8,128)(2,1)S(1)}, bf16[256,256]{1,0:T(8,128)(2,1)S(1)}, u32[]{:S(2)}, u32[]{:S(2)}) collective-permute-start(bf16[256,256]{1,0:T(8,128)(2,1)S(1)} %shard_map.100), channel_id=1, source_target_pairs={{0,16},{8,24},{16,0},{24,8},{1,17},{9,25},{17,1},{25,9},{2,18},{10... | collective-permute-start | bytes 393224 | tf_op jit(solution)/shard_map/ppermute | solution.py:181
  20.2 6.3 %collective-permute-start.8 = (bf16[256,256]{1,0:T(8,128)(2,1)S(1)}, bf16[256,256]{1,0:T(8,128)(2,1)S(1)}, u32[]{:S(2)}, u32[]{:S(2)}) collective-permute-start(bf16[256,256]{1,0:T(8,128)(2,1)S(1)} %shard_map.99), channel_id=1, source_target_pairs={{0,16},{8,24},{16,0},{24,8},{1,17},{9,25},{17,1},{25,9},{2,18},{10... | collective-permute-start | bytes 393224 | tf_op jit(solution)/shard_map/ppermute | solution.py:181

commit v4 on v3

--- a/solution.py
+++ b/solution.py
@@ -8,7 +8,6 @@
 from jax.sharding import PartitionSpec as P
 
 
-CHUNKS = 2
 HD = 128
 F32 = jnp.float32
 BF16 = jnp.bfloat16
@@ -46,6 +45,10 @@
     return jnp.concatenate([part] * (length // HD), axis=1)
 
 
+def head(h):
+    return slice(h * HD, (h + 1) * HD)
+
+
 def lower(length):
     rows = lax.broadcasted_iota(jnp.int32, (length, length), 0)
     return rows <= lax.broadcasted_iota(jnp.int32, (length, length), 1)
@@ -68,36 +71,42 @@
 def prob_body(length, heads, q, k, v, g, pk, seg, pseg, prob, own_grad):
     own, valid = masks(length, seg, pseg)
     for h in range(heads):
-        at = slice(h * HD, (h + 1) * HD)
+        at = head(h)
         prob[h] = head_prob(own, valid, q[:, at], k[:, at], pk[:, at])
         own_grad[h] = dot(v[:, at], g[:, at], 1, 1)
 
 
-def query_body(length, heads, k, g, pk, pv, prob, own_grad, dq, ds):
+def query_body(length, heads, first, k, g, pk, pv, prob, own_grad, dq, ds):
     own = lower(length)
     own_query = jnp.logical_not(own) | (
         lax.broadcasted_iota(jnp.int32, (length, length), 0)
         == lax.broadcasted_iota(jnp.int32, (length, length), 1)
     )
     for h in range(heads):
-        at = slice(h * HD, (h + 1) * HD)
-        grad_prob = jnp.where(own, own_grad[h], dot(pv[:, at], g[:, at], 1, 1))
-        grad_score = prob[h] * (
-            grad_prob - jnp.sum(prob[h] * grad_prob, axis=0, keepdims=True)
+        at = head(first + h)
+        weight = prob[first + h]
+        grad_prob = jnp.where(own, own_grad[first + h], dot(pv[:, at], g[:, at], 1, 1))
+        grad_score = weight * (
+            grad_prob - jnp.sum(weight * grad_prob, axis=0, keepdims=True)
         )
         ds[h] = grad_score
         turned = jnp.transpose(grad_score)
         own_part = jnp.where(own_query, turned, 0.0).astype(BF16)
         prior_part = jnp.where(own_query, 0.0, turned).astype(BF16)
         total = dot(own_part, k[:, at], 1, 0) + dot(prior_part, pk[:, at], 1, 0)
-        dq[:, at] = (total * HD ** (-0.5)).astype(BF16)
-
-
-def terms_body(length, heads, q, g, prob, ds, own_out, back_out):
+        dq[:, head(h)] = (total * HD ** (-0.5)).astype(BF16)
+
+
+def terms_body(length, heads, size, q, g, prob, *refs):
+    own_out, back_out, dq_out = refs[-3:]
+    pieces = [refs[i : i + 2] for i in range(0, len(refs) - 3, 2)]
     own = lower(length)
+    for c, (dq, _) in enumerate(pieces):
+        dq_out[:, c * size * HD : (c + 1) * size * HD] = dq[...]
     for h in range(heads):
-        at = slice(h * HD, (h + 1) * HD)
-        for index, (left, right) in enumerate(((ds[h], q), (prob[h], g))):
+        at = head(h)
+        ds = pieces[h // size][1]
+        for index, (left, right) in enumerate(((ds[h % size], q), (prob[h], g))):
             own_out[index, :, at] = dot(
                 jnp.where(own, left, 0.0).astype(BF16), right[:, at], 1, 0
             )
@@ -124,24 +133,30 @@
                         out[part, :, r * length : (r + 1) * length] = jnp.transpose(tile)
 
 
-def panel_body(count, length, first, step, *refs):
-    frames, grads, out = refs[:2], refs[2:-1], refs[-1]
+def panel_body(count, length, step, first, frames0, frames1, mine, peer, *refs):
+    grads, out = refs[:-1], refs[-1]
     part = lax.rem(lax.div(lax.axis_index("ctx"), 2) + step, lax.axis_size("ctx") // 2)
     wide = lax.axis_index("wide")
-    total = None
-    for k in range(count):
-        rec = lax.rem(wide - k + count, count)
-        at = pl.ds(pl.multiple_of(rec * length, HD), length)
-        for core in range(2):
-            rows = frames[core][part, first : first + out.shape[0], at]
-            term = dot(rows, grads[2 * k + core][...], 1, 0)
-            total = term if total is None else total + term
-    out[...] = total.astype(out.dtype)
+    width = grads[0].shape[1]
+    for c in range(out.shape[1] // width):
+        at = slice((first + c) * width, (first + c + 1) * width)
+        pairs = [(mine[:, at], peer[:, at])]
+        for k in range(count - 1):
+            i = 2 * (c * (count - 1) + k)
+            pairs.append((grads[i][...], grads[i + 1][...]))
+        total = None
+        for k, pair in enumerate(pairs):
+            rec = lax.rem(wide - k + count, count)
+            rows = pl.ds(pl.multiple_of(rec * length, HD), length)
+            for frames, grad in zip((frames0, frames1), pair):
+                term = dot(frames[part, :, rows], grad, 1, 0)
+                total = term if total is None else total + term
+        out[:, c * width : (c + 1) * width] = total.astype(out.dtype)
 
 
 def add_body(first, *refs):
     refs, out = (refs[:-1] if first == 0 else refs[:-2]), refs[-1]
-    total = refs[0][first : first + out.shape[0]]
+    total = refs[0][:, first : first + out.shape[1]]
     for ref in refs[1:]:
         total = total + ref[...].astype(F32)
     out[...] = total
@@ -156,7 +171,7 @@
         grid=(1,),
         out_shape=shape(kept.shape, F32),
         in_specs=[whole] * len(args) + [pl.BlockSpec(memory_space=pl.ANY)] * len(held),
-        out_specs=pl.BlockSpec((rows, columns), lambda i: (first // rows, 0)),
+        out_specs=pl.BlockSpec((rows, columns), lambda i: (0, first // columns)),
         input_output_aliases={len(args): 0} if held else {},
         cost_estimate=pl.CostEstimate(flops=1 << 20, bytes_accessed=1 << 20, transcendentals=0),
         compiler_params=pltpu.CompilerParams(vmem_limit_bytes=24 << 20),
@@ -190,50 +205,58 @@
     )
     given = lax.ppermute(theirs, "ctx", other)
 
+    chunks = 2 if heads % 2 == 0 else 1
+    size = heads // chunks
     square = vmem((heads, length, length), F32)
     prob, own_grad = call(
         functools.partial(prob_body, length, heads), (square, square),
         q, k, v, g, pk, segment, pseg,
     )
-    dq, ds = call(
-        functools.partial(query_body, length, heads), (vmem((length, columns), BF16), square),
-        k, g, pk, pv, prob, own_grad,
-    )
+    found = []
+    for c in range(chunks):
+        found += call(
+            functools.partial(query_body, length, size, c * size),
+            (vmem((length, size * HD), BF16), vmem((size, length, length), F32)),
+            k, g, pk, pv, prob, own_grad,
+        )
+    own, to_prior, dq = call(
+        functools.partial(terms_body, length, heads, size),
+        (
+            vmem((2, length, columns), F32),
+            vmem((2, length, columns), BF16),
+            vmem((length, columns), BF16),
+        ),
+        q, g, prob, *found,
+    )
+    later = sent(to_prior, back)
+    peer = sent(dq, other)
     grads = []
-    for step in range(wide_count):
-        ring = [(i, (i + step) % wide_count) for i in range(wide_count)]
-        piece = dq
-        if step:
-            piece = lax.ppermute(dq, "wide", ring)
-        grads += [piece, sent(piece, other)]
-
-    own, to_prior = call(
-        functools.partial(terms_body, length, heads),
-        (vmem((2, length, columns), F32), vmem((2, length, columns), BF16)),
-        q, g, prob, ds,
-    )
-    later = sent(to_prior, back)
-
-    def panel(first, rows, step, dtype):
+    for c in range(chunks):
+        pieces = []
+        for step in range(1, wide_count):
+            ring = [(i, (i + step) % wide_count) for i in range(wide_count)]
+            piece = lax.ppermute(found[2 * c], "wide", ring)
+            pieces += [piece, sent(piece, other)]
+        grads.append(pieces)
+
+    def panel(step, first, pieces, width, dtype):
         return call(
-            functools.partial(panel_body, wide_count, length, first, step),
-            vmem((rows, columns), dtype),
-            mine, given, *grads,
+            functools.partial(panel_body, wide_count, length, step, first),
+            vmem((block, width), dtype),
+            mine, given, dq, peer, *pieces,
         )
 
-    chunks = CHUNKS
-    rows = block // chunks
     arrived = [[] for _ in range(chunks)]
     for step in range(1, parts):
         ring = [(i, (i + 2 * step) % ctx_count) for i in range(ctx_count)]
         for c in range(chunks):
-            piece = panel(c * rows, rows, step, BF16)
+            piece = panel(step, c, grads[c], size * HD, BF16)
             arrived[c].append(sent(piece, ring))
     dk, dv = call(join_body, (shape((length, columns), BF16),) * 2, own, later)
-    kept = panel(0, block, 0, F32)
+    kept = panel(0, 0, sum(grads, []), columns, F32)
     held = []
     for c in range(chunks):
-        held = [add(c * rows, kept, arrived[c], held)]
+        held = [add(c * size * HD, kept, arrived[c], held)]
     return (dq[None], dk[None], dv[None], held[0][None])
 
 

time: 27.4 us -> 30.2 us (1.10)
  waiting for transfers between devices: 9.49 us -> 10.9 us
  Pallas kernels: 5.38 us -> 6.39 us
  starting transfers between devices: 9.39 us -> 9.73 us
    ppermute x1 -> x2, waiting for transfers between devices: 1.06 us -> 3.73 us  [shards(): piece = lax.ppermute(found[2 * c], 'wide', ring)]
    ppermute x8 -> x9, waiting for transfers between devices: 8.43 us -> 7.16 us  [sent(): return lax.ppermute(value, 'ctx', pairs)]
    pallas_call x8 -> x9, Pallas kernels: 3.93 us -> 4.94 us  [call(): pl.pallas_call(body, out_shape=outs, in_specs=[whole] * len(args), out_sp...]
    ppermute x1 -> x2, starting transfers between devices: 1.86 us -> 2.4 us  [shards(): piece = lax.ppermute(found[2 * c], 'wide', ring)]
    ppermute x8 -> x9, starting transfers between devices: 6.97 us -> 6.78 us  [sent(): return lax.ppermute(value, 'ctx', pairs)]
  transfers between devices with their start and end apart: 10 -> 12, of which waited for: 5 -> 5; matrix products, arithmetic and copies ran while one was open for 2% -> 2% of each run, Pallas kernels for 15% -> 17%
where the time goes in v4:
time: 30.2 us; the launch traced here: 30 us
  waiting for transfers between devices  10.9 us (36%)
  starting transfers between devices  9.73 us (32%)
  Pallas kernels  6.39 us (21%)
  local copies, waits for them, and re-layouts  2.26 us (7%)
  between operations  0.75 us (2%)
    ppermute x9, waiting for transfers between devices, sent(): return lax.ppermute(value, 'ctx', pairs)  7.16 us
    ppermute x9, starting transfers between devices, sent(): return lax.ppermute(value, 'ctx', pairs)  6.78 us
    pallas_call x9, Pallas kernels, call(): pl.pallas_call(body, out_shape=outs, in_specs=[whole] * len(args), out_sp...  4.94 us
    ppermute x2, waiting for transfers between devices, shards(): piece = lax.ppermute(found[2 * c], 'wide', ring)  3.73 us
    ppermute x2, starting transfers between devices, shards(): piece = lax.ppermute(found[2 * c], 'wide', ring)  2.4 us
    unnamed x13, local copies, waits for them, and re-layouts  2.26 us
    pallas_call x2, Pallas kernels, add(): pl.pallas_call(functools.partial(add_body, first), grid=(1,), out_shape=s...  1.45 us
  transfers between devices with their start and end apart: 12, of which 5 were waited for; matrix products, arithmetic and copies ran while one was open for 2% of the time, Pallas kernels for 17%

profile of v4, /device:TPU:0, one launch (start us, length us, event | category | flops | bytes accessed | tf_op | source)
XLA Modules:
  0.0 30.0 jit_solution(15433809608949668683)
XLA Ops:
  0.6 1.6 %copy-done = bf16[2,256,2048]{2,1,0:T(8,128)(2,1)S(1)} copy-done((bf16[2,256,2048]{2,1,0:T(8,128)(2,1)S(1)}, bf16[2,256,2048]{2,1,0:T(8,128)(2,1)}, u32[]{:S(2)}) %copy-start) | copy-done | bytes 2097176
  2.2 0.6 %shard_map.98 = (bf16[2,512,512]{2,1,0:T(8,128)(2,1)S(1)}, bf16[2,512,512]{2,1,0:T(8,128)(2,1)S(1)}) custom-call(bf16[2,256,2048]{2,1,0:T(8,128)(2,1)S(1)} %copy-done), custom_call_target="tpu_custom_call" | custom-call | flops 1048576 | bytes 1048576 | tf_op jit(solution)/shard_map/pallas_call | solution.py:29
  2.9 0.6 %collective-permute-start.4 = (bf16[2,512,512]{2,1,0:T(8,128)(2,1)S(1)}, bf16[2,512,512]{2,1,0:T(8,128)(2,1)S(1)}, u32[]{:S(2)}, u32[]{:S(2)}) collective-permute-start(bf16[2,512,512]{2,1,0:T(8,128)(2,1)S(1)} %get-tuple-element.29), channel_id=1, source_target_pairs={{0,8},{8,0},{16,24},{24,16},{1,9},{9,1},{17,25},{25,17},{2,10},{10... | collective-permute-start | bytes 3145736 | tf_op jit(solution)/shard_map/ppermute | solution.py:206
  3.6 2.6 %collective-permute-start.2 = (bf16[256,256]{1,0:T(8,128)(2,1)S(1)}, bf16[256,256]{1,0:T(8,128)(2,1)S(1)}, u32[]{:S(2)}, u32[]{:S(2)}) collective-permute-start(bf16[256,256]{1,0:T(8,128)(2,1)S(1)} %bitcast.19), channel_id=1, source_target_pairs={{0,8},{8,16},{16,24},{24,0},{1,9},{9,17},{17,25},{25,1},{2,10},{10... | collective-permute-start | bytes 393224 | tf_op jit(solution)/shard_map/ppermute | solution.py:196
  6.6 3.6 %collective-permute-done.1.pseg = s32[1,256]{1,0:T(1,128)S(1)} collective-permute-done((s32[1,256]{1,0:T(1,128)S(1)}, s32[1,256]{1,0:T(1,128)S(1)}, u32[]{:S(2)}, u32[]{:S(2)}) %collective-permute-start.1) | collective-permute-done | bytes 1056 | tf_op jit(solution)/shard_map/ppermute | solution.py:196
  10.2 0.5 %shard_map.93 = (f32[2,256,256]{2,1,0:T(8,128)S(1)}, f32[2,256,256]{2,1,0:T(8,128)S(1)}) custom-call(bf16[256,256]{1,0:T(8,128)(2,1)S(1)} %bitcast.17, bf16[256,256]{1,0:T(8,128)(2,1)S(1)} %bitcast.14, bf16[256,256]{1,0:T(8,128)(2,1)S(1)} %bitcast.20, bf16[256,256]{1,0:T(8,128)(2,1)S(1)} %bitcast.9, bf16[256,256]{1,0:T(8,128)(2,1)S(1)} %collective-permute-done.pk, ...), custom_call_target="tpu_custom_call" | custom-call | flops 1048576 | bytes 1048576 | tf_op jit(solution)/shard_map/pallas_call | solution.py:29
  10.6 0.6 %shard_map.94 = (bf16[256,128]{1,0:T(8,128)(2,1)S(1)}, f32[1,256,256]{2,1,0:T(8,128)S(1)}) custom-call(bf16[256,256]{1,0:T(8,128)(2,1)S(1)} %bitcast.15, bf16[256,256]{1,0:T(8,128)(2,1)S(1)} %bitcast.10, bf16[256,256]{1,0:T(8,128)(2,1)S(1)} %collective-permute-done.pk, bf16[256,256]{1,0:T(8,128)(2,1)S(1)} %collective-permute-done.2.pv, ...), custom_call_target="tpu_custom_call" | custom-call | flops 1048576 | bytes 1048576 | tf_op jit(solution)/shard_map/pallas_call | solution.py:29
  11.2 1.9 %collective-permute-start.6 = (bf16[256,128]{1,0:T(8,128)(2,1)S(1)}, bf16[256,128]{1,0:T(8,128)(2,1)S(1)}, u32[]{:S(2)}, u32[]{:S(2)}) collective-permute-start(bf16[256,128]{1,0:T(8,128)(2,1)S(1)} %get-tuple-element.19.refs_0_), channel_id=1, source_target_pairs={{0,1},{1,0},{2,3},{3,2},{4,5},{5,4},{6,7},{7,6},{8,9},{9,8},{10,11... | collective-permute-start | bytes 196616 | tf_op jit(solution)/shard_map/ppermute | solution.py:238
  13.1 0.6 %shard_map.95 = (bf16[256,128]{1,0:T(8,128)(2,1)S(1)}, f32[1,256,256]{2,1,0:T(8,128)S(1)}) custom-call(bf16[256,256]{1,0:T(8,128)(2,1)S(1)} %bitcast.16, bf16[256,256]{1,0:T(8,128)(2,1)S(1)} %bitcast.11, bf16[256,256]{1,0:T(8,128)(2,1)S(1)} %collective-permute-done.pk, bf16[256,256]{1,0:T(8,128)(2,1)S(1)} %collective-permute-done.2.pv, ...), custom_call_target="tpu_custom_call" | custom-call | flops 1048576 | bytes 1048576 | tf_op jit(solution)/shard_map/pallas_call | solution.py:29
  13.6 0.4 %shard_map.96 = (f32[2,256,256]{2,1,0:T(8,128)S(1)}, bf16[2,256,256]{2,1,0:T(8,128)(2,1)S(1)}, bf16[256,256]{1,0:T(8,128)(2,1)S(1)}) custom-call(bf16[256,256]{1,0:T(8,128)(2,1)S(1)} %bitcast.18, bf16[256,256]{1,0:T(8,128)(2,1)S(1)} %bitcast.12, f32[2,256,256]{2,1,0:T(8,128)S(1)} %get-tuple-element.17.prob, bf16[256,128]{1,0:T(8,128)(2,1)S(1)} %get-tuple-element.19.refs_0_, ...), custom_call_target="tpu_custom_call" | custom-call | flops 1048576 | bytes 1048576 | tf_op jit(solution)/shard_map/pallas_call | solution.py:29
  14.2 1.6 %collective-permute-start.3 = (bf16[2,256,256]{2,1,0:T(8,128)(2,1)S(1)}, bf16[2,256,256]{2,1,0:T(8,128)(2,1)S(1)}, u32[]{:S(2)}, u32[]{:S(2)}) collective-permute-start(bf16[2,256,256]{2,1,0:T(8,128)(2,1)S(1)} %get-tuple-element.25), channel_id=1, source_target_pairs={{0,24},{8,0},{16,8},{24,16},{1,25},{9,1},{17,9},{25,17},{2,26},{10... | collective-permute-start | bytes 786440 | tf_op jit(solution)/shard_map/ppermute | solution.py:196
  15.8 0.5 %collective-permute-start.8 = (bf16[256,128]{1,0:T(8,128)(2,1)S(1)}, bf16[256,128]{1,0:T(8,128)(2,1)S(1)}, u32[]{:S(2)}, u32[]{:S(2)}) collective-permute-start(bf16[256,128]{1,0:T(8,128)(2,1)S(1)} %get-tuple-element.21.refs_2_), channel_id=1, source_target_pairs={{0,1},{1,0},{2,3},{3,2},{4,5},{5,4},{6,7},{7,6},{8,9},{9,8},{10,11... | collective-permute-start | bytes 196616 | tf_op jit(solution)/shard_map/ppermute | solution.py:238
  16.3 3.7 %collective-permute-done.8.refs_2_.refs_0_ = bf16[256,128]{1,0:T(8,128)(2,1)S(1)} collective-permute-done((bf16[256,128]{1,0:T(8,128)(2,1)S(1)}, bf16[256,128]{1,0:T(8,128)(2,1)S(1)}, u32[]{:S(2)}, u32[]{:S(2)}) %collective-permute-start.8) | collective-permute-done | bytes 65568 | tf_op jit(solution)/shard_map/ppermute | solution.py:238
  20.1 0.4 %shard_map.101 = bf16[512,128]{1,0:T(8,128)(2,1)S(1)} custom-call(bf16[2,512,512]{2,1,0:T(8,128)(2,1)S(1)} %get-tuple-element.28.frames0, bf16[2,512,512]{2,1,0:T(8,128)(2,1)S(1)} %collective-permute-done.4.frames1, bf16[256,256]{1,0:T(8,128)(2,1)S(1)} %get-tuple-element.23.mine, bf16[256,256]{1,0:T(8,128)(2,1)S(1)} %collective-permute-done.5.peer, ...), custom_call_target="tpu_custom_call" | custom-call | flops 1048576 | bytes 1048576 | tf_op jit(solution)/shard_map/pallas_call | solution.py:29
  20.5 0.6 %collective-permute-start.11 = (bf16[512,128]{1,0:T(8,128)(2,1)S(1)}, bf16[512,128]{1,0:T(8,128)(2,1)S(1)}, u32[]{:S(2)}, u32[]{:S(2)}) collective-permute-start(bf16[512,128]{1,0:T(8,128)(2,1)S(1)} %shard_map.101), channel_id=1, source_target_pairs={{0,16},{8,24},{16,0},{24,8},{1,17},{9,25},{17,1},{25,9},{2,18},{10... | collective-permute-start | bytes 393224 | tf_op jit(solution)/shard_map/ppermute | solution.py:196
  21.3 0.4 %shard_map.100 = bf16[512,128]{1,0:T(8,128)(2,1)S(1)} custom-call(bf16[2,512,512]{2,1,0:T(8,128)(2,1)S(1)} %get-tuple-element.28.frames0, bf16[2,512,512]{2,1,0:T(8,128)(2,1)S(1)} %collective-permute-done.4.frames1, bf16[256,256]{1,0:T(8,128)(2,1)S(1)} %get-tuple-element.23.mine, bf16[256,256]{1,0:T(8,128)(2,1)S(1)} %collective-permute-done.5.peer, ...), custom_call_target="tpu_custom_call" | custom-call | flops 1048576 | bytes 1048576 | tf_op jit(solution)/shard_map/pallas_call | solution.py:29
  21.7 1.4 %collective-permute-start.10 = (bf16[512,128]{1,0:T(8,128)(2,1)S(1)}, bf16[512,128]{1,0:T(8,128)(2,1)S(1)}, u32[]{:S(2)}, u32[]{:S(2)}) collective-permute-start(bf16[512,128]{1,0:T(8,128)(2,1)S(1)} %shard_map.100), channel_id=1, source_target_pairs={{0,16},{8,24},{16,0},{24,8},{1,17},{9,25},{17,1},{25,9},{2,18},{10... | collective-permute-start | bytes 393224 | tf_op jit(solution)/shard_map/ppermute | solution.py:196
  23.1 0.7 %copy.12 = bf16[1,256,256]{2,1,0:T(8,128)(2,1)} copy(bf16[1,256,256]{2,1,0:T(8,128)(2,1)S(1)} %bitcast.8) | data formatting | bytes 262144
  23.8 0.7 %shard_map.97 = (bf16[256,256]{1,0:T(8,128)(2,1)}, bf16[256,256]{1,0:T(8,128)(2,1)}) custom-call(f32[2,256,256]{2,1,0:T(8,128)S(1)} %get-tuple-element.24.own, bf16[2,256,256]{2,1,0:T(8,128)(2,1)S(1)} %collective-permute-done.3.later), custom_call_target="tpu_custom_call" | custom-call | flops 1048576 | bytes 1048576 | tf_op jit(solution)/shard_map/pallas_call | solution.py:29
  24.5 0.7 %shard_map.99.refs_0_ = f32[512,256]{1,0:T(8,128)S(1)} custom-call(bf16[2,512,512]{2,1,0:T(8,128)(2,1)S(1)} %get-tuple-element.28.frames0, bf16[2,512,512]{2,1,0:T(8,128)(2,1)S(1)} %collective-permute-done.4.frames1, bf16[256,256]{1,0:T(8,128)(2,1)S(1)} %get-tuple-element.23.mine, bf16[256,256]{1,0:T(8,128)(2,1)S(1)} %collective-permute-done.5.peer, ...), custom_call_target="tpu_custom_call" | custom-call | flops 1048576 | bytes 1048576 | tf_op jit(solution)/shard_map/pallas_call | solution.py:29
  25.2 1.7 %collective-permute-done.11.refs_1_ = bf16[512,128]{1,0:T(8,128)(2,1)S(1)} collective-permute-done((bf16[512,128]{1,0:T(8,128)(2,1)S(1)}, bf16[512,128]{1,0:T(8,128)(2,1)S(1)}, u32[]{:S(2)}, u32[]{:S(2)}) %collective-permute-start.11) | collective-permute-done | bytes 131104 | tf_op jit(solution)/shard_map/ppermute | solution.py:196
  27.0 0.7 %shard_map.102.refs_2_ = f32[512,256]{1,0:T(8,128)} custom-call(f32[512,256]{1,0:T(8,128)S(1)} %shard_map.99.refs_0_, bf16[512,128]{1,0:T(8,128)(2,1)S(1)} %collective-permute-done.11.refs_1_), custom_call_target="tpu_custom_call" | custom-call | flops 1048576 | bytes 1048576 | tf_op jit(solution)/shard_map/pallas_call | solution.py:169
  27.7 1.6 %collective-permute-done.10.refs_1_ = bf16[512,128]{1,0:T(8,128)(2,1)S(1)} collective-permute-done((bf16[512,128]{1,0:T(8,128)(2,1)S(1)}, bf16[512,128]{1,0:T(8,128)(2,1)S(1)}, u32[]{:S(2)}, u32[]{:S(2)}) %collective-permute-start.10) | collective-permute-done | bytes 131104 | tf_op jit(solution)/shard_map/ppermute | solution.py:196
  29.3 0.7 %shard_map.103 = f32[512,256]{1,0:T(8,128)} custom-call(f32[512,256]{1,0:T(8,128)S(1)} %shard_map.99.refs_0_, bf16[512,128]{1,0:T(8,128)(2,1)S(1)} %collective-permute-done.10.refs_1_, f32[512,256]{1,0:T(8,128)} %shard_map.102.refs_2_), custom_call_target="tpu_custom_call", output_to_operand_aliasing={{}: (2, {})} | custom-call | flops 1048576 | bytes 1048576 | tf_op jit(solution)/shard_map/pallas_call | solution.py:169
  (24 shorter events, 0.8 us)
Async XLA Ops:
  0.6 1.6 %copy-start = (bf16[2,256,2048]{2,1,0:T(8,128)(2,1)S(1)}, bf16[2,256,2048]{2,1,0:T(8,128)(2,1)}, u32[]{:S(2)}) copy-start(bf16[2,256,2048]{2,1,0:T(8,128)(2,1)} %frames.1) | copy-start | bytes 6291460
  2.2 1.2 %copy-start.2 = (bf16[1,256,256]{2,1,0:T(8,128)(2,1)S(1)}, bf16[1,256,256]{2,1,0:T(8,128)(2,1)}, u32[]{:S(2)}) copy-start(bf16[1,256,256]{2,1,0:T(8,128)(2,1)} %param.7) | copy-start | bytes 393220
  2.2 1.4 %copy-start.4 = (bf16[1,256,256]{2,1,0:T(8,128)(2,1)S(1)}, bf16[1,256,256]{2,1,0:T(8,128)(2,1)}, u32[]{:S(2)}) copy-start(bf16[1,256,256]{2,1,0:T(8,128)(2,1)} %param.8) | copy-start | bytes 393220
  2.2 4.0 %copy-start.5 = (s32[1,256]{1,0:T(1,128)S(1)}, s32[1,256]{1,0:T(1,128)}, u32[]{:S(2)}) copy-start(s32[1,256]{1,0:T(1,128)} %seg.1) | copy-start | bytes 3076
  2.2 7.9 %copy-start.1 = (bf16[1,256,256]{2,1,0:T(8,128)(2,1)S(1)}, bf16[1,256,256]{2,1,0:T(8,128)(2,1)}, u32[]{:S(2)}) copy-start(bf16[1,256,256]{2,1,0:T(8,128)(2,1)} %param.9) | copy-start | bytes 393220
  2.2 7.9 %copy-start.3 = (bf16[1,256,256]{2,1,0:T(8,128)(2,1)S(1)}, bf16[1,256,256]{2,1,0:T(8,128)(2,1)}, u32[]{:S(2)}) copy-start(bf16[1,256,256]{2,1,0:T(8,128)(2,1)} %param.6) | copy-start | bytes 393220
  2.9 17.2 %collective-permute-start.4 = (bf16[2,512,512]{2,1,0:T(8,128)(2,1)S(1)}, bf16[2,512,512]{2,1,0:T(8,128)(2,1)S(1)}, u32[]{:S(2)}, u32[]{:S(2)}) collective-permute-start(bf16[2,512,512]{2,1,0:T(8,128)(2,1)S(1)} %get-tuple-element.29), channel_id=1, source_target_pairs={{0,8},{8,0},{16,24},{24,16},{1,9},{9,1},{17,25},{25,17},{2,10},{10... | collective-permute-start | bytes 3145736 | tf_op jit(solution)/shard_map/ppermute | solution.py:206
  3.4 6.7 %collective-permute-start = (bf16[256,256]{1,0:T(8,128)(2,1)S(1)}, bf16[256,256]{1,0:T(8,128)(2,1)S(1)}, u32[]{:S(2)}, u32[]{:S(2)}) collective-permute-start(bf16[256,256]{1,0:T(8,128)(2,1)S(1)} %bitcast.13), channel_id=1, source_target_pairs={{0,8},{8,16},{16,24},{24,0},{1,9},{9,17},{17,25},{25,1},{2,10},{10... | collective-permute-start | bytes 393224 | tf_op jit(solution)/shard_map/ppermute | solution.py:196
  3.6 7.0 %collective-permute-start.2 = (bf16[256,256]{1,0:T(8,128)(2,1)S(1)}, bf16[256,256]{1,0:T(8,128)(2,1)S(1)}, u32[]{:S(2)}, u32[]{:S(2)}) collective-permute-start(bf16[256,256]{1,0:T(8,128)(2,1)S(1)} %bitcast.19), channel_id=1, source_target_pairs={{0,8},{8,16},{16,24},{24,0},{1,9},{9,17},{17,25},{25,1},{2,10},{10... | collective-permute-start | bytes 393224 | tf_op jit(solution)/shard_map/ppermute | solution.py:196
  6.2 3.9 %collective-permute-start.1 = (s32[1,256]{1,0:T(1,128)S(1)}, s32[1,256]{1,0:T(1,128)S(1)}, u32[]{:S(2)}, u32[]{:S(2)}) collective-permute-start(s32[1,256]{1,0:T(1,128)S(1)} %copy-done.5), channel_id=1, source_target_pairs={{0,8},{8,16},{16,24},{24,0},{1,9},{9,17},{17,25},{25,1},{2,10},{10... | collective-permute-start | bytes 3080 | tf_op jit(solution)/shard_map/ppermute | solution.py:196
  11.2 5.1 %collective-permute-start.6 = (bf16[256,128]{1,0:T(8,128)(2,1)S(1)}, bf16[256,128]{1,0:T(8,128)(2,1)S(1)}, u32[]{:S(2)}, u32[]{:S(2)}) collective-permute-start(bf16[256,128]{1,0:T(8,128)(2,1)S(1)} %get-tuple-element.19.refs_0_), channel_id=1, source_target_pairs={{0,1},{1,0},{2,3},{3,2},{4,5},{5,4},{6,7},{7,6},{8,9},{9,8},{10,11... | collective-permute-start | bytes 196616 | tf_op jit(solution)/shard_map/ppermute | solution.py:238
  14.1 6.0 %collective-permute-start.5 = (bf16[256,256]{1,0:T(8,128)(2,1)S(1)}, bf16[256,256]{1,0:T(8,128)(2,1)S(1)}, u32[]{:S(2)}, u32[]{:S(2)}) collective-permute-start(bf16[256,256]{1,0:T(8,128)(2,1)S(1)} %get-tuple-element.23.mine), channel_id=1, source_target_pairs={{0,8},{8,0},{16,24},{24,16},{1,9},{9,1},{17,25},{25,17},{2,10},{10... | collective-permute-start | bytes 393224 | tf_op jit(solution)/shard_map/ppermute | solution.py:196
  14.2 9.6 %collective-permute-start.3 = (bf16[2,256,256]{2,1,0:T(8,128)(2,1)S(1)}, bf16[2,256,256]{2,1,0:T(8,128)(2,1)S(1)}, u32[]{:S(2)}, u32[]{:S(2)}) collective-permute-start(bf16[2,256,256]{2,1,0:T(8,128)(2,1)S(1)} %get-tuple-element.25), channel_id=1, source_target_pairs={{0,24},{8,0},{16,8},{24,16},{1,25},{9,1},{17,9},{25,17},{2,26},{10... | collective-permute-start | bytes 786440 | tf_op jit(solution)/shard_map/ppermute | solution.py:196
  15.8 4.3 %collective-permute-start.8 = (bf16[256,128]{1,0:T(8,128)(2,1)S(1)}, bf16[256,128]{1,0:T(8,128)(2,1)S(1)}, u32[]{:S(2)}, u32[]{:S(2)}) collective-permute-start(bf16[256,128]{1,0:T(8,128)(2,1)S(1)} %get-tuple-element.21.refs_2_), channel_id=1, source_target_pairs={{0,1},{1,0},{2,3},{3,2},{4,5},{5,4},{6,7},{7,6},{8,9},{9,8},{10,11... | collective-permute-start | bytes 196616 | tf_op jit(solution)/shard_map/ppermute | solution.py:238
  16.3 3.7 %collective-permute-start.7 = (bf16[256,128]{1,0:T(8,128)(2,1)S(1)}, bf16[256,128]{1,0:T(8,128)(2,1)S(1)}, u32[]{:S(2)}, u32[]{:S(2)}) collective-permute-start(bf16[256,128]{1,0:T(8,128)(2,1)S(1)} %collective-permute-done.6.refs_0_), channel_id=1, source_target_pairs={{0,8},{8,0},{16,24},{24,16},{1,9},{9,1},{17,25},{25,17},{2,10},{10... | collective-permute-start | bytes 196616 | tf_op jit(solution)/shard_map/ppermute | solution.py:196
  20.0 1.3 %collective-permute-start.9 = (bf16[256,128]{1,0:T(8,128)(2,1)S(1)}, bf16[256,128]{1,0:T(8,128)(2,1)S(1)}, u32[]{:S(2)}, u32[]{:S(2)}) collective-permute-start(bf16[256,128]{1,0:T(8,128)(2,1)S(1)} %collective-permute-done.8.refs_2_.refs_0_), channel_id=1, source_target_pairs={{0,8},{8,0},{16,24},{24,16},{1,9},{9,1},{17,25},{25,17},{2,10},{10... | collective-permute-start | bytes 196616 | tf_op jit(solution)/shard_map/ppermute | solution.py:196
  20.5 6.4 %collective-permute-start.11 = (bf16[512,128]{1,0:T(8,128)(2,1)S(1)}, bf16[512,128]{1,0:T(8,128)(2,1)S(1)}, u32[]{:S(2)}, u32[]{:S(2)}) collective-permute-start(bf16[512,128]{1,0:T(8,128)(2,1)S(1)} %shard_map.101), channel_id=1, source_target_pairs={{0,16},{8,24},{16,0},{24,8},{1,17},{9,25},{17,1},{25,9},{2,18},{10... | collective-permute-start | bytes 393224 | tf_op jit(solution)/shard_map/ppermute | solution.py:196
  21.7 7.5 %collective-permute-start.10 = (bf16[512,128]{1,0:T(8,128)(2,1)S(1)}, bf16[512,128]{1,0:T(8,128)(2,1)S(1)}, u32[]{:S(2)}, u32[]{:S(2)}) collective-permute-start(bf16[512,128]{1,0:T(8,128)(2,1)S(1)} %shard_map.100), channel_id=1, source_target_pairs={{0,16},{8,24},{16,0},{24,8},{1,17},{9,25},{17,1},{25,9},{2,18},{10... | collective-permute-start | bytes 393224 | tf_op jit(solution)/shard_map/ppermute | solution.py:196

commit v5 on v4

--- a/solution.py
+++ b/solution.py
@@ -133,25 +133,52 @@
                         out[part, :, r * length : (r + 1) * length] = jnp.transpose(tile)
 
 
-def panel_body(count, length, step, first, frames0, frames1, mine, peer, *refs):
-    grads, out = refs[:-1], refs[-1]
+def panel_terms(count, length, step, frames, grads, ages):
     part = lax.rem(lax.div(lax.axis_index("ctx"), 2) + step, lax.axis_size("ctx") // 2)
     wide = lax.axis_index("wide")
-    width = grads[0].shape[1]
+    total = None
+    for frame, grad, age in zip(frames, grads, ages):
+        rec = lax.rem(wide - age + count, count)
+        rows = pl.ds(pl.multiple_of(rec * length, HD), length)
+        term = dot(frame[part, :, rows], grad, 1, 0)
+        total = term if total is None else total + term
+    return total
+
+
+def first_body(count, length, step, chunk, mine_frames, peer_frames, mine, peer, *refs):
+    came, out = refs[:-1], refs[-1]
+    width = out.shape[1]
+    at = slice(chunk * width, (chunk + 1) * width)
+    out[...] = panel_terms(
+        count, length, step,
+        [mine_frames, peer_frames] + [mine_frames] * len(came),
+        [mine[:, at], peer[:, at]] + [ref[...] for ref in came],
+        [0, 0] + list(range(1, count)),
+    )
+
+
+def rest_body(count, length, step, peer_frames, begun, *refs):
+    shared, out = refs[:-1], refs[-1]
+    rest = panel_terms(
+        count, length, step, [peer_frames] * len(shared), [ref[...] for ref in shared], range(1, count)
+    )
+    out[...] = (begun[...] + rest).astype(out.dtype)
+
+
+def panel_body(count, length, mine_frames, peer_frames, mine, peer, *refs):
+    grads, out = refs[:-1], refs[-1]
+    each = 2 * (count - 1)
+    width = out.shape[1] * each // len(grads)
     for c in range(out.shape[1] // width):
-        at = slice((first + c) * width, (first + c + 1) * width)
-        pairs = [(mine[:, at], peer[:, at])]
-        for k in range(count - 1):
-            i = 2 * (c * (count - 1) + k)
-            pairs.append((grads[i][...], grads[i + 1][...]))
-        total = None
-        for k, pair in enumerate(pairs):
-            rec = lax.rem(wide - k + count, count)
-            rows = pl.ds(pl.multiple_of(rec * length, HD), length)
-            for frames, grad in zip((frames0, frames1), pair):
-                term = dot(frames[part, :, rows], grad, 1, 0)
-                total = term if total is None else total + term
-        out[:, c * width : (c + 1) * width] = total.astype(out.dtype)
+        at = slice(c * width, (c + 1) * width)
+        mine_grads = [mine[:, at]] + [ref[...] for ref in grads[c * each : (c + 1) * each : 2]]
+        peer_grads = [peer[:, at]] + [ref[...] for ref in grads[c * each + 1 : (c + 1) * each : 2]]
+        out[:, at] = panel_terms(
+            count, length, 0,
+            [mine_frames] * count + [peer_frames] * count,
+            mine_grads + peer_grads,
+            list(range(count)) * 2,
+        )
 
 
 def add_body(first, *refs):
@@ -239,21 +266,27 @@
             pieces += [piece, sent(piece, other)]
         grads.append(pieces)
 
-    def panel(step, first, pieces, width, dtype):
-        return call(
-            functools.partial(panel_body, wide_count, length, step, first),
-            vmem((block, width), dtype),
-            mine, given, dq, peer, *pieces,
-        )
-
     arrived = [[] for _ in range(chunks)]
     for step in range(1, parts):
         ring = [(i, (i + 2 * step) % ctx_count) for i in range(ctx_count)]
         for c in range(chunks):
-            piece = panel(step, c, grads[c], size * HD, BF16)
+            begun = call(
+                functools.partial(first_body, wide_count, length, step, c),
+                vmem((block, size * HD), F32),
+                mine, given, dq, peer, *grads[c][::2],
+            )
+            piece = call(
+                functools.partial(rest_body, wide_count, length, step),
+                vmem((block, size * HD), BF16),
+                given, begun, *grads[c][1::2],
+            )
             arrived[c].append(sent(piece, ring))
     dk, dv = call(join_body, (shape((length, columns), BF16),) * 2, own, later)
-    kept = panel(0, 0, sum(grads, []), columns, F32)
+    kept = call(
+        functools.partial(panel_body, wide_count, length),
+        vmem((block, columns), F32),
+        mine, given, dq, peer, *sum(grads, []),
+    )
     held = []
     for c in range(chunks):
         held = [add(c * size * HD, kept, arrived[c], held)]

time: 30.2 us -> 30 us (level)
  waiting for transfers between devices: 10.9 us -> 10.5 us
    ppermute x9, waiting for transfers between devices: 7.16 us -> 6.79 us  [sent(): return lax.ppermute(value, 'ctx', pairs)]
    pallas_call x9 -> x11, Pallas kernels: 4.94 us -> 5.24 us  [call(): pl.pallas_call(body, out_shape=outs, in_specs=[whole] * len(args), out_sp...]
  transfers between devices with their start and end apart: 12 -> 12, of which waited for: 5 -> 5; matrix products, arithmetic and copies ran while one was open for 2% -> 2% of each run, Pallas kernels for 17% -> 18%
where the time goes in v5:
time: 30 us; the launch traced here: 29.8 us
  waiting for transfers between devices  10.5 us (35%)
  starting transfers between devices  9.6 us (32%)
  Pallas kernels  6.69 us (22%)
  local copies, waits for them, and re-layouts  2.26 us (8%)
  between operations  0.77 us (3%)
    ppermute x9, waiting for transfers between devices, sent(): return lax.ppermute(value, 'ctx', pairs)  6.79 us
    ppermute x9, starting transfers between devices, sent(): return lax.ppermute(value, 'ctx', pairs)  6.64 us
    pallas_call x11, Pallas kernels, call(): pl.pallas_call(body, out_shape=outs, in_specs=[whole] * len(args), out_sp...  5.24 us
    ppermute x2, waiting for transfers between devices, shards(): piece = lax.ppermute(found[2 * c], 'wide', ring)  3.73 us
    ppermute x2, starting transfers between devices, shards(): piece = lax.ppermute(found[2 * c], 'wide', ring)  2.4 us
    unnamed x13, local copies, waits for them, and re-layouts  2.26 us
    pallas_call x2, Pallas kernels, add(): pl.pallas_call(functools.partial(add_body, first), grid=(1,), out_shape=s...  1.45 us
  transfers between devices with their start and end apart: 12, of which 5 were waited for; matrix products, arithmetic and copies ran while one was open for 2% of the time, Pallas kernels for 18%

profile of v5, /device:TPU:0, one launch (start us, length us, event | category | flops | bytes accessed | tf_op | source)
XLA Modules:
  0.0 29.8 jit_solution(8548585002312115875)
XLA Ops:
  0.6 1.6 %copy-done = bf16[2,256,2048]{2,1,0:T(8,128)(2,1)S(1)} copy-done((bf16[2,256,2048]{2,1,0:T(8,128)(2,1)S(1)}, bf16[2,256,2048]{2,1,0:T(8,128)(2,1)}, u32[]{:S(2)}) %copy-start) | copy-done | bytes 2097176
  2.2 0.6 %shard_map.98 = (bf16[2,512,512]{2,1,0:T(8,128)(2,1)S(1)}, bf16[2,512,512]{2,1,0:T(8,128)(2,1)S(1)}) custom-call(bf16[2,256,2048]{2,1,0:T(8,128)(2,1)S(1)} %copy-done), custom_call_target="tpu_custom_call" | custom-call | flops 1048576 | bytes 1048576 | tf_op jit(solution)/shard_map/pallas_call | solution.py:29
  2.9 0.6 %collective-permute-start.4 = (bf16[2,512,512]{2,1,0:T(8,128)(2,1)S(1)}, bf16[2,512,512]{2,1,0:T(8,128)(2,1)S(1)}, u32[]{:S(2)}, u32[]{:S(2)}) collective-permute-start(bf16[2,512,512]{2,1,0:T(8,128)(2,1)S(1)} %get-tuple-element.29), channel_id=1, source_target_pairs={{0,8},{8,0},{16,24},{24,16},{1,9},{9,1},{17,25},{25,17},{2,10},{10... | collective-permute-start | bytes 3145736 | tf_op jit(solution)/shard_map/ppermute | solution.py:233
  3.6 2.6 %collective-permute-start.2 = (bf16[256,256]{1,0:T(8,128)(2,1)S(1)}, bf16[256,256]{1,0:T(8,128)(2,1)S(1)}, u32[]{:S(2)}, u32[]{:S(2)}) collective-permute-start(bf16[256,256]{1,0:T(8,128)(2,1)S(1)} %bitcast.19), channel_id=1, source_target_pairs={{0,8},{8,16},{16,24},{24,0},{1,9},{9,17},{17,25},{25,1},{2,10},{10... | collective-permute-start | bytes 393224 | tf_op jit(solution)/shard_map/ppermute | solution.py:223
  6.6 3.6 %collective-permute-done.1.pseg = s32[1,256]{1,0:T(1,128)S(1)} collective-permute-done((s32[1,256]{1,0:T(1,128)S(1)}, s32[1,256]{1,0:T(1,128)S(1)}, u32[]{:S(2)}, u32[]{:S(2)}) %collective-permute-start.1) | collective-permute-done | bytes 1056 | tf_op jit(solution)/shard_map/ppermute | solution.py:223
  10.2 0.5 %shard_map.93 = (f32[2,256,256]{2,1,0:T(8,128)S(1)}, f32[2,256,256]{2,1,0:T(8,128)S(1)}) custom-call(bf16[256,256]{1,0:T(8,128)(2,1)S(1)} %bitcast.17, bf16[256,256]{1,0:T(8,128)(2,1)S(1)} %bitcast.14, bf16[256,256]{1,0:T(8,128)(2,1)S(1)} %bitcast.20, bf16[256,256]{1,0:T(8,128)(2,1)S(1)} %bitcast.9, bf16[256,256]{1,0:T(8,128)(2,1)S(1)} %collective-permute-done.pk, ...), custom_call_target="tpu_custom_call" | custom-call | flops 1048576 | bytes 1048576 | tf_op jit(solution)/shard_map/pallas_call | solution.py:29
  10.6 0.6 %shard_map.94 = (bf16[256,128]{1,0:T(8,128)(2,1)S(1)}, f32[1,256,256]{2,1,0:T(8,128)S(1)}) custom-call(bf16[256,256]{1,0:T(8,128)(2,1)S(1)} %bitcast.15, bf16[256,256]{1,0:T(8,128)(2,1)S(1)} %bitcast.10, bf16[256,256]{1,0:T(8,128)(2,1)S(1)} %collective-permute-done.pk, bf16[256,256]{1,0:T(8,128)(2,1)S(1)} %collective-permute-done.2.pv, ...), custom_call_target="tpu_custom_call" | custom-call | flops 1048576 | bytes 1048576 | tf_op jit(solution)/shard_map/pallas_call | solution.py:29
  11.2 0.6 %shard_map.95 = (bf16[256,128]{1,0:T(8,128)(2,1)S(1)}, f32[1,256,256]{2,1,0:T(8,128)S(1)}) custom-call(bf16[256,256]{1,0:T(8,128)(2,1)S(1)} %bitcast.16, bf16[256,256]{1,0:T(8,128)(2,1)S(1)} %bitcast.11, bf16[256,256]{1,0:T(8,128)(2,1)S(1)} %collective-permute-done.pk, bf16[256,256]{1,0:T(8,128)(2,1)S(1)} %collective-permute-done.2.pv, ...), custom_call_target="tpu_custom_call" | custom-call | flops 1048576 | bytes 1048576 | tf_op jit(solution)/shard_map/pallas_call | solution.py:29
  11.8 0.4 %shard_map.96 = (f32[2,256,256]{2,1,0:T(8,128)S(1)}, bf16[2,256,256]{2,1,0:T(8,128)(2,1)S(1)}, bf16[256,256]{1,0:T(8,128)(2,1)S(1)}) custom-call(bf16[256,256]{1,0:T(8,128)(2,1)S(1)} %bitcast.18, bf16[256,256]{1,0:T(8,128)(2,1)S(1)} %bitcast.12, f32[2,256,256]{2,1,0:T(8,128)S(1)} %get-tuple-element.17.prob, bf16[256,128]{1,0:T(8,128)(2,1)S(1)} %get-tuple-element.19.refs_0_, ...), custom_call_target="tpu_custom_call" | custom-call | flops 1048576 | bytes 1048576 | tf_op jit(solution)/shard_map/pallas_call | solution.py:29
  12.3 1.9 %collective-permute-start.6 = (bf16[256,128]{1,0:T(8,128)(2,1)S(1)}, bf16[256,128]{1,0:T(8,128)(2,1)S(1)}, u32[]{:S(2)}, u32[]{:S(2)}) collective-permute-start(bf16[256,128]{1,0:T(8,128)(2,1)S(1)} %get-tuple-element.19.refs_0_), channel_id=1, source_target_pairs={{0,1},{1,0},{2,3},{3,2},{4,5},{5,4},{6,7},{7,6},{8,9},{9,8},{10,11... | collective-permute-start | bytes 196616 | tf_op jit(solution)/shard_map/ppermute | solution.py:265
  14.2 1.3 %collective-permute-start.3 = (bf16[2,256,256]{2,1,0:T(8,128)(2,1)S(1)}, bf16[2,256,256]{2,1,0:T(8,128)(2,1)S(1)}, u32[]{:S(2)}, u32[]{:S(2)}) collective-permute-start(bf16[2,256,256]{2,1,0:T(8,128)(2,1)S(1)} %get-tuple-element.25), channel_id=1, source_target_pairs={{0,24},{8,0},{16,8},{24,16},{1,25},{9,1},{17,9},{25,17},{2,26},{10... | collective-permute-start | bytes 786440 | tf_op jit(solution)/shard_map/ppermute | solution.py:223
  15.4 0.5 %collective-permute-start.8 = (bf16[256,128]{1,0:T(8,128)(2,1)S(1)}, bf16[256,128]{1,0:T(8,128)(2,1)S(1)}, u32[]{:S(2)}, u32[]{:S(2)}) collective-permute-start(bf16[256,128]{1,0:T(8,128)(2,1)S(1)} %get-tuple-element.21.refs_2_), channel_id=1, source_target_pairs={{0,1},{1,0},{2,3},{3,2},{4,5},{5,4},{6,7},{7,6},{8,9},{9,8},{10,11... | collective-permute-start | bytes 196616 | tf_op jit(solution)/shard_map/ppermute | solution.py:265
  16.0 0.9 %collective-permute-done.6.refs_0_ = bf16[256,128]{1,0:T(8,128)(2,1)S(1)} collective-permute-done((bf16[256,128]{1,0:T(8,128)(2,1)S(1)}, bf16[256,128]{1,0:T(8,128)(2,1)S(1)}, u32[]{:S(2)}, u32[]{:S(2)}) %collective-permute-start.6) | collective-permute-done | bytes 65568 | tf_op jit(solution)/shard_map/ppermute | solution.py:265
  16.9 2.9 %collective-permute-done.8.refs_2_.refs_0_ = bf16[256,128]{1,0:T(8,128)(2,1)S(1)} collective-permute-done((bf16[256,128]{1,0:T(8,128)(2,1)S(1)}, bf16[256,128]{1,0:T(8,128)(2,1)S(1)}, u32[]{:S(2)}, u32[]{:S(2)}) %collective-permute-start.8) | collective-permute-done | bytes 65568 | tf_op jit(solution)/shard_map/ppermute | solution.py:265
  19.7 0.4 %shard_map.102.begun = f32[512,128]{1,0:T(8,128)S(1)} custom-call(bf16[2,512,512]{2,1,0:T(8,128)(2,1)S(1)} %get-tuple-element.28.mine_frames, bf16[2,512,512]{2,1,0:T(8,128)(2,1)S(1)} %collective-permute-done.4.peer_frames, bf16[256,256]{1,0:T(8,128)(2,1)S(1)} %get-tuple-element.23.mine, bf16[256,256]{1,0:T(8,128)(2,1)S(1)} %collective-permute-done.5.peer, ...), custom_call_target="tpu_custom_call" | custom-call | flops 1048576 | bytes 1048576 | tf_op jit(solution)/shard_map/pallas_call | solution.py:29
  20.3 0.6 %collective-permute-start.11 = (bf16[512,128]{1,0:T(8,128)(2,1)S(1)}, bf16[512,128]{1,0:T(8,128)(2,1)S(1)}, u32[]{:S(2)}, u32[]{:S(2)}) collective-permute-start(bf16[512,128]{1,0:T(8,128)(2,1)S(1)} %shard_map.103), channel_id=1, source_target_pairs={{0,16},{8,24},{16,0},{24,8},{1,17},{9,25},{17,1},{25,9},{2,18},{10... | collective-permute-start | bytes 393224 | tf_op jit(solution)/shard_map/ppermute | solution.py:223
  21.5 1.6 %collective-permute-start.10 = (bf16[512,128]{1,0:T(8,128)(2,1)S(1)}, bf16[512,128]{1,0:T(8,128)(2,1)S(1)}, u32[]{:S(2)}, u32[]{:S(2)}) collective-permute-start(bf16[512,128]{1,0:T(8,128)(2,1)S(1)} %shard_map.101), channel_id=1, source_target_pairs={{0,16},{8,24},{16,0},{24,8},{1,17},{9,25},{17,1},{25,9},{2,18},{10... | collective-permute-start | bytes 393224 | tf_op jit(solution)/shard_map/ppermute | solution.py:223
  23.1 0.7 %copy.12 = bf16[1,256,256]{2,1,0:T(8,128)(2,1)} copy(bf16[1,256,256]{2,1,0:T(8,128)(2,1)S(1)} %bitcast.8) | data formatting | bytes 262144
  23.8 0.7 %shard_map.97 = (bf16[256,256]{1,0:T(8,128)(2,1)}, bf16[256,256]{1,0:T(8,128)(2,1)}) custom-call(f32[2,256,256]{2,1,0:T(8,128)S(1)} %get-tuple-element.24.own, bf16[2,256,256]{2,1,0:T(8,128)(2,1)S(1)} %collective-permute-done.3.later), custom_call_target="tpu_custom_call" | custom-call | flops 1048576 | bytes 1048576 | tf_op jit(solution)/shard_map/pallas_call | solution.py:29
  24.5 0.7 %shard_map.99.refs_0_ = f32[512,256]{1,0:T(8,128)S(1)} custom-call(bf16[2,512,512]{2,1,0:T(8,128)(2,1)S(1)} %get-tuple-element.28.mine_frames, bf16[2,512,512]{2,1,0:T(8,128)(2,1)S(1)} %collective-permute-done.4.peer_frames, bf16[256,256]{1,0:T(8,128)(2,1)S(1)} %get-tuple-element.23.mine, bf16[256,256]{1,0:T(8,128)(2,1)S(1)} %collective-permute-done.5.peer, ...), custom_call_target="tpu_custom_call" | custom-call | flops 1048576 | bytes 1048576 | tf_op jit(solution)/shard_map/pallas_call | solution.py:29
  25.2 1.6 %collective-permute-done.11.refs_1_ = bf16[512,128]{1,0:T(8,128)(2,1)S(1)} collective-permute-done((bf16[512,128]{1,0:T(8,128)(2,1)S(1)}, bf16[512,128]{1,0:T(8,128)(2,1)S(1)}, u32[]{:S(2)}, u32[]{:S(2)}) %collective-permute-start.11) | collective-permute-done | bytes 131104 | tf_op jit(solution)/shard_map/ppermute | solution.py:223
  26.8 0.7 %shard_map.104.refs_2_ = f32[512,256]{1,0:T(8,128)} custom-call(f32[512,256]{1,0:T(8,128)S(1)} %shard_map.99.refs_0_, bf16[512,128]{1,0:T(8,128)(2,1)S(1)} %collective-permute-done.11.refs_1_), custom_call_target="tpu_custom_call" | custom-call | flops 1048576 | bytes 1048576 | tf_op jit(solution)/shard_map/pallas_call | solution.py:196
  27.5 1.6 %collective-permute-done.10.refs_1_ = bf16[512,128]{1,0:T(8,128)(2,1)S(1)} collective-permute-done((bf16[512,128]{1,0:T(8,128)(2,1)S(1)}, bf16[512,128]{1,0:T(8,128)(2,1)S(1)}, u32[]{:S(2)}, u32[]{:S(2)}) %collective-permute-start.10) | collective-permute-done | bytes 131104 | tf_op jit(solution)/shard_map/ppermute | solution.py:223
  29.1 0.7 %shard_map.105 = f32[512,256]{1,0:T(8,128)} custom-call(f32[512,256]{1,0:T(8,128)S(1)} %shard_map.99.refs_0_, bf16[512,128]{1,0:T(8,128)(2,1)S(1)} %collective-permute-done.10.refs_1_, f32[512,256]{1,0:T(8,128)} %shard_map.104.refs_2_), custom_call_target="tpu_custom_call", output_to_operand_aliasing={{}: (2, {})} | custom-call | flops 1048576 | bytes 1048576 | tf_op jit(solution)/shard_map/pallas_call | solution.py:196
  (26 shorter events, 1.4 us)
Async XLA Ops:
  0.6 1.6 %copy-start = (bf16[2,256,2048]{2,1,0:T(8,128)(2,1)S(1)}, bf16[2,256,2048]{2,1,0:T(8,128)(2,1)}, u32[]{:S(2)}) copy-start(bf16[2,256,2048]{2,1,0:T(8,128)(2,1)} %frames.1) | copy-start | bytes 6291460
  2.2 1.2 %copy-start.2 = (bf16[1,256,256]{2,1,0:T(8,128)(2,1)S(1)}, bf16[1,256,256]{2,1,0:T(8,128)(2,1)}, u32[]{:S(2)}) copy-start(bf16[1,256,256]{2,1,0:T(8,128)(2,1)} %param.7) | copy-start | bytes 393220
  2.2 1.4 %copy-start.4 = (bf16[1,256,256]{2,1,0:T(8,128)(2,1)S(1)}, bf16[1,256,256]{2,1,0:T(8,128)(2,1)}, u32[]{:S(2)}) copy-start(bf16[1,256,256]{2,1,0:T(8,128)(2,1)} %param.8) | copy-start | bytes 393220
  2.2 4.0 %copy-start.5 = (s32[1,256]{1,0:T(1,128)S(1)}, s32[1,256]{1,0:T(1,128)}, u32[]{:S(2)}) copy-start(s32[1,256]{1,0:T(1,128)} %seg.1) | copy-start | bytes 3076
  2.2 7.9 %copy-start.1 = (bf16[1,256,256]{2,1,0:T(8,128)(2,1)S(1)}, bf16[1,256,256]{2,1,0:T(8,128)(2,1)}, u32[]{:S(2)}) copy-start(bf16[1,256,256]{2,1,0:T(8,128)(2,1)} %param.9) | copy-start | bytes 393220
  2.2 7.9 %copy-start.3 = (bf16[1,256,256]{2,1,0:T(8,128)(2,1)S(1)}, bf16[1,256,256]{2,1,0:T(8,128)(2,1)}, u32[]{:S(2)}) copy-start(bf16[1,256,256]{2,1,0:T(8,128)(2,1)} %param.6) | copy-start | bytes 393220
  2.9 16.9 %collective-permute-start.4 = (bf16[2,512,512]{2,1,0:T(8,128)(2,1)S(1)}, bf16[2,512,512]{2,1,0:T(8,128)(2,1)S(1)}, u32[]{:S(2)}, u32[]{:S(2)}) collective-permute-start(bf16[2,512,512]{2,1,0:T(8,128)(2,1)S(1)} %get-tuple-element.29), channel_id=1, source_target_pairs={{0,8},{8,0},{16,24},{24,16},{1,9},{9,1},{17,25},{25,17},{2,10},{10... | collective-permute-start | bytes 3145736 | tf_op jit(solution)/shard_map/ppermute | solution.py:233
  3.4 6.7 %collective-permute-start = (bf16[256,256]{1,0:T(8,128)(2,1)S(1)}, bf16[256,256]{1,0:T(8,128)(2,1)S(1)}, u32[]{:S(2)}, u32[]{:S(2)}) collective-permute-start(bf16[256,256]{1,0:T(8,128)(2,1)S(1)} %bitcast.13), channel_id=1, source_target_pairs={{0,8},{8,16},{16,24},{24,0},{1,9},{9,17},{17,25},{25,1},{2,10},{10... | collective-permute-start | bytes 393224 | tf_op jit(solution)/shard_map/ppermute | solution.py:223
  3.6 7.0 %collective-permute-start.2 = (bf16[256,256]{1,0:T(8,128)(2,1)S(1)}, bf16[256,256]{1,0:T(8,128)(2,1)S(1)}, u32[]{:S(2)}, u32[]{:S(2)}) collective-permute-start(bf16[256,256]{1,0:T(8,128)(2,1)S(1)} %bitcast.19), channel_id=1, source_target_pairs={{0,8},{8,16},{16,24},{24,0},{1,9},{9,17},{17,25},{25,1},{2,10},{10... | collective-permute-start | bytes 393224 | tf_op jit(solution)/shard_map/ppermute | solution.py:223
  6.2 3.9 %collective-permute-start.1 = (s32[1,256]{1,0:T(1,128)S(1)}, s32[1,256]{1,0:T(1,128)S(1)}, u32[]{:S(2)}, u32[]{:S(2)}) collective-permute-start(s32[1,256]{1,0:T(1,128)S(1)} %copy-done.5), channel_id=1, source_target_pairs={{0,8},{8,16},{16,24},{24,0},{1,9},{9,17},{17,25},{25,1},{2,10},{10... | collective-permute-start | bytes 3080 | tf_op jit(solution)/shard_map/ppermute | solution.py:223
  12.2 7.5 %collective-permute-start.5 = (bf16[256,256]{1,0:T(8,128)(2,1)S(1)}, bf16[256,256]{1,0:T(8,128)(2,1)S(1)}, u32[]{:S(2)}, u32[]{:S(2)}) collective-permute-start(bf16[256,256]{1,0:T(8,128)(2,1)S(1)} %get-tuple-element.23.mine), channel_id=1, source_target_pairs={{0,8},{8,0},{16,24},{24,16},{1,9},{9,1},{17,25},{25,17},{2,10},{10... | collective-permute-start | bytes 393224 | tf_op jit(solution)/shard_map/ppermute | solution.py:223
  12.3 4.6 %collective-permute-start.6 = (bf16[256,128]{1,0:T(8,128)(2,1)S(1)}, bf16[256,128]{1,0:T(8,128)(2,1)S(1)}, u32[]{:S(2)}, u32[]{:S(2)}) collective-permute-start(bf16[256,128]{1,0:T(8,128)(2,1)S(1)} %get-tuple-element.19.refs_0_), channel_id=1, source_target_pairs={{0,1},{1,0},{2,3},{3,2},{4,5},{5,4},{6,7},{7,6},{8,9},{9,8},{10,11... | collective-permute-start | bytes 196616 | tf_op jit(solution)/shard_map/ppermute | solution.py:265
  14.2 9.6 %collective-permute-start.3 = (bf16[2,256,256]{2,1,0:T(8,128)(2,1)S(1)}, bf16[2,256,256]{2,1,0:T(8,128)(2,1)S(1)}, u32[]{:S(2)}, u32[]{:S(2)}) collective-permute-start(bf16[2,256,256]{2,1,0:T(8,128)(2,1)S(1)} %get-tuple-element.25), channel_id=1, source_target_pairs={{0,24},{8,0},{16,8},{24,16},{1,25},{9,1},{17,9},{25,17},{2,26},{10... | collective-permute-start | bytes 786440 | tf_op jit(solution)/shard_map/ppermute | solution.py:223
  15.4 4.3 %collective-permute-start.8 = (bf16[256,128]{1,0:T(8,128)(2,1)S(1)}, bf16[256,128]{1,0:T(8,128)(2,1)S(1)}, u32[]{:S(2)}, u32[]{:S(2)}) collective-permute-start(bf16[256,128]{1,0:T(8,128)(2,1)S(1)} %get-tuple-element.21.refs_2_), channel_id=1, source_target_pairs={{0,1},{1,0},{2,3},{3,2},{4,5},{5,4},{6,7},{7,6},{8,9},{9,8},{10,11... | collective-permute-start | bytes 196616 | tf_op jit(solution)/shard_map/ppermute | solution.py:265
  16.8 3.2 %collective-permute-start.7 = (bf16[256,128]{1,0:T(8,128)(2,1)S(1)}, bf16[256,128]{1,0:T(8,128)(2,1)S(1)}, u32[]{:S(2)}, u32[]{:S(2)}) collective-permute-start(bf16[256,128]{1,0:T(8,128)(2,1)S(1)} %collective-permute-done.6.refs_0_), channel_id=1, source_target_pairs={{0,8},{8,0},{16,24},{24,16},{1,9},{9,1},{17,25},{25,17},{2,10},{10... | collective-permute-start | bytes 196616 | tf_op jit(solution)/shard_map/ppermute | solution.py:223
  19.7 1.6 %collective-permute-start.9 = (bf16[256,128]{1,0:T(8,128)(2,1)S(1)}, bf16[256,128]{1,0:T(8,128)(2,1)S(1)}, u32[]{:S(2)}, u32[]{:S(2)}) collective-permute-start(bf16[256,128]{1,0:T(8,128)(2,1)S(1)} %collective-permute-done.8.refs_2_.refs_0_), channel_id=1, source_target_pairs={{0,8},{8,0},{16,24},{24,16},{1,9},{9,1},{17,25},{25,17},{2,10},{10... | collective-permute-start | bytes 196616 | tf_op jit(solution)/shard_map/ppermute | solution.py:223
  20.3 6.4 %collective-permute-start.11 = (bf16[512,128]{1,0:T(8,128)(2,1)S(1)}, bf16[512,128]{1,0:T(8,128)(2,1)S(1)}, u32[]{:S(2)}, u32[]{:S(2)}) collective-permute-start(bf16[512,128]{1,0:T(8,128)(2,1)S(1)} %shard_map.103), channel_id=1, source_target_pairs={{0,16},{8,24},{16,0},{24,8},{1,17},{9,25},{17,1},{25,9},{2,18},{10... | collective-permute-start | bytes 393224 | tf_op jit(solution)/shard_map/ppermute | solution.py:223
  21.5 7.6 %collective-permute-start.10 = (bf16[512,128]{1,0:T(8,128)(2,1)S(1)}, bf16[512,128]{1,0:T(8,128)(2,1)S(1)}, u32[]{:S(2)}, u32[]{:S(2)}) collective-permute-start(bf16[512,128]{1,0:T(8,128)(2,1)S(1)} %shard_map.101), channel_id=1, source_target_pairs={{0,16},{8,24},{16,0},{24,8},{1,17},{9,25},{17,1},{25,9},{2,18},{10... | collective-permute-start | bytes 393224 | tf_op jit(solution)/shard_map/ppermute | solution.py:223

commit v6 on v5

--- a/solution.py
+++ b/solution.py
@@ -68,33 +68,42 @@
     return weight * (1.0 / jnp.sum(weight, axis=0, keepdims=True))
 
 
-def prob_body(length, heads, q, k, v, g, pk, seg, pseg, prob, own_grad):
+def prob_body(length, heads, q, k, v, g, pk, seg, pseg, prob, turned, own_grad):
     own, valid = masks(length, seg, pseg)
     for h in range(heads):
         at = head(h)
         prob[h] = head_prob(own, valid, q[:, at], k[:, at], pk[:, at])
-        own_grad[h] = dot(v[:, at], g[:, at], 1, 1)
-
-
-def query_body(length, heads, first, k, g, pk, pv, prob, own_grad, dq, ds):
-    own = lower(length)
-    own_query = jnp.logical_not(own) | (
-        lax.broadcasted_iota(jnp.int32, (length, length), 0)
-        == lax.broadcasted_iota(jnp.int32, (length, length), 1)
-    )
+        turned[h] = jnp.transpose(prob[h])
+        own_grad[h] = dot(g[:, at], v[:, at], 1, 1)
+
+
+def upper(length):
+    return lax.broadcasted_iota(jnp.int32, (length, length), 1) <= lax.broadcasted_iota(
+        jnp.int32, (length, length), 0
+    )
+
+
+def query_body(length, heads, first, k, g, pk, pv, turned, own_grad, dq, ds):
+    own = upper(length)
+    step = length // 2
+    blocks = [slice(start, start + step) for start in range(0, length, step)]
     for h in range(heads):
         at = head(first + h)
-        weight = prob[first + h]
-        grad_prob = jnp.where(own, own_grad[first + h], dot(pv[:, at], g[:, at], 1, 1))
-        grad_score = weight * (
-            grad_prob - jnp.sum(weight * grad_prob, axis=0, keepdims=True)
-        )
-        ds[h] = grad_score
-        turned = jnp.transpose(grad_score)
-        own_part = jnp.where(own_query, turned, 0.0).astype(BF16)
-        prior_part = jnp.where(own_query, 0.0, turned).astype(BF16)
-        total = dot(own_part, k[:, at], 1, 0) + dot(prior_part, pk[:, at], 1, 0)
-        dq[:, head(h)] = (total * HD ** (-0.5)).astype(BF16)
+        weights = [turned[first + h, rows] for rows in blocks]
+        grads = [
+            jnp.where(own[rows], own_grad[first + h, rows], dot(g[rows, at], pv[:, at], 1, 1))
+            for rows in blocks
+        ]
+        for rows, weight, grad_prob in zip(blocks, weights, grads):
+            grad_score = weight * (
+                grad_prob - jnp.sum(weight * grad_prob, axis=1, keepdims=True)
+            )
+            own_part = jnp.where(own[rows], grad_score, 0.0).astype(BF16)
+            prior_part = jnp.where(own[rows], 0.0, grad_score).astype(BF16)
+            total = dot(own_part, k[:, at], 1, 0) + dot(prior_part, pk[:, at], 1, 0)
+            dq[rows, head(h)] = (total * HD ** (-0.5)).astype(BF16)
+            ds[0, h, rows] = own_part
+            ds[1, h, rows] = prior_part
 
 
 def terms_body(length, heads, size, q, g, prob, *refs):
@@ -106,13 +115,12 @@
     for h in range(heads):
         at = head(h)
         ds = pieces[h // size][1]
-        for index, (left, right) in enumerate(((ds[h % size], q), (prob[h], g))):
-            own_out[index, :, at] = dot(
-                jnp.where(own, left, 0.0).astype(BF16), right[:, at], 1, 0
-            )
-            back_out[index, :, at] = dot(
-                jnp.where(own, 0.0, left).astype(BF16), right[:, at], 1, 0
-            ).astype(BF16)
+        own_out[0, :, at] = dot(ds[0, h % size], q[:, at], 0, 0)
+        back_out[0, :, at] = dot(ds[1, h % size], q[:, at], 0, 0).astype(BF16)
+        own_out[1, :, at] = dot(jnp.where(own, prob[h], 0.0).astype(BF16), g[:, at], 1, 0)
+        back_out[1, :, at] = dot(
+            jnp.where(own, 0.0, prob[h]).astype(BF16), g[:, at], 1, 0
+        ).astype(BF16)
 
 
 def join_body(own, later, dk, dv):
@@ -120,17 +128,56 @@
     dv[...] = (own[1] + later[1].astype(F32)).astype(BF16)
 
 
-def turn_body(recs, length, block, parts, frames, mine, theirs):
-    for side in range(2):
-
-        @pl.when(lax.rem(lax.axis_index("ctx"), 2) == side)
-        def _():
-            for part in range(parts):
-                for r in range(recs):
-                    for out, which in ((mine, side), (theirs, 1 - side)):
-                        start = (2 * part + which) * block
-                        tile = frames[r, :, start : start + block]
-                        out[part, :, r * length : (r + 1) * length] = jnp.transpose(tile)
+def open_body(block, parts, *refs):
+    count = (len(refs) - 6) // 2
+    sources, frames = refs[:count], refs[count]
+    outs, (mine, theirs) = refs[count + 1 : 2 * count + 1], refs[2 * count + 1 : 2 * count + 3]
+    held, sems, frame_sems = refs[-3:]
+    recs, length, _ = frames.shape
+    copies = [
+        pltpu.make_async_copy(source, out, sems.at[n]) for n, (source, out) in enumerate(zip(sources, outs))
+    ]
+    tiles = [(r, part) for part in range(parts) for r in range(recs)]
+    loads = [
+        pltpu.make_async_copy(
+            frames.at[r, :, pl.ds(2 * part * block, 2 * block)], held.at[n], frame_sems.at[n]
+        )
+        for n, (r, part) in enumerate(tiles)
+    ]
+    for copy in loads + copies:
+        copy.start()
+    for n, (r, part) in enumerate(tiles):
+        loads[n].wait()
+        for side in range(2):
+
+            @pl.when(lax.rem(lax.axis_index("ctx"), 2) == side)
+            def _():
+                for out, which in ((mine, side), (theirs, 1 - side)):
+                    tile = held[n, :, which * block : (which + 1) * block]
+                    out[part, :, r * length : (r + 1) * length] = jnp.transpose(tile)
+
+    for copy in copies:
+        copy.wait()
+
+
+def open_all(parts, block, frames, *arrays):
+    recs, length, _ = frames.shape
+    outs = [vmem(a.shape, a.dtype) for a in arrays]
+    outs += [vmem((parts, block, recs * length), BF16)] * 2
+    return pl.pallas_call(
+        functools.partial(open_body, block, parts),
+        out_shape=tuple(outs),
+        in_specs=[pl.BlockSpec(memory_space=pltpu.HBM)] * (len(arrays) + 1),
+        out_specs=(pl.BlockSpec(memory_space=pltpu.VMEM),) * len(outs),
+        scratch_shapes=[
+            pltpu.VMEM((recs * parts, length, 2 * block), BF16),
+            pltpu.SemaphoreType.DMA((len(arrays),)),
+            pltpu.SemaphoreType.DMA((recs * parts,)),
+        ],
+        cost_estimate=pl.CostEstimate(flops=1 << 20, bytes_accessed=4 << 20, transcendentals=0),
+        compiler_params=pltpu.CompilerParams(vmem_limit_bytes=24 << 20),
+        name="open",
+    )(*[pltpu.with_memory_space_constraint(a, pltpu.HBM) for a in (*arrays, frames)])
 
 
 def panel_terms(count, length, step, frames, grads, ages):
@@ -226,25 +273,22 @@
     pk = sent(k, onward)
     pv = sent(v, onward)
 
-    turned = vmem((parts, block, recs * length), BF16)
-    mine, theirs = call(
-        functools.partial(turn_body, recs, length, block, parts), (turned, turned), frames
-    )
+    q, k, v, g, segment, mine, theirs = open_all(parts, block, frames, q, k, v, g, segment)
     given = lax.ppermute(theirs, "ctx", other)
 
     chunks = 2 if heads % 2 == 0 else 1
     size = heads // chunks
     square = vmem((heads, length, length), F32)
-    prob, own_grad = call(
-        functools.partial(prob_body, length, heads), (square, square),
+    prob, turned_prob, own_grad = call(
+        functools.partial(prob_body, length, heads), (square, square, square),
         q, k, v, g, pk, segment, pseg,
     )
     found = []
     for c in range(chunks):
         found += call(
             functools.partial(query_body, length, size, c * size),
-            (vmem((length, size * HD), BF16), vmem((size, length, length), F32)),
-            k, g, pk, pv, prob, own_grad,
+            (vmem((length, size * HD), BF16), vmem((2, size, length, length), BF16)),
+            k, g, pk, pv, turned_prob, own_grad,
         )
     own, to_prior, dq = call(
         functools.partial(terms_body, length, heads, size),

time: 30 us -> 29.6 us (0.987)
  local copies, waits for them, and re-layouts: 2.26 us -> 0.67 us
  Pallas kernels: 6.69 us -> 8.06 us
    pallas_call x0 -> x1, Pallas kernels: none -> 2.03 us  [open_all(): pl.pallas_call(functools.partial(open_body, block, parts), out_shape=tupl...]
    unnamed x13 -> x7, local copies, waits for them, and re-layouts: 2.26 us -> 0.67 us
    pallas_call x11 -> x10, Pallas kernels: 5.24 us -> 4.58 us  [call(): pl.pallas_call(body, out_shape=outs, in_specs=[whole] * len(args), out_sp...]
where the time goes in v6:
time: 29.6 us; the launch traced here: 29.5 us
  waiting for transfers between devices  10.5 us (35%)
  starting transfers between devices  9.47 us (32%)
  Pallas kernels  8.06 us (27%)
  between operations  0.75 us (3%)
  local copies, waits for them, and re-layouts  0.67 us (2%)
    ppermute x9, waiting for transfers between devices, sent(): return lax.ppermute(value, 'ctx', pairs)  6.79 us
    ppermute x9, starting transfers between devices, sent(): return lax.ppermute(value, 'ctx', pairs)  6.64 us
    pallas_call x10, Pallas kernels, call(): pl.pallas_call(body, out_shape=outs, in_specs=[whole] * len(args), out_sp...  4.58 us
    ppermute x2, waiting for transfers between devices, shards(): piece = lax.ppermute(found[2 * c], 'wide', ring)  3.73 us
    ppermute x2, starting transfers between devices, shards(): piece = lax.ppermute(found[2 * c], 'wide', ring)  2.28 us
    pallas_call x1, Pallas kernels, open_all(): pl.pallas_call(functools.partial(open_body, block, parts), out_shape=tupl...  2.03 us
    pallas_call x2, Pallas kernels, add(): pl.pallas_call(functools.partial(add_body, first), grid=(1,), out_shape=s...  1.45 us
    unnamed x7, local copies, waits for them, and re-layouts  0.67 us
  transfers between devices with their start and end apart: 12, of which 5 were waited for; matrix products, arithmetic and copies ran while one was open for 2% of the time, Pallas kernels for 18%

profile of v6, /device:TPU:0, one launch (start us, length us, event | category | flops | bytes accessed | tf_op | source)
XLA Modules:
  0.0 29.5 jit_solution(11460705961377003510)
XLA Ops:
  0.7 2.0 %open.1 = (bf16[256,256]{1,0:T(8,128)(2,1)S(1)}, bf16[256,256]{1,0:T(8,128)(2,1)S(1)}, bf16[256,256]{1,0:T(8,128)(2,1)S(1)}, bf16[256,256]{1,0:T(8,128)(2,1)S(1)...) custom-call(bf16[256,256]{1,0:T(8,128)(2,1)} %bitcast.10, ...), custom_call_target="tpu_custom_call" | custom-call | flops 1048576 | bytes 4194304 | tf_op jit(solution)/shard_map/open/pallas_call | solution.py:167
  2.7 0.6 %collective-permute-start.4 = (bf16[2,512,512]{2,1,0:T(8,128)(2,1)S(1)}, bf16[2,512,512]{2,1,0:T(8,128)(2,1)S(1)}, u32[]{:S(2)}, u32[]{:S(2)}) collective-permute-start(bf16[2,512,512]{2,1,0:T(8,128)(2,1)S(1)} %get-tuple-element.41), channel_id=1, source_target_pairs={{0,8},{8,0},{16,24},{24,16},{1,9},{9,1},{17,25},{25,17},{2,10},{10... | collective-permute-start | bytes 3145736 | tf_op jit(solution)/shard_map/ppermute | solution.py:277
  3.3 2.6 %collective-permute-start.2 = (bf16[256,256]{1,0:T(8,128)(2,1)S(1)}, bf16[256,256]{1,0:T(8,128)(2,1)S(1)}, u32[]{:S(2)}, u32[]{:S(2)}) collective-permute-start(bf16[256,256]{1,0:T(8,128)(2,1)S(1)} %bitcast.15), channel_id=1, source_target_pairs={{0,8},{8,16},{16,24},{24,0},{1,9},{9,17},{17,25},{25,1},{2,10},{10... | collective-permute-start | bytes 393224 | tf_op jit(solution)/shard_map/ppermute | solution.py:270
  6.0 0.4 %collective-permute-start.1 = (s32[1,256]{1,0:T(1,128)S(1)}, s32[1,256]{1,0:T(1,128)S(1)}, u32[]{:S(2)}, u32[]{:S(2)}) collective-permute-start(s32[1,256]{1,0:T(1,128)S(1)} %copy-done.2), channel_id=1, source_target_pairs={{0,8},{8,16},{16,24},{24,0},{1,9},{9,17},{17,25},{25,1},{2,10},{10... | collective-permute-start | bytes 3080 | tf_op jit(solution)/shard_map/ppermute | solution.py:270
  6.4 3.6 %collective-permute-done.1.pseg = s32[1,256]{1,0:T(1,128)S(1)} collective-permute-done((s32[1,256]{1,0:T(1,128)S(1)}, s32[1,256]{1,0:T(1,128)S(1)}, u32[]{:S(2)}, u32[]{:S(2)}) %collective-permute-start.1) | collective-permute-done | bytes 1056 | tf_op jit(solution)/shard_map/ppermute | solution.py:270
  10.0 0.6 %shard_map.93 = (f32[2,256,256]{2,1,0:T(8,128)S(1)}, f32[2,256,256]{2,1,0:T(8,128)S(1)}, f32[2,256,256]{2,1,0:T(8,128)S(1)}) custom-call(bf16[256,256]{1,0:T(8,128)(2,1)S(1)} %get-tuple-element.23.q, bf16[256,256]{1,0:T(8,128)(2,1)S(1)} %get-tuple-element.25.k, bf16[256,256]{1,0:T(8,128)(2,1)S(1)} %get-tuple-element.26.v, ...), custom_call_target="tpu_custom_call" | custom-call | flops 1048576 | bytes 1048576 | tf_op jit(solution)/shard_map/pallas_call | solution.py:29
  10.6 0.4 %shard_map.95 = (bf16[256,128]{1,0:T(8,128)(2,1)S(1)}, bf16[2,1,256,256]{3,2,1,0:T(8,128)(2,1)S(1)}) custom-call(bf16[256,256]{1,0:T(8,128)(2,1)S(1)} %get-tuple-element.25.k, bf16[256,256]{1,0:T(8,128)(2,1)S(1)} %get-tuple-element.24.g, bf16[256,256]{1,0:T(8,128)(2,1)S(1)} %collective-permute-done.pk, bf16[256,256]{1,0:T(8,128)(2,1)S(1)} %collective-permute-done.2.pv, ...), custom_call_target="tpu_custom_call" | custom-call | flops 1048576 | bytes 1048576 | tf_op jit(solution)/shard_map/pallas_call | solution.py:29
  11.0 0.4 %shard_map.94 = (bf16[256,128]{1,0:T(8,128)(2,1)S(1)}, bf16[2,1,256,256]{3,2,1,0:T(8,128)(2,1)S(1)}) custom-call(bf16[256,256]{1,0:T(8,128)(2,1)S(1)} %get-tuple-element.25.k, bf16[256,256]{1,0:T(8,128)(2,1)S(1)} %get-tuple-element.24.g, bf16[256,256]{1,0:T(8,128)(2,1)S(1)} %collective-permute-done.pk, bf16[256,256]{1,0:T(8,128)(2,1)S(1)} %collective-permute-done.2.pv, ...), custom_call_target="tpu_custom_call" | custom-call | flops 1048576 | bytes 1048576 | tf_op jit(solution)/shard_map/pallas_call | solution.py:29
  11.5 0.5 %shard_map.96 = (f32[2,256,256]{2,1,0:T(8,128)S(1)}, bf16[2,256,256]{2,1,0:T(8,128)(2,1)S(1)}, bf16[256,256]{1,0:T(8,128)(2,1)S(1)}) custom-call(bf16[256,256]{1,0:T(8,128)(2,1)S(1)} %get-tuple-element.23.q, bf16[256,256]{1,0:T(8,128)(2,1)S(1)} %get-tuple-element.24.g, f32[2,256,256]{2,1,0:T(8,128)S(1)} %get-tuple-element.28.prob, ...), custom_call_target="tpu_custom_call" | custom-call | flops 1048576 | bytes 1048576 | tf_op jit(solution)/shard_map/pallas_call | solution.py:29
  12.0 1.7 %collective-permute-start.6 = (bf16[256,128]{1,0:T(8,128)(2,1)S(1)}, bf16[256,128]{1,0:T(8,128)(2,1)S(1)}, u32[]{:S(2)}, u32[]{:S(2)}) collective-permute-start(bf16[256,128]{1,0:T(8,128)(2,1)S(1)} %get-tuple-element.31.refs_0_), channel_id=1, source_target_pairs={{0,1},{1,0},{2,3},{3,2},{4,5},{5,4},{6,7},{7,6},{8,9},{9,8},{10,11... | collective-permute-start | bytes 196616 | tf_op jit(solution)/shard_map/ppermute | solution.py:309
  13.8 1.3 %collective-permute-start.3 = (bf16[2,256,256]{2,1,0:T(8,128)(2,1)S(1)}, bf16[2,256,256]{2,1,0:T(8,128)(2,1)S(1)}, u32[]{:S(2)}, u32[]{:S(2)}) collective-permute-start(bf16[2,256,256]{2,1,0:T(8,128)(2,1)S(1)} %get-tuple-element.37), channel_id=1, source_target_pairs={{0,24},{8,0},{16,8},{24,16},{1,25},{9,1},{17,9},{25,17},{2,26},{10... | collective-permute-start | bytes 786440 | tf_op jit(solution)/shard_map/ppermute | solution.py:270
  15.1 0.5 %collective-permute-start.8 = (bf16[256,128]{1,0:T(8,128)(2,1)S(1)}, bf16[256,128]{1,0:T(8,128)(2,1)S(1)}, u32[]{:S(2)}, u32[]{:S(2)}) collective-permute-start(bf16[256,128]{1,0:T(8,128)(2,1)S(1)} %get-tuple-element.33.refs_2_), channel_id=1, source_target_pairs={{0,1},{1,0},{2,3},{3,2},{4,5},{5,4},{6,7},{7,6},{8,9},{9,8},{10,11... | collective-permute-start | bytes 196616 | tf_op jit(solution)/shard_map/ppermute | solution.py:309
  15.6 0.9 %collective-permute-done.6.refs_0_ = bf16[256,128]{1,0:T(8,128)(2,1)S(1)} collective-permute-done((bf16[256,128]{1,0:T(8,128)(2,1)S(1)}, bf16[256,128]{1,0:T(8,128)(2,1)S(1)}, u32[]{:S(2)}, u32[]{:S(2)}) %collective-permute-start.6) | collective-permute-done | bytes 65568 | tf_op jit(solution)/shard_map/ppermute | solution.py:309
  16.5 2.8 %collective-permute-done.8.refs_2_.refs_0_ = bf16[256,128]{1,0:T(8,128)(2,1)S(1)} collective-permute-done((bf16[256,128]{1,0:T(8,128)(2,1)S(1)}, bf16[256,128]{1,0:T(8,128)(2,1)S(1)}, u32[]{:S(2)}, u32[]{:S(2)}) %collective-permute-start.8) | collective-permute-done | bytes 65568 | tf_op jit(solution)/shard_map/ppermute | solution.py:309
  19.3 0.4 %shard_map.101.begun = f32[512,128]{1,0:T(8,128)S(1)} custom-call(bf16[2,512,512]{2,1,0:T(8,128)(2,1)S(1)} %get-tuple-element.40.mine_frames, bf16[2,512,512]{2,1,0:T(8,128)(2,1)S(1)} %collective-permute-done.4.peer_frames, bf16[256,256]{1,0:T(8,128)(2,1)S(1)} %get-tuple-element.35.mine, bf16[256,256]{1,0:T(8,128)(2,1)S(1)} %collective-permute-done.5.peer, ...), custom_call_target="tpu_custom_call" | custom-call | flops 1048576 | bytes 1048576 | tf_op jit(solution)/shard_map/pallas_call | solution.py:29
  20.0 0.6 %collective-permute-start.11 = (bf16[512,128]{1,0:T(8,128)(2,1)S(1)}, bf16[512,128]{1,0:T(8,128)(2,1)S(1)}, u32[]{:S(2)}, u32[]{:S(2)}) collective-permute-start(bf16[512,128]{1,0:T(8,128)(2,1)S(1)} %shard_map.102), channel_id=1, source_target_pairs={{0,16},{8,24},{16,0},{24,8},{1,17},{9,25},{17,1},{25,9},{2,18},{10... | collective-permute-start | bytes 393224 | tf_op jit(solution)/shard_map/ppermute | solution.py:270
  21.1 1.6 %collective-permute-start.10 = (bf16[512,128]{1,0:T(8,128)(2,1)S(1)}, bf16[512,128]{1,0:T(8,128)(2,1)S(1)}, u32[]{:S(2)}, u32[]{:S(2)}) collective-permute-start(bf16[512,128]{1,0:T(8,128)(2,1)S(1)} %shard_map.100), channel_id=1, source_target_pairs={{0,16},{8,24},{16,0},{24,8},{1,17},{9,25},{17,1},{25,9},{2,18},{10... | collective-permute-start | bytes 393224 | tf_op jit(solution)/shard_map/ppermute | solution.py:270
  22.7 0.7 %copy.12 = bf16[1,256,256]{2,1,0:T(8,128)(2,1)} copy(bf16[1,256,256]{2,1,0:T(8,128)(2,1)S(1)} %bitcast.8) | data formatting | bytes 262144
  23.4 0.7 %shard_map.97 = (bf16[256,256]{1,0:T(8,128)(2,1)}, bf16[256,256]{1,0:T(8,128)(2,1)}) custom-call(f32[2,256,256]{2,1,0:T(8,128)S(1)} %get-tuple-element.36.own, bf16[2,256,256]{2,1,0:T(8,128)(2,1)S(1)} %collective-permute-done.3.later), custom_call_target="tpu_custom_call" | custom-call | flops 1048576 | bytes 1048576 | tf_op jit(solution)/shard_map/pallas_call | solution.py:29
  24.1 0.7 %shard_map.98.refs_0_ = f32[512,256]{1,0:T(8,128)S(1)} custom-call(bf16[2,512,512]{2,1,0:T(8,128)(2,1)S(1)} %get-tuple-element.40.mine_frames, bf16[2,512,512]{2,1,0:T(8,128)(2,1)S(1)} %collective-permute-done.4.peer_frames, bf16[256,256]{1,0:T(8,128)(2,1)S(1)} %get-tuple-element.35.mine, bf16[256,256]{1,0:T(8,128)(2,1)S(1)} %collective-permute-done.5.peer, ...), custom_call_target="tpu_custom_call" | custom-call | flops 1048576 | bytes 1048576 | tf_op jit(solution)/shard_map/pallas_call | solution.py:29
  24.8 1.6 %collective-permute-done.11.refs_1_ = bf16[512,128]{1,0:T(8,128)(2,1)S(1)} collective-permute-done((bf16[512,128]{1,0:T(8,128)(2,1)S(1)}, bf16[512,128]{1,0:T(8,128)(2,1)S(1)}, u32[]{:S(2)}, u32[]{:S(2)}) %collective-permute-start.11) | collective-permute-done | bytes 131104 | tf_op jit(solution)/shard_map/ppermute | solution.py:270
  26.4 0.7 %shard_map.103.refs_2_ = f32[512,256]{1,0:T(8,128)} custom-call(f32[512,256]{1,0:T(8,128)S(1)} %shard_map.98.refs_0_, bf16[512,128]{1,0:T(8,128)(2,1)S(1)} %collective-permute-done.11.refs_1_), custom_call_target="tpu_custom_call" | custom-call | flops 1048576 | bytes 1048576 | tf_op jit(solution)/shard_map/pallas_call | solution.py:243
  27.1 1.6 %collective-permute-done.10.refs_1_ = bf16[512,128]{1,0:T(8,128)(2,1)S(1)} collective-permute-done((bf16[512,128]{1,0:T(8,128)(2,1)S(1)}, bf16[512,128]{1,0:T(8,128)(2,1)S(1)}, u32[]{:S(2)}, u32[]{:S(2)}) %collective-permute-start.10) | collective-permute-done | bytes 131104 | tf_op jit(solution)/shard_map/ppermute | solution.py:270
  28.7 0.7 %shard_map.104 = f32[512,256]{1,0:T(8,128)} custom-call(f32[512,256]{1,0:T(8,128)S(1)} %shard_map.98.refs_0_, bf16[512,128]{1,0:T(8,128)(2,1)S(1)} %collective-permute-done.10.refs_1_, f32[512,256]{1,0:T(8,128)} %shard_map.103.refs_2_), custom_call_target="tpu_custom_call", output_to_operand_aliasing={{}: (2, {})} | custom-call | flops 1048576 | bytes 1048576 | tf_op jit(solution)/shard_map/pallas_call | solution.py:243
  (20 shorter events, 1.0 us)
Async XLA Ops:
  0.6 5.3 %copy-start.2 = (s32[1,256]{1,0:T(1,128)S(1)}, s32[1,256]{1,0:T(1,128)}, u32[]{:S(2)}) copy-start(s32[1,256]{1,0:T(1,128)} %refs_4_.1) | copy-start | bytes 3076
  0.6 2.7 %copy-start.1 = (bf16[1,256,256]{2,1,0:T(8,128)(2,1)S(1)}, bf16[1,256,256]{2,1,0:T(8,128)(2,1)}, u32[]{:S(2)}) copy-start(bf16[1,256,256]{2,1,0:T(8,128)(2,1)} %param.8) | copy-start | bytes 393220
  0.7 2.6 %copy-start = (bf16[1,256,256]{2,1,0:T(8,128)(2,1)S(1)}, bf16[1,256,256]{2,1,0:T(8,128)(2,1)}, u32[]{:S(2)}) copy-start(bf16[1,256,256]{2,1,0:T(8,128)(2,1)} %param.7) | copy-start | bytes 393220
  2.7 16.6 %collective-permute-start.4 = (bf16[2,512,512]{2,1,0:T(8,128)(2,1)S(1)}, bf16[2,512,512]{2,1,0:T(8,128)(2,1)S(1)}, u32[]{:S(2)}, u32[]{:S(2)}) collective-permute-start(bf16[2,512,512]{2,1,0:T(8,128)(2,1)S(1)} %get-tuple-element.41), channel_id=1, source_target_pairs={{0,8},{8,0},{16,24},{24,16},{1,9},{9,1},{17,25},{25,17},{2,10},{10... | collective-permute-start | bytes 3145736 | tf_op jit(solution)/shard_map/ppermute | solution.py:277
  3.3 6.7 %collective-permute-start = (bf16[256,256]{1,0:T(8,128)(2,1)S(1)}, bf16[256,256]{1,0:T(8,128)(2,1)S(1)}, u32[]{:S(2)}, u32[]{:S(2)}) collective-permute-start(bf16[256,256]{1,0:T(8,128)(2,1)S(1)} %bitcast.13), channel_id=1, source_target_pairs={{0,8},{8,16},{16,24},{24,0},{1,9},{9,17},{17,25},{25,1},{2,10},{10... | collective-permute-start | bytes 393224 | tf_op jit(solution)/shard_map/ppermute | solution.py:270
  3.3 7.2 %collective-permute-start.2 = (bf16[256,256]{1,0:T(8,128)(2,1)S(1)}, bf16[256,256]{1,0:T(8,128)(2,1)S(1)}, u32[]{:S(2)}, u32[]{:S(2)}) collective-permute-start(bf16[256,256]{1,0:T(8,128)(2,1)S(1)} %bitcast.15), channel_id=1, source_target_pairs={{0,8},{8,16},{16,24},{24,0},{1,9},{9,17},{17,25},{25,1},{2,10},{10... | collective-permute-start | bytes 393224 | tf_op jit(solution)/shard_map/ppermute | solution.py:270
  6.0 4.0 %collective-permute-start.1 = (s32[1,256]{1,0:T(1,128)S(1)}, s32[1,256]{1,0:T(1,128)S(1)}, u32[]{:S(2)}, u32[]{:S(2)}) collective-permute-start(s32[1,256]{1,0:T(1,128)S(1)} %copy-done.2), channel_id=1, source_target_pairs={{0,8},{8,16},{16,24},{24,0},{1,9},{9,17},{17,25},{25,1},{2,10},{10... | collective-permute-start | bytes 3080 | tf_op jit(solution)/shard_map/ppermute | solution.py:270
  12.0 7.4 %collective-permute-start.5 = (bf16[256,256]{1,0:T(8,128)(2,1)S(1)}, bf16[256,256]{1,0:T(8,128)(2,1)S(1)}, u32[]{:S(2)}, u32[]{:S(2)}) collective-permute-start(bf16[256,256]{1,0:T(8,128)(2,1)S(1)} %get-tuple-element.35.mine), channel_id=1, source_target_pairs={{0,8},{8,0},{16,24},{24,16},{1,9},{9,1},{17,25},{25,17},{2,10},{10... | collective-permute-start | bytes 393224 | tf_op jit(solution)/shard_map/ppermute | solution.py:270
  12.0 4.5 %collective-permute-start.6 = (bf16[256,128]{1,0:T(8,128)(2,1)S(1)}, bf16[256,128]{1,0:T(8,128)(2,1)S(1)}, u32[]{:S(2)}, u32[]{:S(2)}) collective-permute-start(bf16[256,128]{1,0:T(8,128)(2,1)S(1)} %get-tuple-element.31.refs_0_), channel_id=1, source_target_pairs={{0,1},{1,0},{2,3},{3,2},{4,5},{5,4},{6,7},{7,6},{8,9},{9,8},{10,11... | collective-permute-start | bytes 196616 | tf_op jit(solution)/shard_map/ppermute | solution.py:309
  13.8 9.6 %collective-permute-start.3 = (bf16[2,256,256]{2,1,0:T(8,128)(2,1)S(1)}, bf16[2,256,256]{2,1,0:T(8,128)(2,1)S(1)}, u32[]{:S(2)}, u32[]{:S(2)}) collective-permute-start(bf16[2,256,256]{2,1,0:T(8,128)(2,1)S(1)} %get-tuple-element.37), channel_id=1, source_target_pairs={{0,24},{8,0},{16,8},{24,16},{1,25},{9,1},{17,9},{25,17},{2,26},{10... | collective-permute-start | bytes 786440 | tf_op jit(solution)/shard_map/ppermute | solution.py:270
  15.1 4.3 %collective-permute-start.8 = (bf16[256,128]{1,0:T(8,128)(2,1)S(1)}, bf16[256,128]{1,0:T(8,128)(2,1)S(1)}, u32[]{:S(2)}, u32[]{:S(2)}) collective-permute-start(bf16[256,128]{1,0:T(8,128)(2,1)S(1)} %get-tuple-element.33.refs_2_), channel_id=1, source_target_pairs={{0,1},{1,0},{2,3},{3,2},{4,5},{5,4},{6,7},{7,6},{8,9},{9,8},{10,11... | collective-permute-start | bytes 196616 | tf_op jit(solution)/shard_map/ppermute | solution.py:309
  16.5 3.2 %collective-permute-start.7 = (bf16[256,128]{1,0:T(8,128)(2,1)S(1)}, bf16[256,128]{1,0:T(8,128)(2,1)S(1)}, u32[]{:S(2)}, u32[]{:S(2)}) collective-permute-start(bf16[256,128]{1,0:T(8,128)(2,1)S(1)} %collective-permute-done.6.refs_0_), channel_id=1, source_target_pairs={{0,8},{8,0},{16,24},{24,16},{1,9},{9,1},{17,25},{25,17},{2,10},{10... | collective-permute-start | bytes 196616 | tf_op jit(solution)/shard_map/ppermute | solution.py:270
  19.3 1.6 %collective-permute-start.9 = (bf16[256,128]{1,0:T(8,128)(2,1)S(1)}, bf16[256,128]{1,0:T(8,128)(2,1)S(1)}, u32[]{:S(2)}, u32[]{:S(2)}) collective-permute-start(bf16[256,128]{1,0:T(8,128)(2,1)S(1)} %collective-permute-done.8.refs_2_.refs_0_), channel_id=1, source_target_pairs={{0,8},{8,0},{16,24},{24,16},{1,9},{9,1},{17,25},{25,17},{2,10},{10... | collective-permute-start | bytes 196616 | tf_op jit(solution)/shard_map/ppermute | solution.py:270
  20.0 6.4 %collective-permute-start.11 = (bf16[512,128]{1,0:T(8,128)(2,1)S(1)}, bf16[512,128]{1,0:T(8,128)(2,1)S(1)}, u32[]{:S(2)}, u32[]{:S(2)}) collective-permute-start(bf16[512,128]{1,0:T(8,128)(2,1)S(1)} %shard_map.102), channel_id=1, source_target_pairs={{0,16},{8,24},{16,0},{24,8},{1,17},{9,25},{17,1},{25,9},{2,18},{10... | collective-permute-start | bytes 393224 | tf_op jit(solution)/shard_map/ppermute | solution.py:270
  21.1 7.6 %collective-permute-start.10 = (bf16[512,128]{1,0:T(8,128)(2,1)S(1)}, bf16[512,128]{1,0:T(8,128)(2,1)S(1)}, u32[]{:S(2)}, u32[]{:S(2)}) collective-permute-start(bf16[512,128]{1,0:T(8,128)(2,1)S(1)} %shard_map.100), channel_id=1, source_target_pairs={{0,16},{8,24},{16,0},{24,8},{1,17},{9,25},{17,1},{25,9},{2,18},{10... | collective-permute-start | bytes 393224 | tf_op jit(solution)/shard_map/ppermute | solution.py:270

commit v7 on v6

--- a/solution.py
+++ b/solution.py
@@ -106,26 +106,31 @@
             ds[1, h, rows] = prior_part
 
 
-def terms_body(length, heads, size, q, g, prob, *refs):
+def values_body(length, heads, g, prob, own_out, back_out):
+    own = lower(length)
+    for h in range(heads):
+        at = head(h)
+        own_out[:, at] = dot(jnp.where(own, prob[h], 0.0).astype(BF16), g[:, at], 1, 0)
+        back_out[:, at] = dot(
+            jnp.where(own, 0.0, prob[h]).astype(BF16), g[:, at], 1, 0
+        ).astype(BF16)
+
+
+def keys_body(heads, size, q, *refs):
     own_out, back_out, dq_out = refs[-3:]
     pieces = [refs[i : i + 2] for i in range(0, len(refs) - 3, 2)]
-    own = lower(length)
     for c, (dq, _) in enumerate(pieces):
         dq_out[:, c * size * HD : (c + 1) * size * HD] = dq[...]
     for h in range(heads):
         at = head(h)
         ds = pieces[h // size][1]
-        own_out[0, :, at] = dot(ds[0, h % size], q[:, at], 0, 0)
-        back_out[0, :, at] = dot(ds[1, h % size], q[:, at], 0, 0).astype(BF16)
-        own_out[1, :, at] = dot(jnp.where(own, prob[h], 0.0).astype(BF16), g[:, at], 1, 0)
-        back_out[1, :, at] = dot(
-            jnp.where(own, 0.0, prob[h]).astype(BF16), g[:, at], 1, 0
-        ).astype(BF16)
-
-
-def join_body(own, later, dk, dv):
-    dk[...] = ((own[0] + later[0].astype(F32)) * HD ** (-0.5)).astype(BF16)
-    dv[...] = (own[1] + later[1].astype(F32)).astype(BF16)
+        own_out[:, at] = dot(ds[0, h % size], q[:, at], 0, 0)
+        back_out[:, at] = dot(ds[1, h % size], q[:, at], 0, 0).astype(BF16)
+
+
+def join_body(own_key, later_key, own_value, later_value, dk, dv):
+    dk[...] = ((own_key[...] + later_key[...].astype(F32)) * HD ** (-0.5)).astype(BF16)
+    dv[...] = (own_value[...] + later_value[...].astype(F32)).astype(BF16)
 
 
 def open_body(block, parts, *refs):
@@ -283,6 +288,9 @@
         functools.partial(prob_body, length, heads), (square, square, square),
         q, k, v, g, pk, segment, pseg,
     )
+    sums = (vmem((length, columns), F32), vmem((length, columns), BF16))
+    own_value, back_value = call(functools.partial(values_body, length, heads), sums, g, prob)
+    later_value = sent(back_value, back)
     found = []
     for c in range(chunks):
         found += call(
@@ -290,16 +298,12 @@
             (vmem((length, size * HD), BF16), vmem((2, size, length, length), BF16)),
             k, g, pk, pv, turned_prob, own_grad,
         )
-    own, to_prior, dq = call(
-        functools.partial(terms_body, length, heads, size),
-        (
-            vmem((2, length, columns), F32),
-            vmem((2, length, columns), BF16),
-            vmem((length, columns), BF16),
-        ),
-        q, g, prob, *found,
-    )
-    later = sent(to_prior, back)
+    own_key, back_key, dq = call(
+        functools.partial(keys_body, heads, size),
+        (*sums, vmem((length, columns), BF16)),
+        q, *found,
+    )
+    later_key = sent(back_key, back)
     peer = sent(dq, other)
     grads = []
     for c in range(chunks):
@@ -325,7 +329,7 @@
                 given, begun, *grads[c][1::2],
             )
             arrived[c].append(sent(piece, ring))
-    dk, dv = call(join_body, (shape((length, columns), BF16),) * 2, own, later)
+    dk, dv = call(join_body, (shape((length, columns), BF16),) * 2, own_key, later_key, own_value, later_value)
     kept = call(
         functools.partial(panel_body, wide_count, length),
         vmem((block, columns), F32),

time: 29.6 us -> 31.3 us (1.057)
  waiting for transfers between devices: 10.5 us -> 11.6 us
  starting transfers between devices: 9.47 us -> 9.85 us
    ppermute x9 -> x10, waiting for transfers between devices: 6.79 us -> 7.72 us  [sent(): return lax.ppermute(value, 'ctx', pairs)]
    ppermute x9 -> x10, starting transfers between devices: 6.64 us -> 7.2 us  [sent(): return lax.ppermute(value, 'ctx', pairs)]
    pallas_call x10 -> x11, Pallas kernels: 4.58 us -> 4.72 us  [call(): pl.pallas_call(body, out_shape=outs, in_specs=[whole] * len(args), out_sp...]
  transfers between devices with their start and end apart: 12 -> 13, of which waited for: 5 -> 6; matrix products, arithmetic and copies ran while one was open for 2% -> 2% of each run, Pallas kernels for 18% -> 18%
where the time goes in v7:
time: 31.3 us; the launch traced here: 31.1 us
  waiting for transfers between devices  11.6 us (37%)
  starting transfers between devices  9.85 us (31%)
  Pallas kernels  8.2 us (26%)
  between operations  0.76 us (2%)
  local copies, waits for them, and re-layouts  0.67 us (2%)
    ppermute x10, waiting for transfers between devices, sent(): return lax.ppermute(value, 'ctx', pairs)  7.72 us
    ppermute x10, starting transfers between devices, sent(): return lax.ppermute(value, 'ctx', pairs)  7.2 us
    pallas_call x11, Pallas kernels, call(): pl.pallas_call(body, out_shape=outs, in_specs=[whole] * len(args), out_sp...  4.72 us
    ppermute x2, waiting for transfers between devices, shards(): piece = lax.ppermute(found[2 * c], 'wide', ring)  3.91 us
    ppermute x2, starting transfers between devices, shards(): piece = lax.ppermute(found[2 * c], 'wide', ring)  2.09 us
    pallas_call x1, Pallas kernels, open_all(): pl.pallas_call(functools.partial(open_body, block, parts), out_shape=tupl...  2.03 us
    pallas_call x2, Pallas kernels, add(): pl.pallas_call(functools.partial(add_body, first), grid=(1,), out_shape=s...  1.45 us
    unnamed x7, local copies, waits for them, and re-layouts  0.67 us
  transfers between devices with their start and end apart: 13, of which 6 were waited for; matrix products, arithmetic and copies ran while one was open for 2% of the time, Pallas kernels for 18%

profile of v7, /device:TPU:0, one launch (start us, length us, event | category | flops | bytes accessed | tf_op | source)
XLA Modules:
  0.0 31.1 jit_solution(4517556455100723388)
XLA Ops:
  0.7 2.0 %open.1 = (bf16[256,256]{1,0:T(8,128)(2,1)S(1)}, bf16[256,256]{1,0:T(8,128)(2,1)S(1)}, bf16[256,256]{1,0:T(8,128)(2,1)S(1)}, bf16[256,256]{1,0:T(8,128)(2,1)S(1)...) custom-call(bf16[256,256]{1,0:T(8,128)(2,1)} %bitcast.10, ...), custom_call_target="tpu_custom_call" | custom-call | flops 1048576 | bytes 4194304 | tf_op jit(solution)/shard_map/open/pallas_call | solution.py:172
  2.7 0.6 %collective-permute-start.5 = (bf16[2,512,512]{2,1,0:T(8,128)(2,1)S(1)}, bf16[2,512,512]{2,1,0:T(8,128)(2,1)S(1)}, u32[]{:S(2)}, u32[]{:S(2)}) collective-permute-start(bf16[2,512,512]{2,1,0:T(8,128)(2,1)S(1)} %get-tuple-element.45), channel_id=1, source_target_pairs={{0,8},{8,0},{16,24},{24,16},{1,9},{9,1},{17,25},{25,17},{2,10},{10... | collective-permute-start | bytes 3145736 | tf_op jit(solution)/shard_map/ppermute | solution.py:282
  3.3 2.6 %collective-permute-start.1 = (bf16[256,256]{1,0:T(8,128)(2,1)S(1)}, bf16[256,256]{1,0:T(8,128)(2,1)S(1)}, u32[]{:S(2)}, u32[]{:S(2)}) collective-permute-start(bf16[256,256]{1,0:T(8,128)(2,1)S(1)} %bitcast.15), channel_id=1, source_target_pairs={{0,8},{8,16},{16,24},{24,0},{1,9},{9,17},{17,25},{25,1},{2,10},{10... | collective-permute-start | bytes 393224 | tf_op jit(solution)/shard_map/ppermute | solution.py:275
  6.0 0.4 %collective-permute-start.2 = (s32[1,256]{1,0:T(1,128)S(1)}, s32[1,256]{1,0:T(1,128)S(1)}, u32[]{:S(2)}, u32[]{:S(2)}) collective-permute-start(s32[1,256]{1,0:T(1,128)S(1)} %copy-done.2), channel_id=1, source_target_pairs={{0,8},{8,16},{16,24},{24,0},{1,9},{9,17},{17,25},{25,1},{2,10},{10... | collective-permute-start | bytes 3080 | tf_op jit(solution)/shard_map/ppermute | solution.py:275
  6.4 3.6 %collective-permute-done.2.pseg = s32[1,256]{1,0:T(1,128)S(1)} collective-permute-done((s32[1,256]{1,0:T(1,128)S(1)}, s32[1,256]{1,0:T(1,128)S(1)}, u32[]{:S(2)}, u32[]{:S(2)}) %collective-permute-start.2) | collective-permute-done | bytes 1056 | tf_op jit(solution)/shard_map/ppermute | solution.py:275
  10.0 0.6 %shard_map.93 = (f32[2,256,256]{2,1,0:T(8,128)S(1)}, f32[2,256,256]{2,1,0:T(8,128)S(1)}, f32[2,256,256]{2,1,0:T(8,128)S(1)}) custom-call(bf16[256,256]{1,0:T(8,128)(2,1)S(1)} %get-tuple-element.25.q, bf16[256,256]{1,0:T(8,128)(2,1)S(1)} %get-tuple-element.26.k, bf16[256,256]{1,0:T(8,128)(2,1)S(1)} %get-tuple-element.28.v, ...), custom_call_target="tpu_custom_call" | custom-call | flops 1048576 | bytes 1048576 | tf_op jit(solution)/shard_map/pallas_call | solution.py:29
  10.6 0.4 %shard_map.95 = (bf16[256,128]{1,0:T(8,128)(2,1)S(1)}, bf16[2,1,256,256]{3,2,1,0:T(8,128)(2,1)S(1)}) custom-call(bf16[256,256]{1,0:T(8,128)(2,1)S(1)} %get-tuple-element.26.k, bf16[256,256]{1,0:T(8,128)(2,1)S(1)} %get-tuple-element.27.g, bf16[256,256]{1,0:T(8,128)(2,1)S(1)} %collective-permute-done.pk, bf16[256,256]{1,0:T(8,128)(2,1)S(1)} %collective-permute-done.1.pv, ...), custom_call_target="tpu_custom_call" | custom-call | flops 1048576 | bytes 1048576 | tf_op jit(solution)/shard_map/pallas_call | solution.py:29
  11.0 0.4 %shard_map.94 = (bf16[256,128]{1,0:T(8,128)(2,1)S(1)}, bf16[2,1,256,256]{3,2,1,0:T(8,128)(2,1)S(1)}) custom-call(bf16[256,256]{1,0:T(8,128)(2,1)S(1)} %get-tuple-element.26.k, bf16[256,256]{1,0:T(8,128)(2,1)S(1)} %get-tuple-element.27.g, bf16[256,256]{1,0:T(8,128)(2,1)S(1)} %collective-permute-done.pk, bf16[256,256]{1,0:T(8,128)(2,1)S(1)} %collective-permute-done.1.pv, ...), custom_call_target="tpu_custom_call" | custom-call | flops 1048576 | bytes 1048576 | tf_op jit(solution)/shard_map/pallas_call | solution.py:29
  11.9 1.7 %collective-permute-start.7 = (bf16[256,128]{1,0:T(8,128)(2,1)S(1)}, bf16[256,128]{1,0:T(8,128)(2,1)S(1)}, u32[]{:S(2)}, u32[]{:S(2)}) collective-permute-start(bf16[256,128]{1,0:T(8,128)(2,1)S(1)} %get-tuple-element.32.refs_0_), channel_id=1, source_target_pairs={{0,1},{1,0},{2,3},{3,2},{4,5},{5,4},{6,7},{7,6},{8,9},{9,8},{10,11... | collective-permute-start | bytes 196616 | tf_op jit(solution)/shard_map/ppermute | solution.py:313
  14.0 2.4 %collective-permute-done.7.refs_0_ = bf16[256,128]{1,0:T(8,128)(2,1)S(1)} collective-permute-done((bf16[256,128]{1,0:T(8,128)(2,1)S(1)}, bf16[256,128]{1,0:T(8,128)(2,1)S(1)}, u32[]{:S(2)}, u32[]{:S(2)}) %collective-permute-start.7) | collective-permute-done | bytes 65568 | tf_op jit(solution)/shard_map/ppermute | solution.py:313
  16.4 1.5 %collective-permute-done.9.refs_2_.refs_0_ = bf16[256,128]{1,0:T(8,128)(2,1)S(1)} collective-permute-done((bf16[256,128]{1,0:T(8,128)(2,1)S(1)}, bf16[256,128]{1,0:T(8,128)(2,1)S(1)}, u32[]{:S(2)}, u32[]{:S(2)}) %collective-permute-start.9) | collective-permute-done | bytes 65568 | tf_op jit(solution)/shard_map/ppermute | solution.py:313
  18.2 1.8 %collective-permute-start.4 = (bf16[256,256]{1,0:T(8,128)(2,1)S(1)}, bf16[256,256]{1,0:T(8,128)(2,1)S(1)}, u32[]{:S(2)}, u32[]{:S(2)}) collective-permute-start(bf16[256,256]{1,0:T(8,128)(2,1)S(1)} %get-tuple-element.41), channel_id=1, source_target_pairs={{0,24},{8,0},{16,8},{24,16},{1,25},{9,1},{17,9},{25,17},{2,26},{10... | collective-permute-start | bytes 393224 | tf_op jit(solution)/shard_map/ppermute | solution.py:275
  20.1 0.4 %shard_map.102.begun = f32[512,128]{1,0:T(8,128)S(1)} custom-call(bf16[2,512,512]{2,1,0:T(8,128)(2,1)S(1)} %get-tuple-element.44.mine_frames, bf16[2,512,512]{2,1,0:T(8,128)(2,1)S(1)} %collective-permute-done.5.peer_frames, bf16[256,256]{1,0:T(8,128)(2,1)S(1)} %get-tuple-element.36.mine, bf16[256,256]{1,0:T(8,128)(2,1)S(1)} %collective-permute-done.6.peer, ...), custom_call_target="tpu_custom_call" | custom-call | flops 1048576 | bytes 1048576 | tf_op jit(solution)/shard_map/pallas_call | solution.py:29
  20.7 0.5 %collective-permute-start.12 = (bf16[512,128]{1,0:T(8,128)(2,1)S(1)}, bf16[512,128]{1,0:T(8,128)(2,1)S(1)}, u32[]{:S(2)}, u32[]{:S(2)}) collective-permute-start(bf16[512,128]{1,0:T(8,128)(2,1)S(1)} %shard_map.103), channel_id=1, source_target_pairs={{0,16},{8,24},{16,0},{24,8},{1,17},{9,25},{17,1},{25,9},{2,18},{10... | collective-permute-start | bytes 393224 | tf_op jit(solution)/shard_map/ppermute | solution.py:275
  21.2 0.4 %shard_map.100.begun = f32[512,128]{1,0:T(8,128)S(1)} custom-call(bf16[2,512,512]{2,1,0:T(8,128)(2,1)S(1)} %get-tuple-element.44.mine_frames, bf16[2,512,512]{2,1,0:T(8,128)(2,1)S(1)} %collective-permute-done.5.peer_frames, bf16[256,256]{1,0:T(8,128)(2,1)S(1)} %get-tuple-element.36.mine, bf16[256,256]{1,0:T(8,128)(2,1)S(1)} %collective-permute-done.6.peer, ...), custom_call_target="tpu_custom_call" | custom-call | flops 1048576 | bytes 1048576 | tf_op jit(solution)/shard_map/pallas_call | solution.py:29
  21.8 1.7 %collective-permute-start.11 = (bf16[512,128]{1,0:T(8,128)(2,1)S(1)}, bf16[512,128]{1,0:T(8,128)(2,1)S(1)}, u32[]{:S(2)}, u32[]{:S(2)}) collective-permute-start(bf16[512,128]{1,0:T(8,128)(2,1)S(1)} %shard_map.101), channel_id=1, source_target_pairs={{0,16},{8,24},{16,0},{24,8},{1,17},{9,25},{17,1},{25,9},{2,18},{10... | collective-permute-start | bytes 393224 | tf_op jit(solution)/shard_map/ppermute | solution.py:275
  23.4 0.7 %copy.12 = bf16[1,256,256]{2,1,0:T(8,128)(2,1)} copy(bf16[1,256,256]{2,1,0:T(8,128)(2,1)S(1)} %bitcast.8) | data formatting | bytes 262144
  24.1 1.9 %collective-permute-done.3.later_key = bf16[256,256]{1,0:T(8,128)(2,1)S(1)} collective-permute-done((bf16[256,256]{1,0:T(8,128)(2,1)S(1)}, bf16[256,256]{1,0:T(8,128)(2,1)S(1)}, u32[]{:S(2)}, u32[]{:S(2)}) %collective-permute-start.3) | collective-permute-done | bytes 131104 | tf_op jit(solution)/shard_map/ppermute | solution.py:275
  26.0 0.7 %shard_map.98 = (bf16[256,256]{1,0:T(8,128)(2,1)}, bf16[256,256]{1,0:T(8,128)(2,1)}) custom-call(f32[256,256]{1,0:T(8,128)S(1)} %get-tuple-element.37.own_key, bf16[256,256]{1,0:T(8,128)(2,1)S(1)} %collective-permute-done.3.later_key, f32[256,256]{1,0:T(8,128)S(1)} %get-tuple-element.40.own_value, bf16[256,256]{1,0:T(8,128)(2,1)S(1)} %collective-permute-done.4.later_value), custom_call_target="tpu_custom_call" | custom-call | flops 1048576 | bytes 1048576 | tf_op jit(solution)/shard_map/pallas_call | solution.py:29
  26.7 0.7 %shard_map.99.refs_0_ = f32[512,256]{1,0:T(8,128)S(1)} custom-call(bf16[2,512,512]{2,1,0:T(8,128)(2,1)S(1)} %get-tuple-element.44.mine_frames, bf16[2,512,512]{2,1,0:T(8,128)(2,1)S(1)} %collective-permute-done.5.peer_frames, bf16[256,256]{1,0:T(8,128)(2,1)S(1)} %get-tuple-element.36.mine, bf16[256,256]{1,0:T(8,128)(2,1)S(1)} %collective-permute-done.6.peer, ...), custom_call_target="tpu_custom_call" | custom-call | flops 1048576 | bytes 1048576 | tf_op jit(solution)/shard_map/pallas_call | solution.py:29
  27.5 1.1 %collective-permute-done.12.refs_1_ = bf16[512,128]{1,0:T(8,128)(2,1)S(1)} collective-permute-done((bf16[512,128]{1,0:T(8,128)(2,1)S(1)}, bf16[512,128]{1,0:T(8,128)(2,1)S(1)}, u32[]{:S(2)}, u32[]{:S(2)}) %collective-permute-start.12) | collective-permute-done | bytes 131104 | tf_op jit(solution)/shard_map/ppermute | solution.py:275
  28.6 0.7 %shard_map.104.refs_2_ = f32[512,256]{1,0:T(8,128)} custom-call(f32[512,256]{1,0:T(8,128)S(1)} %shard_map.99.refs_0_, bf16[512,128]{1,0:T(8,128)(2,1)S(1)} %collective-permute-done.12.refs_1_), custom_call_target="tpu_custom_call" | custom-call | flops 1048576 | bytes 1048576 | tf_op jit(solution)/shard_map/pallas_call | solution.py:248
  29.3 1.1 %collective-permute-done.11.refs_1_ = bf16[512,128]{1,0:T(8,128)(2,1)S(1)} collective-permute-done((bf16[512,128]{1,0:T(8,128)(2,1)S(1)}, bf16[512,128]{1,0:T(8,128)(2,1)S(1)}, u32[]{:S(2)}, u32[]{:S(2)}) %collective-permute-start.11) | collective-permute-done | bytes 131104 | tf_op jit(solution)/shard_map/ppermute | solution.py:275
  30.4 0.7 %shard_map.105 = f32[512,256]{1,0:T(8,128)} custom-call(f32[512,256]{1,0:T(8,128)S(1)} %shard_map.99.refs_0_, bf16[512,128]{1,0:T(8,128)(2,1)S(1)} %collective-permute-done.11.refs_1_, f32[512,256]{1,0:T(8,128)} %shard_map.104.refs_2_), custom_call_target="tpu_custom_call", output_to_operand_aliasing={{}: (2, {})} | custom-call | flops 1048576 | bytes 1048576 | tf_op jit(solution)/shard_map/pallas_call | solution.py:248
  (23 shorter events, 1.7 us)
Async XLA Ops:
  0.6 5.3 %copy-start.2 = (s32[1,256]{1,0:T(1,128)S(1)}, s32[1,256]{1,0:T(1,128)}, u32[]{:S(2)}) copy-start(s32[1,256]{1,0:T(1,128)} %refs_4_.1) | copy-start | bytes 3076
  0.6 2.7 %copy-start.1 = (bf16[1,256,256]{2,1,0:T(8,128)(2,1)S(1)}, bf16[1,256,256]{2,1,0:T(8,128)(2,1)}, u32[]{:S(2)}) copy-start(bf16[1,256,256]{2,1,0:T(8,128)(2,1)} %param.8) | copy-start | bytes 393220
  0.7 2.6 %copy-start = (bf16[1,256,256]{2,1,0:T(8,128)(2,1)S(1)}, bf16[1,256,256]{2,1,0:T(8,128)(2,1)}, u32[]{:S(2)}) copy-start(bf16[1,256,256]{2,1,0:T(8,128)(2,1)} %param.7) | copy-start | bytes 393220
  2.7 17.4 %collective-permute-start.5 = (bf16[2,512,512]{2,1,0:T(8,128)(2,1)S(1)}, bf16[2,512,512]{2,1,0:T(8,128)(2,1)S(1)}, u32[]{:S(2)}, u32[]{:S(2)}) collective-permute-start(bf16[2,512,512]{2,1,0:T(8,128)(2,1)S(1)} %get-tuple-element.45), channel_id=1, source_target_pairs={{0,8},{8,0},{16,24},{24,16},{1,9},{9,1},{17,25},{25,17},{2,10},{10... | collective-permute-start | bytes 3145736 | tf_op jit(solution)/shard_map/ppermute | solution.py:282
  3.3 6.7 %collective-permute-start = (bf16[256,256]{1,0:T(8,128)(2,1)S(1)}, bf16[256,256]{1,0:T(8,128)(2,1)S(1)}, u32[]{:S(2)}, u32[]{:S(2)}) collective-permute-start(bf16[256,256]{1,0:T(8,128)(2,1)S(1)} %bitcast.13), channel_id=1, source_target_pairs={{0,8},{8,16},{16,24},{24,0},{1,9},{9,17},{17,25},{25,1},{2,10},{10... | collective-permute-start | bytes 393224 | tf_op jit(solution)/shard_map/ppermute | solution.py:275
  3.3 7.3 %collective-permute-start.1 = (bf16[256,256]{1,0:T(8,128)(2,1)S(1)}, bf16[256,256]{1,0:T(8,128)(2,1)S(1)}, u32[]{:S(2)}, u32[]{:S(2)}) collective-permute-start(bf16[256,256]{1,0:T(8,128)(2,1)S(1)} %bitcast.15), channel_id=1, source_target_pairs={{0,8},{8,16},{16,24},{24,0},{1,9},{9,17},{17,25},{25,1},{2,10},{10... | collective-permute-start | bytes 393224 | tf_op jit(solution)/shard_map/ppermute | solution.py:275
  6.0 4.0 %collective-permute-start.2 = (s32[1,256]{1,0:T(1,128)S(1)}, s32[1,256]{1,0:T(1,128)S(1)}, u32[]{:S(2)}, u32[]{:S(2)}) collective-permute-start(s32[1,256]{1,0:T(1,128)S(1)} %copy-done.2), channel_id=1, source_target_pairs={{0,8},{8,16},{16,24},{24,0},{1,9},{9,17},{17,25},{25,1},{2,10},{10... | collective-permute-start | bytes 3080 | tf_op jit(solution)/shard_map/ppermute | solution.py:275
  11.8 8.1 %collective-permute-start.6 = (bf16[256,256]{1,0:T(8,128)(2,1)S(1)}, bf16[256,256]{1,0:T(8,128)(2,1)S(1)}, u32[]{:S(2)}, u32[]{:S(2)}) collective-permute-start(bf16[256,256]{1,0:T(8,128)(2,1)S(1)} %get-tuple-element.36.mine), channel_id=1, source_target_pairs={{0,8},{8,0},{16,24},{24,16},{1,9},{9,1},{17,25},{25,17},{2,10},{10... | collective-permute-start | bytes 393224 | tf_op jit(solution)/shard_map/ppermute | solution.py:275
  11.9 4.5 %collective-permute-start.7 = (bf16[256,128]{1,0:T(8,128)(2,1)S(1)}, bf16[256,128]{1,0:T(8,128)(2,1)S(1)}, u32[]{:S(2)}, u32[]{:S(2)}) collective-permute-start(bf16[256,128]{1,0:T(8,128)(2,1)S(1)} %get-tuple-element.32.refs_0_), channel_id=1, source_target_pairs={{0,1},{1,0},{2,3},{3,2},{4,5},{5,4},{6,7},{7,6},{8,9},{9,8},{10,11... | collective-permute-start | bytes 196616 | tf_op jit(solution)/shard_map/ppermute | solution.py:313
  13.7 4.3 %collective-permute-start.9 = (bf16[256,128]{1,0:T(8,128)(2,1)S(1)}, bf16[256,128]{1,0:T(8,128)(2,1)S(1)}, u32[]{:S(2)}, u32[]{:S(2)}) collective-permute-start(bf16[256,128]{1,0:T(8,128)(2,1)S(1)} %get-tuple-element.34.refs_2_), channel_id=1, source_target_pairs={{0,1},{1,0},{2,3},{3,2},{4,5},{5,4},{6,7},{7,6},{8,9},{9,8},{10,11... | collective-permute-start | bytes 196616 | tf_op jit(solution)/shard_map/ppermute | solution.py:313
  16.4 4.0 %collective-permute-start.8 = (bf16[256,128]{1,0:T(8,128)(2,1)S(1)}, bf16[256,128]{1,0:T(8,128)(2,1)S(1)}, u32[]{:S(2)}, u32[]{:S(2)}) collective-permute-start(bf16[256,128]{1,0:T(8,128)(2,1)S(1)} %collective-permute-done.7.refs_0_), channel_id=1, source_target_pairs={{0,8},{8,0},{16,24},{24,16},{1,9},{9,1},{17,25},{25,17},{2,10},{10... | collective-permute-start | bytes 196616 | tf_op jit(solution)/shard_map/ppermute | solution.py:275
  17.9 3.6 %collective-permute-start.10 = (bf16[256,128]{1,0:T(8,128)(2,1)S(1)}, bf16[256,128]{1,0:T(8,128)(2,1)S(1)}, u32[]{:S(2)}, u32[]{:S(2)}) collective-permute-start(bf16[256,128]{1,0:T(8,128)(2,1)S(1)} %collective-permute-done.9.refs_2_.refs_0_), channel_id=1, source_target_pairs={{0,8},{8,0},{16,24},{24,16},{1,9},{9,1},{17,25},{25,17},{2,10},{10... | collective-permute-start | bytes 196616 | tf_op jit(solution)/shard_map/ppermute | solution.py:275
  18.2 5.9 %collective-permute-start.4 = (bf16[256,256]{1,0:T(8,128)(2,1)S(1)}, bf16[256,256]{1,0:T(8,128)(2,1)S(1)}, u32[]{:S(2)}, u32[]{:S(2)}) collective-permute-start(bf16[256,256]{1,0:T(8,128)(2,1)S(1)} %get-tuple-element.41), channel_id=1, source_target_pairs={{0,24},{8,0},{16,8},{24,16},{1,25},{9,1},{17,9},{25,17},{2,26},{10... | collective-permute-start | bytes 393224 | tf_op jit(solution)/shard_map/ppermute | solution.py:275
  20.0 6.0 %collective-permute-start.3 = (bf16[256,256]{1,0:T(8,128)(2,1)S(1)}, bf16[256,256]{1,0:T(8,128)(2,1)S(1)}, u32[]{:S(2)}, u32[]{:S(2)}) collective-permute-start(bf16[256,256]{1,0:T(8,128)(2,1)S(1)} %get-tuple-element.38), channel_id=1, source_target_pairs={{0,24},{8,0},{16,8},{24,16},{1,25},{9,1},{17,9},{25,17},{2,26},{10... | collective-permute-start | bytes 393224 | tf_op jit(solution)/shard_map/ppermute | solution.py:275
  20.7 7.9 %collective-permute-start.12 = (bf16[512,128]{1,0:T(8,128)(2,1)S(1)}, bf16[512,128]{1,0:T(8,128)(2,1)S(1)}, u32[]{:S(2)}, u32[]{:S(2)}) collective-permute-start(bf16[512,128]{1,0:T(8,128)(2,1)S(1)} %shard_map.103), channel_id=1, source_target_pairs={{0,16},{8,24},{16,0},{24,8},{1,17},{9,25},{17,1},{25,9},{2,18},{10... | collective-permute-start | bytes 393224 | tf_op jit(solution)/shard_map/ppermute | solution.py:275
  21.8 8.6 %collective-permute-start.11 = (bf16[512,128]{1,0:T(8,128)(2,1)S(1)}, bf16[512,128]{1,0:T(8,128)(2,1)S(1)}, u32[]{:S(2)}, u32[]{:S(2)}) collective-permute-start(bf16[512,128]{1,0:T(8,128)(2,1)S(1)} %shard_map.101), channel_id=1, source_target_pairs={{0,16},{8,24},{16,0},{24,8},{1,17},{9,25},{17,1},{25,9},{2,18},{10... | collective-permute-start | bytes 393224 | tf_op jit(solution)/shard_map/ppermute | solution.py:275

commit v8 on v7

--- a/solution.py
+++ b/solution.py
@@ -235,9 +235,11 @@
 
 def add_body(first, *refs):
     refs, out = (refs[:-1] if first == 0 else refs[:-2]), refs[-1]
-    total = refs[0][:, first : first + out.shape[1]]
+    size = out.shape[0]
+    rows = pl.ds(pl.multiple_of(pl.program_id(0) * size, 8), size)
+    total = refs[0][rows, first : first + out.shape[1]]
     for ref in refs[1:]:
-        total = total + ref[...].astype(F32)
+        total = total + ref[rows].astype(F32)
     out[...] = total
 
 
@@ -247,10 +249,10 @@
     args = [pltpu.with_memory_space_constraint(a, pltpu.VMEM) for a in (kept, *arrived)]
     return pl.pallas_call(
         functools.partial(add_body, first),
-        grid=(1,),
+        grid=(2,),
         out_shape=shape(kept.shape, F32),
         in_specs=[whole] * len(args) + [pl.BlockSpec(memory_space=pl.ANY)] * len(held),
-        out_specs=pl.BlockSpec((rows, columns), lambda i: (0, first // columns)),
+        out_specs=pl.BlockSpec((rows // 2, columns), lambda i: (i, first // columns)),
         input_output_aliases={len(args): 0} if held else {},
         cost_estimate=pl.CostEstimate(flops=1 << 20, bytes_accessed=1 << 20, transcendentals=0),
         compiler_params=pltpu.CompilerParams(vmem_limit_bytes=24 << 20),

time: 31.3 us -> 31.2 us (level)
  transfers between devices with their start and end apart: 13 -> 13, of which waited for: 6 -> 6; matrix products, arithmetic and copies ran while one was open for 2% -> 2% of each run, Pallas kernels for 18% -> 17%
where the time goes in v8:
time: 31.2 us; the launch traced here: 31.1 us
  waiting for transfers between devices  11.6 us (37%)
  starting transfers between devices  9.85 us (32%)
  Pallas kernels  8.17 us (26%)
  between operations  0.76 us (2%)
  local copies, waits for them, and re-layouts  0.67 us (2%)
    ppermute x10, waiting for transfers between devices, sent(): return lax.ppermute(value, 'ctx', pairs)  7.73 us
    ppermute x10, starting transfers between devices, sent(): return lax.ppermute(value, 'ctx', pairs)  7.2 us
    pallas_call x11, Pallas kernels, call(): pl.pallas_call(body, out_shape=outs, in_specs=[whole] * len(args), out_sp...  4.72 us
    ppermute x2, waiting for transfers between devices, shards(): piece = lax.ppermute(found[2 * c], 'wide', ring)  3.91 us
    ppermute x2, starting transfers between devices, shards(): piece = lax.ppermute(found[2 * c], 'wide', ring)  2.09 us
    pallas_call x1, Pallas kernels, open_all(): pl.pallas_call(functools.partial(open_body, block, parts), out_shape=tupl...  2.03 us
    pallas_call x2, Pallas kernels, add(): pl.pallas_call(functools.partial(add_body, first), grid=(2,), out_shape=s...  1.42 us
    unnamed x7, local copies, waits for them, and re-layouts  0.67 us
  transfers between devices with their start and end apart: 13, of which 6 were waited for; matrix products, arithmetic and copies ran while one was open for 2% of the time, Pallas kernels for 17%

profile of v8, /device:TPU:0, one launch (start us, length us, event | category | flops | bytes accessed | tf_op | source)
XLA Modules:
  0.0 31.1 jit_solution(3136751761598881169)
XLA Ops:
  0.7 2.0 %open.1 = (bf16[256,256]{1,0:T(8,128)(2,1)S(1)}, bf16[256,256]{1,0:T(8,128)(2,1)S(1)}, bf16[256,256]{1,0:T(8,128)(2,1)S(1)}, bf16[256,256]{1,0:T(8,128)(2,1)S(1)...) custom-call(bf16[256,256]{1,0:T(8,128)(2,1)} %bitcast.10, ...), custom_call_target="tpu_custom_call" | custom-call | flops 1048576 | bytes 4194304 | tf_op jit(solution)/shard_map/open/pallas_call | solution.py:172
  2.7 0.6 %collective-permute-start.5 = (bf16[2,512,512]{2,1,0:T(8,128)(2,1)S(1)}, bf16[2,512,512]{2,1,0:T(8,128)(2,1)S(1)}, u32[]{:S(2)}, u32[]{:S(2)}) collective-permute-start(bf16[2,512,512]{2,1,0:T(8,128)(2,1)S(1)} %get-tuple-element.45), channel_id=1, source_target_pairs={{0,8},{8,0},{16,24},{24,16},{1,9},{9,1},{17,25},{25,17},{2,10},{10... | collective-permute-start | bytes 3145736 | tf_op jit(solution)/shard_map/ppermute | solution.py:284
  3.3 2.6 %collective-permute-start.1 = (bf16[256,256]{1,0:T(8,128)(2,1)S(1)}, bf16[256,256]{1,0:T(8,128)(2,1)S(1)}, u32[]{:S(2)}, u32[]{:S(2)}) collective-permute-start(bf16[256,256]{1,0:T(8,128)(2,1)S(1)} %bitcast.15), channel_id=1, source_target_pairs={{0,8},{8,16},{16,24},{24,0},{1,9},{9,17},{17,25},{25,1},{2,10},{10... | collective-permute-start | bytes 393224 | tf_op jit(solution)/shard_map/ppermute | solution.py:277
  6.0 0.4 %collective-permute-start.2 = (s32[1,256]{1,0:T(1,128)S(1)}, s32[1,256]{1,0:T(1,128)S(1)}, u32[]{:S(2)}, u32[]{:S(2)}) collective-permute-start(s32[1,256]{1,0:T(1,128)S(1)} %copy-done.2), channel_id=1, source_target_pairs={{0,8},{8,16},{16,24},{24,0},{1,9},{9,17},{17,25},{25,1},{2,10},{10... | collective-permute-start | bytes 3080 | tf_op jit(solution)/shard_map/ppermute | solution.py:277
  6.4 3.6 %collective-permute-done.2.pseg = s32[1,256]{1,0:T(1,128)S(1)} collective-permute-done((s32[1,256]{1,0:T(1,128)S(1)}, s32[1,256]{1,0:T(1,128)S(1)}, u32[]{:S(2)}, u32[]{:S(2)}) %collective-permute-start.2) | collective-permute-done | bytes 1056 | tf_op jit(solution)/shard_map/ppermute | solution.py:277
  10.0 0.6 %shard_map.93 = (f32[2,256,256]{2,1,0:T(8,128)S(1)}, f32[2,256,256]{2,1,0:T(8,128)S(1)}, f32[2,256,256]{2,1,0:T(8,128)S(1)}) custom-call(bf16[256,256]{1,0:T(8,128)(2,1)S(1)} %get-tuple-element.25.q, bf16[256,256]{1,0:T(8,128)(2,1)S(1)} %get-tuple-element.26.k, bf16[256,256]{1,0:T(8,128)(2,1)S(1)} %get-tuple-element.28.v, ...), custom_call_target="tpu_custom_call" | custom-call | flops 1048576 | bytes 1048576 | tf_op jit(solution)/shard_map/pallas_call | solution.py:29
  10.6 0.4 %shard_map.95 = (bf16[256,128]{1,0:T(8,128)(2,1)S(1)}, bf16[2,1,256,256]{3,2,1,0:T(8,128)(2,1)S(1)}) custom-call(bf16[256,256]{1,0:T(8,128)(2,1)S(1)} %get-tuple-element.26.k, bf16[256,256]{1,0:T(8,128)(2,1)S(1)} %get-tuple-element.27.g, bf16[256,256]{1,0:T(8,128)(2,1)S(1)} %collective-permute-done.pk, bf16[256,256]{1,0:T(8,128)(2,1)S(1)} %collective-permute-done.1.pv, ...), custom_call_target="tpu_custom_call" | custom-call | flops 1048576 | bytes 1048576 | tf_op jit(solution)/shard_map/pallas_call | solution.py:29
  11.0 0.4 %shard_map.94 = (bf16[256,128]{1,0:T(8,128)(2,1)S(1)}, bf16[2,1,256,256]{3,2,1,0:T(8,128)(2,1)S(1)}) custom-call(bf16[256,256]{1,0:T(8,128)(2,1)S(1)} %get-tuple-element.26.k, bf16[256,256]{1,0:T(8,128)(2,1)S(1)} %get-tuple-element.27.g, bf16[256,256]{1,0:T(8,128)(2,1)S(1)} %collective-permute-done.pk, bf16[256,256]{1,0:T(8,128)(2,1)S(1)} %collective-permute-done.1.pv, ...), custom_call_target="tpu_custom_call" | custom-call | flops 1048576 | bytes 1048576 | tf_op jit(solution)/shard_map/pallas_call | solution.py:29
  11.9 1.7 %collective-permute-start.7 = (bf16[256,128]{1,0:T(8,128)(2,1)S(1)}, bf16[256,128]{1,0:T(8,128)(2,1)S(1)}, u32[]{:S(2)}, u32[]{:S(2)}) collective-permute-start(bf16[256,128]{1,0:T(8,128)(2,1)S(1)} %get-tuple-element.32.refs_0_), channel_id=1, source_target_pairs={{0,1},{1,0},{2,3},{3,2},{4,5},{5,4},{6,7},{7,6},{8,9},{9,8},{10,11... | collective-permute-start | bytes 196616 | tf_op jit(solution)/shard_map/ppermute | solution.py:315
  14.0 2.4 %collective-permute-done.7.refs_0_ = bf16[256,128]{1,0:T(8,128)(2,1)S(1)} collective-permute-done((bf16[256,128]{1,0:T(8,128)(2,1)S(1)}, bf16[256,128]{1,0:T(8,128)(2,1)S(1)}, u32[]{:S(2)}, u32[]{:S(2)}) %collective-permute-start.7) | collective-permute-done | bytes 65568 | tf_op jit(solution)/shard_map/ppermute | solution.py:315
  16.4 1.5 %collective-permute-done.9.refs_2_.refs_0_ = bf16[256,128]{1,0:T(8,128)(2,1)S(1)} collective-permute-done((bf16[256,128]{1,0:T(8,128)(2,1)S(1)}, bf16[256,128]{1,0:T(8,128)(2,1)S(1)}, u32[]{:S(2)}, u32[]{:S(2)}) %collective-permute-start.9) | collective-permute-done | bytes 65568 | tf_op jit(solution)/shard_map/ppermute | solution.py:315
  18.2 1.8 %collective-permute-start.4 = (bf16[256,256]{1,0:T(8,128)(2,1)S(1)}, bf16[256,256]{1,0:T(8,128)(2,1)S(1)}, u32[]{:S(2)}, u32[]{:S(2)}) collective-permute-start(bf16[256,256]{1,0:T(8,128)(2,1)S(1)} %get-tuple-element.41), channel_id=1, source_target_pairs={{0,24},{8,0},{16,8},{24,16},{1,25},{9,1},{17,9},{25,17},{2,26},{10... | collective-permute-start | bytes 393224 | tf_op jit(solution)/shard_map/ppermute | solution.py:277
  20.1 0.4 %shard_map.102.begun = f32[512,128]{1,0:T(8,128)S(1)} custom-call(bf16[2,512,512]{2,1,0:T(8,128)(2,1)S(1)} %get-tuple-element.44.mine_frames, bf16[2,512,512]{2,1,0:T(8,128)(2,1)S(1)} %collective-permute-done.5.peer_frames, bf16[256,256]{1,0:T(8,128)(2,1)S(1)} %get-tuple-element.36.mine, bf16[256,256]{1,0:T(8,128)(2,1)S(1)} %collective-permute-done.6.peer, ...), custom_call_target="tpu_custom_call" | custom-call | flops 1048576 | bytes 1048576 | tf_op jit(solution)/shard_map/pallas_call | solution.py:29
  20.7 0.5 %collective-permute-start.12 = (bf16[512,128]{1,0:T(8,128)(2,1)S(1)}, bf16[512,128]{1,0:T(8,128)(2,1)S(1)}, u32[]{:S(2)}, u32[]{:S(2)}) collective-permute-start(bf16[512,128]{1,0:T(8,128)(2,1)S(1)} %shard_map.103), channel_id=1, source_target_pairs={{0,16},{8,24},{16,0},{24,8},{1,17},{9,25},{17,1},{25,9},{2,18},{10... | collective-permute-start | bytes 393224 | tf_op jit(solution)/shard_map/ppermute | solution.py:277
  21.2 0.4 %shard_map.100.begun = f32[512,128]{1,0:T(8,128)S(1)} custom-call(bf16[2,512,512]{2,1,0:T(8,128)(2,1)S(1)} %get-tuple-element.44.mine_frames, bf16[2,512,512]{2,1,0:T(8,128)(2,1)S(1)} %collective-permute-done.5.peer_frames, bf16[256,256]{1,0:T(8,128)(2,1)S(1)} %get-tuple-element.36.mine, bf16[256,256]{1,0:T(8,128)(2,1)S(1)} %collective-permute-done.6.peer, ...), custom_call_target="tpu_custom_call" | custom-call | flops 1048576 | bytes 1048576 | tf_op jit(solution)/shard_map/pallas_call | solution.py:29
  21.8 1.7 %collective-permute-start.11 = (bf16[512,128]{1,0:T(8,128)(2,1)S(1)}, bf16[512,128]{1,0:T(8,128)(2,1)S(1)}, u32[]{:S(2)}, u32[]{:S(2)}) collective-permute-start(bf16[512,128]{1,0:T(8,128)(2,1)S(1)} %shard_map.101), channel_id=1, source_target_pairs={{0,16},{8,24},{16,0},{24,8},{1,17},{9,25},{17,1},{25,9},{2,18},{10... | collective-permute-start | bytes 393224 | tf_op jit(solution)/shard_map/ppermute | solution.py:277
  23.4 0.7 %copy.12 = bf16[1,256,256]{2,1,0:T(8,128)(2,1)} copy(bf16[1,256,256]{2,1,0:T(8,128)(2,1)S(1)} %bitcast.8) | data formatting | bytes 262144
  24.1 1.9 %collective-permute-done.3.later_key = bf16[256,256]{1,0:T(8,128)(2,1)S(1)} collective-permute-done((bf16[256,256]{1,0:T(8,128)(2,1)S(1)}, bf16[256,256]{1,0:T(8,128)(2,1)S(1)}, u32[]{:S(2)}, u32[]{:S(2)}) %collective-permute-start.3) | collective-permute-done | bytes 131104 | tf_op jit(solution)/shard_map/ppermute | solution.py:277
  26.0 0.7 %shard_map.98 = (bf16[256,256]{1,0:T(8,128)(2,1)}, bf16[256,256]{1,0:T(8,128)(2,1)}) custom-call(f32[256,256]{1,0:T(8,128)S(1)} %get-tuple-element.37.own_key, bf16[256,256]{1,0:T(8,128)(2,1)S(1)} %collective-permute-done.3.later_key, f32[256,256]{1,0:T(8,128)S(1)} %get-tuple-element.40.own_value, bf16[256,256]{1,0:T(8,128)(2,1)S(1)} %collective-permute-done.4.later_value), custom_call_target="tpu_custom_call" | custom-call | flops 1048576 | bytes 1048576 | tf_op jit(solution)/shard_map/pallas_call | solution.py:29
  26.7 0.7 %shard_map.99.refs_0_ = f32[512,256]{1,0:T(8,128)S(1)} custom-call(bf16[2,512,512]{2,1,0:T(8,128)(2,1)S(1)} %get-tuple-element.44.mine_frames, bf16[2,512,512]{2,1,0:T(8,128)(2,1)S(1)} %collective-permute-done.5.peer_frames, bf16[256,256]{1,0:T(8,128)(2,1)S(1)} %get-tuple-element.36.mine, bf16[256,256]{1,0:T(8,128)(2,1)S(1)} %collective-permute-done.6.peer, ...), custom_call_target="tpu_custom_call" | custom-call | flops 1048576 | bytes 1048576 | tf_op jit(solution)/shard_map/pallas_call | solution.py:29
  27.5 1.1 %collective-permute-done.12.refs_1_ = bf16[512,128]{1,0:T(8,128)(2,1)S(1)} collective-permute-done((bf16[512,128]{1,0:T(8,128)(2,1)S(1)}, bf16[512,128]{1,0:T(8,128)(2,1)S(1)}, u32[]{:S(2)}, u32[]{:S(2)}) %collective-permute-start.12) | collective-permute-done | bytes 131104 | tf_op jit(solution)/shard_map/ppermute | solution.py:277
  28.6 0.7 %shard_map.104.refs_2_ = f32[512,256]{1,0:T(8,128)} custom-call(f32[512,256]{1,0:T(8,128)S(1)} %shard_map.99.refs_0_, bf16[512,128]{1,0:T(8,128)(2,1)S(1)} %collective-permute-done.12.refs_1_), custom_call_target="tpu_custom_call" | custom-call | flops 1048576 | bytes 1048576 | tf_op jit(solution)/shard_map/pallas_call | solution.py:250
  29.3 1.1 %collective-permute-done.11.refs_1_ = bf16[512,128]{1,0:T(8,128)(2,1)S(1)} collective-permute-done((bf16[512,128]{1,0:T(8,128)(2,1)S(1)}, bf16[512,128]{1,0:T(8,128)(2,1)S(1)}, u32[]{:S(2)}, u32[]{:S(2)}) %collective-permute-start.11) | collective-permute-done | bytes 131104 | tf_op jit(solution)/shard_map/ppermute | solution.py:277
  30.4 0.7 %shard_map.105 = f32[512,256]{1,0:T(8,128)} custom-call(f32[512,256]{1,0:T(8,128)S(1)} %shard_map.99.refs_0_, bf16[512,128]{1,0:T(8,128)(2,1)S(1)} %collective-permute-done.11.refs_1_, f32[512,256]{1,0:T(8,128)} %shard_map.104.refs_2_), custom_call_target="tpu_custom_call", output_to_operand_aliasing={{}: (2, {})} | custom-call | flops 1048576 | bytes 1048576 | tf_op jit(solution)/shard_map/pallas_call | solution.py:250
  (23 shorter events, 1.7 us)
Async XLA Ops:
  0.6 5.3 %copy-start.2 = (s32[1,256]{1,0:T(1,128)S(1)}, s32[1,256]{1,0:T(1,128)}, u32[]{:S(2)}) copy-start(s32[1,256]{1,0:T(1,128)} %refs_4_.1) | copy-start | bytes 3076
  0.6 2.7 %copy-start.1 = (bf16[1,256,256]{2,1,0:T(8,128)(2,1)S(1)}, bf16[1,256,256]{2,1,0:T(8,128)(2,1)}, u32[]{:S(2)}) copy-start(bf16[1,256,256]{2,1,0:T(8,128)(2,1)} %param.8) | copy-start | bytes 393220
  0.7 2.6 %copy-start = (bf16[1,256,256]{2,1,0:T(8,128)(2,1)S(1)}, bf16[1,256,256]{2,1,0:T(8,128)(2,1)}, u32[]{:S(2)}) copy-start(bf16[1,256,256]{2,1,0:T(8,128)(2,1)} %param.7) | copy-start | bytes 393220
  2.7 17.4 %collective-permute-start.5 = (bf16[2,512,512]{2,1,0:T(8,128)(2,1)S(1)}, bf16[2,512,512]{2,1,0:T(8,128)(2,1)S(1)}, u32[]{:S(2)}, u32[]{:S(2)}) collective-permute-start(bf16[2,512,512]{2,1,0:T(8,128)(2,1)S(1)} %get-tuple-element.45), channel_id=1, source_target_pairs={{0,8},{8,0},{16,24},{24,16},{1,9},{9,1},{17,25},{25,17},{2,10},{10... | collective-permute-start | bytes 3145736 | tf_op jit(solution)/shard_map/ppermute | solution.py:284
  3.3 6.7 %collective-permute-start = (bf16[256,256]{1,0:T(8,128)(2,1)S(1)}, bf16[256,256]{1,0:T(8,128)(2,1)S(1)}, u32[]{:S(2)}, u32[]{:S(2)}) collective-permute-start(bf16[256,256]{1,0:T(8,128)(2,1)S(1)} %bitcast.13), channel_id=1, source_target_pairs={{0,8},{8,16},{16,24},{24,0},{1,9},{9,17},{17,25},{25,1},{2,10},{10... | collective-permute-start | bytes 393224 | tf_op jit(solution)/shard_map/ppermute | solution.py:277
  3.3 7.3 %collective-permute-start.1 = (bf16[256,256]{1,0:T(8,128)(2,1)S(1)}, bf16[256,256]{1,0:T(8,128)(2,1)S(1)}, u32[]{:S(2)}, u32[]{:S(2)}) collective-permute-start(bf16[256,256]{1,0:T(8,128)(2,1)S(1)} %bitcast.15), channel_id=1, source_target_pairs={{0,8},{8,16},{16,24},{24,0},{1,9},{9,17},{17,25},{25,1},{2,10},{10... | collective-permute-start | bytes 393224 | tf_op jit(solution)/shard_map/ppermute | solution.py:277
  6.0 4.0 %collective-permute-start.2 = (s32[1,256]{1,0:T(1,128)S(1)}, s32[1,256]{1,0:T(1,128)S(1)}, u32[]{:S(2)}, u32[]{:S(2)}) collective-permute-start(s32[1,256]{1,0:T(1,128)S(1)} %copy-done.2), channel_id=1, source_target_pairs={{0,8},{8,16},{16,24},{24,0},{1,9},{9,17},{17,25},{25,1},{2,10},{10... | collective-permute-start | bytes 3080 | tf_op jit(solution)/shard_map/ppermute | solution.py:277
  11.8 8.1 %collective-permute-start.6 = (bf16[256,256]{1,0:T(8,128)(2,1)S(1)}, bf16[256,256]{1,0:T(8,128)(2,1)S(1)}, u32[]{:S(2)}, u32[]{:S(2)}) collective-permute-start(bf16[256,256]{1,0:T(8,128)(2,1)S(1)} %get-tuple-element.36.mine), channel_id=1, source_target_pairs={{0,8},{8,0},{16,24},{24,16},{1,9},{9,1},{17,25},{25,17},{2,10},{10... | collective-permute-start | bytes 393224 | tf_op jit(solution)/shard_map/ppermute | solution.py:277
  11.9 4.5 %collective-permute-start.7 = (bf16[256,128]{1,0:T(8,128)(2,1)S(1)}, bf16[256,128]{1,0:T(8,128)(2,1)S(1)}, u32[]{:S(2)}, u32[]{:S(2)}) collective-permute-start(bf16[256,128]{1,0:T(8,128)(2,1)S(1)} %get-tuple-element.32.refs_0_), channel_id=1, source_target_pairs={{0,1},{1,0},{2,3},{3,2},{4,5},{5,4},{6,7},{7,6},{8,9},{9,8},{10,11... | collective-permute-start | bytes 196616 | tf_op jit(solution)/shard_map/ppermute | solution.py:315
  13.7 4.3 %collective-permute-start.9 = (bf16[256,128]{1,0:T(8,128)(2,1)S(1)}, bf16[256,128]{1,0:T(8,128)(2,1)S(1)}, u32[]{:S(2)}, u32[]{:S(2)}) collective-permute-start(bf16[256,128]{1,0:T(8,128)(2,1)S(1)} %get-tuple-element.34.refs_2_), channel_id=1, source_target_pairs={{0,1},{1,0},{2,3},{3,2},{4,5},{5,4},{6,7},{7,6},{8,9},{9,8},{10,11... | collective-permute-start | bytes 196616 | tf_op jit(solution)/shard_map/ppermute | solution.py:315
  16.4 4.0 %collective-permute-start.8 = (bf16[256,128]{1,0:T(8,128)(2,1)S(1)}, bf16[256,128]{1,0:T(8,128)(2,1)S(1)}, u32[]{:S(2)}, u32[]{:S(2)}) collective-permute-start(bf16[256,128]{1,0:T(8,128)(2,1)S(1)} %collective-permute-done.7.refs_0_), channel_id=1, source_target_pairs={{0,8},{8,0},{16,24},{24,16},{1,9},{9,1},{17,25},{25,17},{2,10},{10... | collective-permute-start | bytes 196616 | tf_op jit(solution)/shard_map/ppermute | solution.py:277
  17.9 3.6 %collective-permute-start.10 = (bf16[256,128]{1,0:T(8,128)(2,1)S(1)}, bf16[256,128]{1,0:T(8,128)(2,1)S(1)}, u32[]{:S(2)}, u32[]{:S(2)}) collective-permute-start(bf16[256,128]{1,0:T(8,128)(2,1)S(1)} %collective-permute-done.9.refs_2_.refs_0_), channel_id=1, source_target_pairs={{0,8},{8,0},{16,24},{24,16},{1,9},{9,1},{17,25},{25,17},{2,10},{10... | collective-permute-start | bytes 196616 | tf_op jit(solution)/shard_map/ppermute | solution.py:277
  18.2 5.9 %collective-permute-start.4 = (bf16[256,256]{1,0:T(8,128)(2,1)S(1)}, bf16[256,256]{1,0:T(8,128)(2,1)S(1)}, u32[]{:S(2)}, u32[]{:S(2)}) collective-permute-start(bf16[256,256]{1,0:T(8,128)(2,1)S(1)} %get-tuple-element.41), channel_id=1, source_target_pairs={{0,24},{8,0},{16,8},{24,16},{1,25},{9,1},{17,9},{25,17},{2,26},{10... | collective-permute-start | bytes 393224 | tf_op jit(solution)/shard_map/ppermute | solution.py:277
  20.0 6.0 %collective-permute-start.3 = (bf16[256,256]{1,0:T(8,128)(2,1)S(1)}, bf16[256,256]{1,0:T(8,128)(2,1)S(1)}, u32[]{:S(2)}, u32[]{:S(2)}) collective-permute-start(bf16[256,256]{1,0:T(8,128)(2,1)S(1)} %get-tuple-element.38), channel_id=1, source_target_pairs={{0,24},{8,0},{16,8},{24,16},{1,25},{9,1},{17,9},{25,17},{2,26},{10... | collective-permute-start | bytes 393224 | tf_op jit(solution)/shard_map/ppermute | solution.py:277
  20.7 7.9 %collective-permute-start.12 = (bf16[512,128]{1,0:T(8,128)(2,1)S(1)}, bf16[512,128]{1,0:T(8,128)(2,1)S(1)}, u32[]{:S(2)}, u32[]{:S(2)}) collective-permute-start(bf16[512,128]{1,0:T(8,128)(2,1)S(1)} %shard_map.103), channel_id=1, source_target_pairs={{0,16},{8,24},{16,0},{24,8},{1,17},{9,25},{17,1},{25,9},{2,18},{10... | collective-permute-start | bytes 393224 | tf_op jit(solution)/shard_map/ppermute | solution.py:277
  21.8 8.6 %collective-permute-start.11 = (bf16[512,128]{1,0:T(8,128)(2,1)S(1)}, bf16[512,128]{1,0:T(8,128)(2,1)S(1)}, u32[]{:S(2)}, u32[]{:S(2)}) collective-permute-start(bf16[512,128]{1,0:T(8,128)(2,1)S(1)} %shard_map.101), channel_id=1, source_target_pairs={{0,16},{8,24},{16,0},{24,8},{1,17},{9,25},{17,1},{25,9},{2,18},{10... | collective-permute-start | bytes 393224 | tf_op jit(solution)/shard_map/ppermute | solution.py:277
